TPU v7x, 512 devices: a whole 4x4x16 slice. The times are simulated.
512 devices in a mesh: dp: 8 (over y, core), expert: 64 (over x, z).
Axes of the slice: x: 4, y: 4, z: 16, core: 2. Of those that a mesh axis runs over, the one named last changes fastest.
Arguments:
- pre_query: bfloat16 [8192, 16, 576], P(('dp', 'expert')), may hold values from -25 to 25
- pre_latent: bfloat16 [8192, 576], P(('dp', 'expert')), may hold values from -5 to 5
- pre_resid: bfloat16 [8192, 2048], P(('dp', 'expert')), may hold values from -6 to 6
- dec_query: bfloat16 [512, 16, 576], P(('dp', 'expert')), may hold values from -25 to 25
- dec_latent: bfloat16 [512, 576], P(('dp', 'expert')), may hold values from -5 to 5
- dec_resid: bfloat16 [512, 2048], P(('dp', 'expert')), may hold values from -6 to 6
- cache_lengths: int32 [512], P(('dp', 'expert')), may hold values from 1 to 32768
- latent_cache: bfloat16 [512, 1024, 576], P(('dp', 'expert')), may hold values from -5 to 5
- sink_logits: float32 [16], replicated, may hold values from -1 to 3
- uv_weight: bfloat16 [16, 512, 128], P('dp', 'expert'), may hold values from -0.25 to 0.25
- out_weight: bfloat16 [16, 128, 2048], P('dp', 'expert'), may hold values from -0.125 to 0.125
- norm_gain: bfloat16 [2048], replicated, may hold values from 0.5 to 1.5
- router: bfloat16 [2048, 64], P(None, 'expert'), may hold values from -0.125 to 0.125
- routes: int32 [8704, 6], P(('dp', 'expert')), may hold values from 0 to 63, all different within a row; in each aligned block of 17 rows (0 to 16, 17 to 33, ...) at most 2 rows name the same one
- gate_weight: bfloat16 [64, 2048, 1408], P('expert', None, 'dp'), may hold values from -0.125 to 0.125
- up_weight: bfloat16 [64, 2048, 1408], P('expert', None, 'dp'), may hold values from -0.125 to 0.125
- down_weight: bfloat16 [64, 1408, 2048], P('expert', None, 'dp'), may hold values from -0.15625 to 0.15625
- shared_gate: bfloat16 [2048, 1408], P('expert', 'dp'), may hold values from -0.125 to 0.125
- shared_up: bfloat16 [2048, 1408], P('expert', 'dp'), may hold values from -0.125 to 0.125
- shared_down: bfloat16 [1408, 2048], P('expert', 'dp'), may hold values from -0.15625 to 0.15625
Outputs:
- pre_out: bfloat16 [8192, 2048], P(('dp', 'expert'))
- dec_out: bfloat16 [512, 2048], P(('dp', 'expert'))
Inputs may be any that keep to these rules, and one draw needn't show every extreme that they name: `routes`: each row names 6 different experts; in each aligned block of 17 rows no expert is named by more than 2 rows.
All inputs are finite; a program needn't handle non-finite values.
Results may differ from a plain program's by a relative error of at most 0.015.
Values may be sent and summed in bfloat16 or wider, within the bound.
A program may use at most 64 MiB of HBM per device.

v0:
```python
from functools import partial

import jax
import jax.numpy as jnp
from jax import lax
from jax.sharding import PartitionSpec as P

D = 2048
LATENT = 512
ROPE = 64
QK_NOPE = 128
TOPK = 6


ROUTE_SCALE = 2.446
NORM_EPS = 1e-06
NEG_FILL = -1e30


def assign_slots(route_rows, experts):
    flat_routes = route_rows.reshape(-1)
    one_hot = (flat_routes[:, None] == jnp.arange(experts, dtype=jnp.int32)[None, :]).astype(
        jnp.int32
    )
    running = jnp.cumsum(one_hot, axis=0)
    slot_rank = jnp.sum(running * one_hot, axis=1) - 1
    return slot_rank.reshape(route_rows.shape)


def dispatch_matrix(route_rows, slot_rows, experts, capacity):
    target = route_rows * capacity + slot_rows
    places = jnp.arange(experts * capacity, dtype=jnp.int32)
    total = jnp.zeros((route_rows.shape[0], experts * capacity), jnp.bfloat16)
    for column in range(route_rows.shape[1]):
        total = total + (target[:, column][:, None] == places[None, :]).astype(jnp.bfloat16)
    return total


def shards(
    pre_query,
    pre_latent,
    pre_resid,
    dec_query,
    dec_latent,
    dec_resid,
    cache_lengths,
    latent_cache,
    sink_logits,
    uv_weight,
    out_weight,
    norm_gain,
    router,
    routes,
    gate_weight,
    up_weight,
    down_weight,
    shared_gate,
    shared_up,
    shared_down,
):
    groups = lax.axis_size("dp")
    members = lax.axis_size("expert")
    pre_rows = pre_query.shape[0]
    rows_dev = pre_rows + 1
    scale_qk = (QK_NOPE + ROPE) ** (-0.5)
    pre_scores = (
        jnp.einsum("thc,uc->thu", pre_query, pre_latent, preferred_element_type=jnp.float32)
        * scale_qk
    )
    places = jnp.arange(pre_rows, dtype=jnp.int32)
    allowed = (places[None, :] <= places[:, None])[:, None, :]
    masked = jnp.where(allowed, pre_scores, NEG_FILL)
    pre_max = jnp.maximum(jnp.max(masked, axis=2), sink_logits[None, :])
    exp_terms = jnp.where(allowed, jnp.exp(masked - pre_max[:, :, None]), 0.0)
    denominator = jnp.sum(exp_terms, axis=2) + jnp.exp(sink_logits[None, :] - pre_max)
    numerator = jnp.einsum(
        "thu,ul->thl",
        exp_terms.astype(jnp.bfloat16),
        pre_latent[:, :LATENT],
        preferred_element_type=jnp.float32,
    )
    pre_att = (numerator / denominator[:, :, None]).astype(jnp.bfloat16)
    window = latent_cache.shape[1]
    slot_ids = jnp.arange(window, dtype=jnp.int32)
    newest = cache_lengths - 1
    position = newest[:, None] - jnp.mod(newest[:, None] - slot_ids[None, :], window)
    usable = ((position >= 0) & (position > cache_lengths[:, None] - window))[:, None, :]
    cache_scores = (
        jnp.einsum("rhc,rsc->rhs", dec_query, latent_cache, preferred_element_type=jnp.float32)
        * scale_qk
    )
    own_scores = (
        jnp.einsum("rhc,rc->rh", dec_query, dec_latent, preferred_element_type=jnp.float32)
        * scale_qk
    )
    cache_masked = jnp.where(usable, cache_scores, NEG_FILL)
    top_score = jnp.maximum(
        jnp.maximum(jnp.max(cache_masked, axis=2), own_scores), sink_logits[None, :]
    )
    cache_exp = jnp.where(usable, jnp.exp(cache_masked - top_score[:, :, None]), 0.0)
    own_exp = jnp.exp(own_scores - top_score)
    dec_numer = jnp.einsum(
        "rhs,rsl->rhl",
        cache_exp.astype(jnp.bfloat16),
        latent_cache[:, :, :LATENT],
        preferred_element_type=jnp.float32,
    )
    dec_numer = dec_numer + own_exp.astype(jnp.bfloat16).astype(jnp.float32)[
        :, :, None
    ] * dec_latent[:, None, :LATENT].astype(jnp.float32)
    dec_total = jnp.sum(cache_exp, axis=2) + own_exp + jnp.exp(sink_logits[None, :] - top_score)
    dec_att = (dec_numer / dec_total[:, :, None]).astype(jnp.bfloat16)
    attention = jnp.concatenate([pre_att, dec_att], axis=0)
    spread = lax.all_to_all(attention, "dp", split_axis=1, concat_axis=0, tiled=True)
    uv_full, out_full = (
        lax.all_gather(uv_weight, "expert", axis=1, tiled=True),
        lax.all_gather(out_weight, "expert", axis=1, tiled=True),
    )
    head_values = jnp.einsum(
        "thl,hlv->thv", spread, uv_full, preferred_element_type=jnp.float32
    ).astype(jnp.bfloat16)
    head_partial = jnp.einsum(
        "thv,hvd->td", head_values, out_full, preferred_element_type=jnp.float32
    )
    attn_out = lax.psum_scatter(
        head_partial.astype(jnp.bfloat16), "dp", scatter_dimension=0, tiled=True
    ).astype(jnp.float32)
    resid = jnp.concatenate([pre_resid, dec_resid], axis=0)
    hidden = (resid.astype(jnp.float32) + attn_out).astype(jnp.bfloat16)
    hidden_up = lax.optimization_barrier(hidden).astype(jnp.float32)
    mean_square = jnp.mean(hidden_up * hidden_up, axis=1, keepdims=True)
    normed = (
        hidden_up * lax.rsqrt(mean_square + NORM_EPS) * norm_gain.astype(jnp.float32)[None, :]
    ).astype(jnp.bfloat16)
    capacity = max(2, (rows_dev * TOPK + members - 1) // members)
    group_tokens = lax.all_gather(normed, "dp", axis=0, tiled=True)
    group_routes = lax.all_gather(routes, "dp", axis=0, tiled=True)
    routes_by_group = group_routes.reshape(groups, rows_dev, TOPK)
    slots_by_group = jax.vmap(partial(assign_slots, experts=members))(routes_by_group)
    tokens_by_group = group_tokens.reshape(groups, rows_dev, D)
    all_matrix = jax.vmap(partial(dispatch_matrix, experts=members, capacity=capacity))(
        routes_by_group, slots_by_group
    )
    all_matrix = all_matrix.reshape(groups, rows_dev, members, capacity)
    outgoing = jnp.einsum(
        "grxc,grd->xgcd", all_matrix, tokens_by_group, preferred_element_type=jnp.bfloat16
    )
    expert_rows = lax.all_to_all(outgoing, "expert", split_axis=0, concat_axis=0, tiled=True)
    expert_rows = expert_rows.reshape(-1, D)
    gate_score = jax.nn.sigmoid(
        jnp.dot(expert_rows, router[:, 0], preferred_element_type=jnp.float32)
    )
    gate_proj = jnp.dot(expert_rows, gate_weight[0], preferred_element_type=jnp.float32)
    up_proj = jnp.dot(expert_rows, up_weight[0], preferred_element_type=jnp.float32)
    expert_act = (jax.nn.silu(gate_proj) * up_proj).astype(jnp.bfloat16)
    shared_gate_full, shared_up_full, shared_down_full = (
        lax.all_gather(shared_gate, "expert", axis=0, tiled=True),
        lax.all_gather(shared_up, "expert", axis=0, tiled=True),
        lax.all_gather(shared_down, "expert", axis=0, tiled=True),
    )
    shared_act = (
        jax.nn.silu(jnp.dot(group_tokens, shared_gate_full, preferred_element_type=jnp.float32))
        * jnp.dot(group_tokens, shared_up_full, preferred_element_type=jnp.float32)
    ).astype(jnp.bfloat16)
    down_local = down_weight[0]
    col_width = down_local.shape[1]
    routed_piece = lax.all_gather(expert_act, "dp", axis=1, tiled=True)
    shared_piece = lax.all_gather(shared_act, "dp", axis=1, tiled=True)
    routed_cols = jnp.dot(routed_piece, down_local, preferred_element_type=jnp.float32)
    shared_cols = jnp.dot(shared_piece, shared_down_full, preferred_element_type=jnp.float32)
    expert_out = routed_cols.astype(jnp.bfloat16)
    shared_out = shared_cols.astype(jnp.bfloat16)
    returned = lax.all_to_all(
        expert_out.reshape(members, groups * capacity, col_width),
        "expert",
        split_axis=0,
        concat_axis=0,
        tiled=True,
    )
    returned_scores = lax.all_to_all(
        gate_score.reshape(members, groups * capacity),
        "expert",
        split_axis=0,
        concat_axis=0,
        tiled=True,
    )
    group_offset = (jnp.arange(groups, dtype=jnp.int32) * capacity)[:, None, None]
    lookup = (routes_by_group * (groups * capacity) + group_offset + slots_by_group).reshape(
        groups * rows_dev, TOPK
    )
    picked = jnp.take(returned.reshape(-1, col_width), lookup, axis=0)
    picked_scores = jnp.take(returned_scores.reshape(-1), lookup, axis=0)
    route_weight = ROUTE_SCALE * picked_scores / jnp.sum(picked_scores, axis=1, keepdims=True)
    moe_cols = shared_out.astype(jnp.float32) + jnp.sum(
        route_weight[:, :, None] * picked.astype(jnp.float32), axis=1
    )
    moe_home = lax.all_to_all(
        moe_cols.reshape(groups, rows_dev, col_width).astype(jnp.bfloat16),
        "dp",
        split_axis=0,
        concat_axis=2,
        tiled=True,
    ).astype(jnp.float32)
    final = (hidden_up + moe_home[0]).astype(jnp.bfloat16)
    return (final[:pre_rows], final[pre_rows:])


def solution(mesh):
    in_specs = (
        P(("dp", "expert"), None, None),
        P(("dp", "expert"), None),
        P(("dp", "expert"), None),
        P(("dp", "expert"), None, None),
        P(("dp", "expert"), None),
        P(("dp", "expert"), None),
        P(("dp", "expert")),
        P(("dp", "expert"), None, None),
        P(),
        P("dp", "expert", None),
        P("dp", "expert", None),
        P(),
        P(None, "expert"),
        P(("dp", "expert"), None),
        P("expert", None, "dp"),
        P("expert", None, "dp"),
        P("expert", None, "dp"),
        P("expert", "dp"),
        P("expert", "dp"),
        P("expert", "dp"),
    )
    out_specs = (P(("dp", "expert"), None), P(("dp", "expert"), None))
    return jax.shard_map(shards, mesh=mesh, in_specs=in_specs, out_specs=out_specs, check_vma=False)
```

profile of v0, /device:TPU:1, one launch (start us, length us, event | category | flops | bytes accessed | tf_op | source)
XLA Modules:
  0.0 847.5 jit_solution(9631233575967358655)
XLA Ops:
  7.2 1.4 copy.83
  9.3 1.6 fusion.80
  11.6 1.7 fusion.79
  13.2 0.9 convert_convert_fusion
  14.5 0.7 exponential_add_fusion.1
  15.1 0.7 slice_convert_fusion
  15.8 1.6 fusion.21
  17.4 0.7 exponential_add_fusion
  18.1 1.1 fusion.3
  19.3 0.9 copy.80
  20.2 10.2 %all-to-all-start = ((bf16[17,16,512]{2,0,1:T(8,128)(2,1)}), bf16[17,16,512]{2,0,1:T(8,128)(2,1)S(1)}, u32[]{:S(2)}, u32[]{:S(2)}) async-start(bf16[17,16,512]{2,0,1:T(8,128)(2,1)} %copy.80), calls=%async_computation | async-start | bytes 786432 | tf_op jit(solution)/shard_map/all_to_all | solution.py:114
  30.4 14.7 %all-gather.3 = s32[8,17,6]{1,2,0:T(8,128)S(1)} all-gather(s32[1,17,6]{1,2,0:T(8,128)S(1)} %bitcast.124), channel_id=1, replica_groups=mesh['dp'=8,'expert'=64] {'dp'}, dimensions={0}, use_global_device_ids=true | all-gather | bytes 3672 | tf_op jit(solution)/shard_map/all_gather | solution.py:137
  45.4 2.0 select_reduce_fusion
  47.6 80.0 %all_gather.27 = bf16[2,512,128]{2,1,0:T(8,128)(2,1)S(1)} all-gather(bf16[2,8,128]{2,1,0:T(8,128)(2,1)S(1)} %copy-done.9), channel_id=1, replica_groups=mesh['dp'=8,'expert'=64] {'expert'}, dimensions={1}, use_global_device_ids=true | all-gather | bytes 266240 | tf_op jit(solution)/shard_map/all_gather | solution.py:116
  127.6 1.0 slice_reduce_fusion.5
  128.9 17.4 %all-gather.7.cloned.1.call-done = bf16[2,128,2048]{2,0,1:T(2,128)(2,1)} async-done(((bf16[2,2,2048]{2,0,1:T(2,128)(2,1)}), bf16[2,128,2048]{2,0,1:T(2,128)(2,1)}) %all-gather.7.cloned.1.call-update) | async-done | bytes 1048592 | tf_op jit(solution)/shard_map/all_gather | solution.py:117
  146.3 2.1 fusion.1
  148.4 24.8 %fusion = bf16[24,2048]{1,0:T(8,128)(2,1)S(1)} fusion(bf16[136,2048]{1,0:T(8,128)(2,1)S(1)} %fusion.1), kind=kCustom, calls=%all-reduce-scatter | all-reduce-scatter fusion | flops 393217 | bytes 657408
  173.2 3.6 collective-permute-start
  176.8 2.0 collective-permute-start.1
  178.8 5.1 collective-permute-start.2
  183.9 1.3 dynamic-slice.4
  186.8 13.8 %all-gather = bf16[8,17,2048]{2,1,0:T(8,128)(2,1)S(1)} all-gather(bf16[1,17,2048]{2,1,0:T(8,128)(2,1)S(1)} %fusion.48), channel_id=1, replica_groups=mesh['dp'=8,'expert'=64] {'dp'}, dimensions={0}, use_global_device_ids=true | all-gather | bytes 626688 | tf_op jit(solution)/shard_map/all_gather | solution.py:136
  200.6 1.4 convolution_bitcast_fusion
  202.0 6.3 copy.92
  208.2 192.1 %all_to_all.46 = bf16[64,8,2,2048]{3,2,1,0:T(2,128)(2,1)} all-to-all(bf16[64,8,2,2048]{3,2,1,0:T(2,128)(2,1)} %copy.92), channel_id=1, replica_groups=mesh['dp'=8,'expert'=64] {'expert'}, dimensions={0} | all-to-all | bytes 8388608 | tf_op jit(solution)/shard_map/all_to_all | solution.py:148
  400.4 7.3 reshape.248
  407.6 3.9 fusion.29
  411.6 2.3 fusion.2
  414.2 3.4 fusion.82
  417.6 0.7 all_to_all.37
  418.3 13.8 %all-to-all-start.2 = ((f32[64,1,16]{2,1,0:T(1,128)}), f32[64,1,16]{2,1,0:T(1,128)S(1)}, u32[]{:S(2)}, u32[]{:S(2)}) async-start(f32[64,1,16]{2,1,0:T(1,128)} %bitcast.24), calls=%async_computation.2 | async-start | bytes 65536 | tf_op jit(solution)/shard_map/all_to_all | solution.py:180
  432.2 14.7 %all-gather.9.cloned.1.call-done = bf16[1024,1408]{0,1:T(8,128)(2,1)} async-done(((bf16[1024,176]{0,1:T(8,128)(2,1)}), bf16[1024,1408]{0,1:T(8,128)(2,1)}) %all-gather.9.cloned.1.call-update) | async-done | bytes 2883600 | tf_op jit(solution)/shard_map/all_gather | solution.py:167
  446.8 3.6 convolution_convert_fusion
  450.5 15.3 %all-to-all-start.3 = ((bf16[64,16,256]{2,1,0:T(8,128)(2,1)}), bf16[64,16,256]{2,1,0:T(8,128)(2,1)S(1)}, u32[]{:S(2)}, u32[]{:S(2)}) async-start(bf16[64,16,256]{2,1,0:T(8,128)(2,1)} %bitcast.28), calls=%async_computation.3 | async-start | bytes 1048576 | tf_op jit(solution)/shard_map/all_to_all | solution.py:173
  466.3 93.9 %all-gather.2 = bf16[64,22,256]{2,1,0:T(8,128)(2,1)S(1)} all-gather(bf16[1,22,256]{2,1,0:T(8,128)(2,1)S(1)} %bitcast.123), channel_id=1, replica_groups=mesh['dp'=8,'expert'=64] {'expert'}, dimensions={0}, use_global_device_ids=true | all-gather | bytes 732160 | tf_op jit(solution)/shard_map/all_gather | solution.py:159
  560.2 1.1 reshape.280
  561.3 84.0 %all_gather.30 = bf16[2048,176]{1,0:T(8,128)(2,1)} all-gather(bf16[32,176]{1,0:T(8,128)(2,1)S(1)} %copy-done.4), channel_id=1, replica_groups=mesh['dp'=8,'expert'=64] {'expert'}, dimensions={0}, use_global_device_ids=true | all-gather | bytes 732160 | tf_op jit(solution)/shard_map/all_gather | solution.py:157
  645.3 83.0 %all_gather.31 = bf16[2048,176]{1,0:T(8,128)(2,1)} all-gather(bf16[32,176]{1,0:T(8,128)(2,1)S(1)} %copy-done.5), channel_id=1, replica_groups=mesh['dp'=8,'expert'=64] {'expert'}, dimensions={0}, use_global_device_ids=true | all-gather | bytes 732160 | tf_op jit(solution)/shard_map/all_gather | solution.py:158
  728.5 1.6 fusion.81
  730.1 1.6 fusion.11
  731.7 87.1 %all-gather.1 = bf16[8,176,136]{1,2,0:T(8,128)(2,1)S(1)} all-gather(bf16[1,176,136]{1,2,0:T(8,128)(2,1)S(1)} %fusion.11), channel_id=1, replica_groups=mesh['dp'=8,'expert'=64] {'dp'}, dimensions={0}, use_global_device_ids=true | all-gather | bytes 430848 | tf_op jit(solution)/shard_map/all_gather | solution.py:168
  818.9 1.2 reshape.278
  820.7 0.7 reduce.19
  821.5 3.5 gather_fusion
  825.5 3.4 gather_fusion.1
  829.6 1.3 fusion.10
  830.9 8.3 all_to_all.47
  (92 shorter events, 6.9 us)
Async XLA Ops:
  7.2 439.7 %copy-start = (bf16[1,1408,256]{2,1,0:T(8,128)(2,1)S(1)}, bf16[1,1408,256]{2,1,0:T(8,128)(2,1)}, u32[]{:S(2)}) copy-start(bf16[1,1408,256]{2,1,0:T(8,128)(2,1)} %param.36) | copy-start | bytes 2162692
  7.2 23.2 %copy-start.10 = (s32[17,6]{0,1:T(8,128)S(1)}, s32[17,6]{0,1:T(8,128)}, u32[]{:S(2)}) copy-start(s32[17,6]{0,1:T(8,128)} %param.33) | copy-start | bytes 1228
  7.2 40.4 %copy-start.9 = (bf16[2,8,128]{2,1,0:T(8,128)(2,1)S(1)}, bf16[2,8,128]{2,1,0:T(8,128)(2,1)}, u32[]{:S(2)}) copy-start(bf16[2,8,128]{2,1,0:T(8,128)(2,1)} %param.29) | copy-start | bytes 12292
  7.2 139.1 %all-gather.7.cloned.1.call-start = ((), (), s32[]{:S(2)}) async-start(), calls=%async_computation.5 | async-start | bytes 1064960 | tf_op jit(solution)/shard_map/all_gather | solution.py:117
  18.1 165.8 %copy-start.11 = (bf16[2048]{0:T(1024)(128)(2,1)S(1)}, bf16[2048]{0:T(1024)(128)(2,1)}, u32[]{:S(2)}) copy-start(bf16[2048]{0:T(1024)(128)(2,1)} %param.31) | copy-start | bytes 12292
  19.2 167.3 %copy-start.3 = (bf16[16,2048]{1,0:T(8,128)(2,1)S(1)}, bf16[16,2048]{1,0:T(8,128)(2,1)}, u32[]{:S(2)}) copy-start(bf16[16,2048]{1,0:T(8,128)(2,1)} %param.22) | copy-start | bytes 196612
  19.2 167.3 %copy-start.8 = (bf16[1,2048]{1,0:T(2,128)(2,1)S(1)}, bf16[1,2048]{1,0:T(2,128)(2,1)}, u32[]{:S(2)}) copy-start(bf16[1,2048]{1,0:T(2,128)(2,1)} %param.25) | copy-start | bytes 12292
  20.2 108.4 %all-to-all-start = ((bf16[17,16,512]{2,0,1:T(8,128)(2,1)}), bf16[17,16,512]{2,0,1:T(8,128)(2,1)S(1)}, u32[]{:S(2)}, u32[]{:S(2)}) async-start(bf16[17,16,512]{2,0,1:T(8,128)(2,1)} %copy.80), calls=%async_computation | async-start | bytes 786432 | tf_op jit(solution)/shard_map/all_to_all | solution.py:114
  30.4 416.4 %all-gather.9.cloned.1.call-start = ((), (), s32[]{:S(2)}) async-start(), calls=%async_computation.6 | async-start | bytes 3244032 | tf_op jit(solution)/shard_map/all_gather | solution.py:167
  173.2 12.6 %collective-permute-start = (bf16[24,2048]{1,0:T(8,128)(2,1)S(1)}, bf16[24,2048]{1,0:T(8,128)(2,1)S(1)}, u32[]{:S(2)}, u32[]{:S(2)}) collective-permute-start(bf16[24,2048]{1,0:T(8,128)(2,1)S(1)} %fusion), channel_id=1, source_target_pairs={{0,64},{64,128},{128,192},{192,256},{256,320},{320,384},{384,448},... | collective-permute-start | bytes 294920
  176.8 9.1 %collective-permute-start.1 = (bf16[24,2048]{1,0:T(8,128)(2,1)S(1)}, bf16[24,2048]{1,0:T(8,128)(2,1)S(1)}, u32[]{:S(2)}, u32[]{:S(2)}) collective-permute-start(bf16[24,2048]{1,0:T(8,128)(2,1)S(1)} %fusion), channel_id=1, source_target_pairs={{0,128},{64,192},{128,256},{192,320},{256,384},{320,448},{1,129},{... | collective-permute-start | bytes 294920
  178.8 7.1 collective-permute-start.2
  400.4 7.3 copy-start.12
  407.6 3.9 copy-start.1
  407.6 3.9 copy-start.13
  411.5 2.6 copy-start.7
  417.6 48.7 %copy-start.6 = (bf16[22,256]{1,0:T(8,128)(2,1)S(1)}, bf16[22,256]{1,0:T(8,128)(2,1)}, u32[]{:S(2)}) copy-start(bf16[22,256]{1,0:T(8,128)(2,1)} %param.39) | copy-start | bytes 33796
  418.3 32.2 %all-to-all-start.2 = ((f32[64,1,16]{2,1,0:T(1,128)}), f32[64,1,16]{2,1,0:T(1,128)S(1)}, u32[]{:S(2)}, u32[]{:S(2)}) async-start(f32[64,1,16]{2,1,0:T(1,128)} %bitcast.24), calls=%async_computation.2 | async-start | bytes 65536 | tf_op jit(solution)/shard_map/all_to_all | solution.py:180
  432.1 129.1 %copy-start.4 = (bf16[32,176]{1,0:T(8,128)(2,1)S(1)}, bf16[32,176]{1,0:T(8,128)(2,1)}, u32[]{:S(2)}) copy-start(bf16[32,176]{1,0:T(8,128)(2,1)} %param.37) | copy-start | bytes 33796
  432.1 213.2 %copy-start.5 = (bf16[32,176]{1,0:T(8,128)(2,1)S(1)}, bf16[32,176]{1,0:T(8,128)(2,1)}, u32[]{:S(2)}) copy-start(bf16[32,176]{1,0:T(8,128)(2,1)} %param.38) | copy-start | bytes 33796
  450.5 375.0 %all-to-all-start.3 = ((bf16[64,16,256]{2,1,0:T(8,128)(2,1)}), bf16[64,16,256]{2,1,0:T(8,128)(2,1)S(1)}, u32[]{:S(2)}, u32[]{:S(2)}) async-start(bf16[64,16,256]{2,1,0:T(8,128)(2,1)} %bitcast.28), calls=%async_computation.3 | async-start | bytes 1048576 | tf_op jit(solution)/shard_map/all_to_all | solution.py:173
  825.0 4.6 copy-start.2
Sparse Core Ops, SparseCore 0:
  11.6 134.6 all-gather.6
  414.0 32.7 all-gather.8
where the time goes:
time: 849 us; the launch traced here: 847 us
  blocking collectives  682 us (80%)
  starting transfers between devices  50.1 us (6%)
  local copies, waits for them, and re-layouts  32.9 us (4%)
  waiting for transfers between devices  32.1 us (4%)
  matrix products  27.9 us (3%)
  between operations  15.9 us (2%)
    all_to_all x1, blocking collectives, shards(): lax.all_to_all(outgoing, 'expert', split_axis=0, concat_axis=0, tiled=True)  192 us
    all_gather x1, blocking collectives, shards(): lax.all_gather(shared_down, 'expert', axis=0, tiled=True)  93.9 us
    all_gather x1, blocking collectives, shards(): shared_piece = lax.all_gather(shared_act, 'dp', axis=1, tiled=True)  87.1 us
    all_gather x1, blocking collectives, shards(): lax.all_gather(shared_gate, 'expert', axis=0, tiled=True)  84 us
    all_gather x1, blocking collectives, shards(): lax.all_gather(shared_up, 'expert', axis=0, tiled=True)  83 us
    all_gather x1, blocking collectives, shards(): lax.all_gather(uv_weight, 'expert', axis=1, tiled=True)  80 us
    unnamed x1, blocking collectives  24.8 us
    all_gather x1, waiting for transfers between devices, shards(): lax.all_gather(out_weight, 'expert', axis=1, tiled=True)  17.4 us
  transfers between devices with their start and end apart: 8, of which 2 were waited for; matrix products, arithmetic and copies ran while one was open for 4% of the time, Pallas kernels for 0%

commit v1 on v0

--- a/solution.py
+++ b/solution.py
@@ -34,6 +34,28 @@
     for column in range(route_rows.shape[1]):
         total = total + (target[:, column][:, None] == places[None, :]).astype(jnp.bfloat16)
     return total
+
+
+def gather_weights(members, **parts):
+    names = list(parts)
+    flat = jnp.concatenate([parts[n][0].reshape(-1) for n in names])
+    lanes = 128
+    total = flat.shape[0]
+    padded = -(-total // lanes) * lanes
+    flat = jnp.pad(flat, (0, padded - total)).reshape(1, padded // lanes, lanes)
+    everyone = lax.all_gather(flat, "expert", axis=0, tiled=True).reshape(members, padded)
+    out = {}
+    start = 0
+    for n in names:
+        local, axis = parts[n]
+        size = local.size
+        piece = everyone[:, start : start + size].reshape((members,) + local.shape)
+        piece = jnp.moveaxis(piece, 0, axis)
+        shape = list(local.shape)
+        shape[axis] *= members
+        out[n] = piece.reshape(shape)
+        start += size
+    return out
 
 
 def shards(
@@ -63,6 +85,14 @@
     pre_rows = pre_query.shape[0]
     rows_dev = pre_rows + 1
     scale_qk = (QK_NOPE + ROPE) ** (-0.5)
+    weights = gather_weights(
+        members,
+        uv=(uv_weight, 1),
+        out=(out_weight, 1),
+        shared_gate=(shared_gate, 0),
+        shared_up=(shared_up, 0),
+        shared_down=(shared_down, 0),
+    )
     pre_scores = (
         jnp.einsum("thc,uc->thu", pre_query, pre_latent, preferred_element_type=jnp.float32)
         * scale_qk
@@ -112,10 +142,7 @@
     dec_att = (dec_numer / dec_total[:, :, None]).astype(jnp.bfloat16)
     attention = jnp.concatenate([pre_att, dec_att], axis=0)
     spread = lax.all_to_all(attention, "dp", split_axis=1, concat_axis=0, tiled=True)
-    uv_full, out_full = (
-        lax.all_gather(uv_weight, "expert", axis=1, tiled=True),
-        lax.all_gather(out_weight, "expert", axis=1, tiled=True),
-    )
+    uv_full, out_full = weights["uv"], weights["out"]
     head_values = jnp.einsum(
         "thl,hlv->thv", spread, uv_full, preferred_element_type=jnp.float32
     ).astype(jnp.bfloat16)
@@ -154,9 +181,9 @@
     up_proj = jnp.dot(expert_rows, up_weight[0], preferred_element_type=jnp.float32)
     expert_act = (jax.nn.silu(gate_proj) * up_proj).astype(jnp.bfloat16)
     shared_gate_full, shared_up_full, shared_down_full = (
-        lax.all_gather(shared_gate, "expert", axis=0, tiled=True),
-        lax.all_gather(shared_up, "expert", axis=0, tiled=True),
-        lax.all_gather(shared_down, "expert", axis=0, tiled=True),
+        weights["shared_gate"],
+        weights["shared_up"],
+        weights["shared_down"],
     )
     shared_act = (
         jax.nn.silu(jnp.dot(group_tokens, shared_gate_full, preferred_element_type=jnp.float32))

time: 849 us -> 539 us (0.63)
  blocking collectives: 682 us -> 265 us
  waiting for transfers between devices: 32.1 us -> 118 us
  local copies, waits for them, and re-layouts: 32.9 us -> 57.3 us
    all_gather x4 -> x0, blocking collectives: 341 us -> none  [the longest x1 93.9 us: shards(): lax.all_gather(shared_down, 'expert', axis=0, tiled=True)]
    all_gather x1, waiting for transfers between devices: 17.4 us -> 103 us  [gather_weights(): lax.all_gather(flat, 'expert', axis=0, tiled=True).reshape(members, padded)]
    all_gather x1, blocking collectives: 87.1 us -> 13.5 us  [shards(): shared_piece = lax.all_gather(shared_act, 'dp', axis=1, tiled=True)]
    another operation x0 -> x3, local copies, waits for them, and re-layouts: none -> 9.56 us  [gather_weights(): out[n] = piece.reshape(shape)]
  transfers between devices with their start and end apart: 8 -> 8, of which waited for: 2 -> 2; matrix products, arithmetic and copies ran while one was open for 4% -> 9% of each run, Pallas kernels for 0% -> 0%
where the time goes in v1:
time: 539 us; the launch traced here: 537 us
  blocking collectives  265 us (49%)
  waiting for transfers between devices  118 us (22%)
  local copies, waits for them, and re-layouts  57.3 us (11%)
  starting transfers between devices  49.7 us (9%)
  matrix products  25.9 us (5%)
  between operations  16 us (3%)
  other arithmetic  6.09 us (1%)
    all_to_all x1, blocking collectives, shards(): lax.all_to_all(outgoing, 'expert', split_axis=0, concat_axis=0, tiled=True)  191 us
    all_gather x1, waiting for transfers between devices, gather_weights(): lax.all_gather(flat, 'expert', axis=0, tiled=True).reshape(members, padded)  103 us
    unnamed x1, blocking collectives  23.4 us
    all_to_all x1, starting transfers between devices, shards(): lax.all_to_all(expert_out.reshape(members, groups * capacity, col_width),...  15.3 us
    all_gather x1, blocking collectives, shards(): group_routes = lax.all_gather(routes, 'dp', axis=0, tiled=True)  14.7 us
    all_gather x1, waiting for transfers between devices, shards(): routed_piece = lax.all_gather(expert_act, 'dp', axis=1, tiled=True)  14.2 us
    all_to_all x1, starting transfers between devices, shards(): lax.all_to_all(gate_score.reshape(members, groups * capacity), 'expert',...  13.8 us
    all_gather x1, blocking collectives, shards(): group_tokens = lax.all_gather(normed, 'dp', axis=0, tiled=True)  13.8 us
  transfers between devices with their start and end apart: 8, of which 2 were waited for; matrix products, arithmetic and copies ran while one was open for 9% of the time, Pallas kernels for 0%

profile of v1, /device:TPU:1, one launch (start us, length us, event | category | flops | bytes accessed | tf_op | source)
XLA Modules:
  0.0 537.1 jit_solution(8622716932991419900)
XLA Ops:
  7.2 0.9 reshape.278
  8.1 0.8 reshape.279
  13.2 1.7 fusion.83
  14.8 0.9 convert_convert_fusion
  15.9 1.6 fusion.84
  19.6 1.6 fusion.21
  21.7 0.9 copy.83
  22.6 10.2 %all-to-all-start = ((bf16[17,16,512]{2,0,1:T(8,128)(2,1)}), bf16[17,16,512]{2,0,1:T(8,128)(2,1)S(1)}, u32[]{:S(2)}, u32[]{:S(2)}) async-start(bf16[17,16,512]{2,0,1:T(8,128)(2,1)} %copy.83), calls=%async_computation | async-start | bytes 786432 | tf_op jit(solution)/shard_map/all_to_all | solution.py:144
  32.8 14.7 %all-gather.2 = s32[8,17,6]{1,2,0:T(8,128)S(1)} all-gather(s32[1,17,6]{1,2,0:T(8,128)S(1)} %bitcast.151), channel_id=1, replica_groups=mesh['dp'=8,'expert'=64] {'dp'}, dimensions={0}, use_global_device_ids=true | all-gather | bytes 3672 | tf_op jit(solution)/shard_map/all_gather | solution.py:164
  47.8 2.0 select_reduce_fusion
  50.0 1.0 slice_reduce_fusion.5
  51.3 103.2 %all-gather.6.cloned.1.call-done = bf16[64,212,128]{2,1,0:T(8,128)(2,1)} async-done(((bf16[1,212,128]{2,1,0:T(8,128)(2,1)}), bf16[64,212,128]{2,1,0:T(8,128)(2,1)}) %all-gather.6.cloned.1.call-update) | async-done | bytes 3473424 | tf_op jit(solution)/shard_map/all_gather | solution.py:46
  154.5 2.4 copy.120
  157.0 1.8 copy-done.2
  158.9 0.8 reshape.289
  159.8 1.7 copy.86
  161.5 1.5 reshape.290
  163.4 23.4 %fusion = bf16[24,2048]{1,0:T(8,128)(2,1)S(1)} fusion(bf16[136,2048]{1,0:T(8,128)(2,1)S(1)} %fusion.1), kind=kCustom, calls=%all-reduce-scatter | all-reduce-scatter fusion | flops 393217 | bytes 657408
  186.9 1.3 collective-permute-start.1
  188.2 4.5 collective-permute-start
  192.7 4.5 collective-permute-start.2
  197.2 1.3 dynamic-slice.4
  200.1 13.8 %all-gather = bf16[8,17,2048]{2,1,0:T(8,128)(2,1)S(1)} all-gather(bf16[1,17,2048]{2,1,0:T(8,128)(2,1)S(1)} %fusion.51), channel_id=1, replica_groups=mesh['dp'=8,'expert'=64] {'dp'}, dimensions={0}, use_global_device_ids=true | all-gather | bytes 626688 | tf_op jit(solution)/shard_map/all_gather | solution.py:163
  213.9 1.4 convolution_bitcast_fusion
  215.3 6.3 %copy.94 = bf16[64,8,2,2048]{3,2,1,0:T(2,128)(2,1)} copy(bf16[64,8,2,2048]{3,0,2,1:T(8,128)(2,1)S(1)} %convolution_bitcast_fusion) | data formatting | bytes 8388608 | tf_op jit(solution)/shard_map/grxc,grd->xgcd/transpose | solution.py:172
  221.6 191.1 %all_to_all.46 = bf16[64,8,2,2048]{3,2,1,0:T(2,128)(2,1)} all-to-all(bf16[64,8,2,2048]{3,2,1,0:T(2,128)(2,1)} %copy.94), channel_id=1, replica_groups=mesh['dp'=8,'expert'=64] {'expert'}, dimensions={0} | all-to-all | bytes 8388608 | tf_op jit(solution)/shard_map/all_to_all | solution.py:175
  412.6 7.3 %reshape.292 = bf16[1024,2048]{1,0:T(8,128)(2,1)} reshape(bf16[64,8,2,2048]{3,2,1,0:T(2,128)(2,1)} %all_to_all.46) | data formatting | bytes 8388608 | tf_op jit(solution)/shard_map/reshape | solution.py:176
  419.9 3.9 fusion.28
  423.8 2.3 fusion.2
  426.9 3.4 fusion.86
  431.0 13.8 %all-to-all-start.2 = ((f32[64,1,16]{2,1,0:T(1,128)}), f32[64,1,16]{2,1,0:T(1,128)S(1)}, u32[]{:S(2)}, u32[]{:S(2)}) async-start(f32[64,1,16]{2,1,0:T(1,128)} %bitcast.28), calls=%async_computation.2 | async-start | bytes 65536 | tf_op jit(solution)/shard_map/all_to_all | solution.py:207
  444.9 14.2 %all-gather.8.cloned.1.call-done = bf16[1024,1408]{0,1:T(8,128)(2,1)} async-done(((bf16[1024,176]{0,1:T(8,128)(2,1)}), bf16[1024,1408]{0,1:T(8,128)(2,1)}) %all-gather.8.cloned.1.call-update) | async-done | bytes 2883600 | tf_op jit(solution)/shard_map/all_gather | solution.py:194
  459.1 3.6 convolution_convert_fusion
  462.8 15.3 %all-to-all-start.3 = ((bf16[64,16,256]{2,1,0:T(8,128)(2,1)}), bf16[64,16,256]{2,1,0:T(8,128)(2,1)S(1)}, u32[]{:S(2)}, u32[]{:S(2)}) async-start(bf16[64,16,256]{2,1,0:T(8,128)(2,1)} %bitcast.32), calls=%async_computation.3 | async-start | bytes 1048576 | tf_op jit(solution)/shard_map/all_to_all | solution.py:200
  478.1 3.0 fusion.82
  481.1 2.0 reshape_reshape.12
  483.1 3.8 reshape_reshape.11
  486.9 3.8 reshape_reshape.10
  490.6 1.0 reshape.320
  491.7 1.7 fusion.85
  493.4 1.7 fusion.11
  495.1 13.5 %all-gather.1 = bf16[8,176,136]{1,2,0:T(8,128)(2,1)S(1)} all-gather(bf16[1,176,136]{1,2,0:T(8,128)(2,1)S(1)} %fusion.11), channel_id=1, replica_groups=mesh['dp'=8,'expert'=64] {'dp'}, dimensions={0}, use_global_device_ids=true | all-gather | bytes 430848 | tf_op jit(solution)/shard_map/all_gather | solution.py:195
  508.7 1.2 reshape.322
  510.5 0.7 reduce.19
  511.3 3.5 gather_fusion
  515.3 3.4 gather_fusion.1
  519.4 1.3 fusion.10
  520.7 8.1 %all_to_all.47 = bf16[8,17,256]{2,1,0:T(8,128)(2,1)S(1)} all-to-all(bf16[8,17,256]{2,1,0:T(8,128)(2,1)S(1)} %convert_element_type.163), channel_id=1, replica_groups=mesh['dp'=8,'expert'=64] {'dp'}, dimensions={0} | all-to-all | bytes 139264 | tf_op jit(solution)/shard_map/all_to_all | solution.py:224
  (104 shorter events, 13.3 us)
Async XLA Ops:
  7.2 452.0 %copy-start = (bf16[1,1408,256]{2,1,0:T(8,128)(2,1)S(1)}, bf16[1,1408,256]{2,1,0:T(8,128)(2,1)}, u32[]{:S(2)}) copy-start(bf16[1,1408,256]{2,1,0:T(8,128)(2,1)} %param.36) | copy-start | bytes 2162692
  7.2 14.1 %copy-start.7 = (f32[16]{0:T(128)S(1)}, f32[16]{0:T(128)}, u32[]{:S(2)}) copy-start(f32[16]{0:T(128)} %param.28) | copy-start | bytes 196
  7.2 14.1 %copy-start.12 = (bf16[16,576]{1,0:T(8,128)(2,1)S(1)}, bf16[16,576]{1,0:T(8,128)(2,1)}, u32[]{:S(2)}) copy-start(bf16[16,576]{1,0:T(8,128)(2,1)} %param.21) | copy-start | bytes 55300
  7.2 147.3 %all-gather.6.cloned.1.call-start = ((), (), s32[]{:S(2)}) async-start(), calls=%async_computation.5 | async-start | bytes 3594240 | tf_op jit(solution)/shard_map/all_gather | solution.py:46
  11.8 0.6 copy-start.4
  13.1 19.7 %copy-start.8 = (s32[17,6]{0,1:T(8,128)S(1)}, s32[17,6]{0,1:T(8,128)}, u32[]{:S(2)}) copy-start(s32[17,6]{0,1:T(8,128)} %param.33) | copy-start | bytes 1228
  22.6 28.4 %all-to-all-start = ((bf16[17,16,512]{2,0,1:T(8,128)(2,1)}), bf16[17,16,512]{2,0,1:T(8,128)(2,1)S(1)}, u32[]{:S(2)}, u32[]{:S(2)}) async-start(bf16[17,16,512]{2,0,1:T(8,128)(2,1)} %copy.83), calls=%async_computation | async-start | bytes 786432 | tf_op jit(solution)/shard_map/all_to_all | solution.py:144
  32.8 426.3 %all-gather.8.cloned.1.call-start = ((), (), s32[]{:S(2)}) async-start(), calls=%async_computation.6 | async-start | bytes 3244032 | tf_op jit(solution)/shard_map/all_gather | solution.py:194
  157.0 1.8 copy-start.2
  159.7 37.5 %copy-start.9 = (bf16[2048]{0:T(1024)(128)(2,1)S(1)}, bf16[2048]{0:T(1024)(128)(2,1)}, u32[]{:S(2)}) copy-start(bf16[2048]{0:T(1024)(128)(2,1)} %param.31) | copy-start | bytes 12292
  159.7 40.1 %copy-start.3 = (bf16[16,2048]{1,0:T(8,128)(2,1)S(1)}, bf16[16,2048]{1,0:T(8,128)(2,1)}, u32[]{:S(2)}) copy-start(bf16[16,2048]{1,0:T(8,128)(2,1)} %param.22) | copy-start | bytes 196612
  159.7 40.1 %copy-start.6 = (bf16[1,2048]{1,0:T(2,128)(2,1)S(1)}, bf16[1,2048]{1,0:T(2,128)(2,1)}, u32[]{:S(2)}) copy-start(bf16[1,2048]{1,0:T(2,128)(2,1)} %param.25) | copy-start | bytes 12292
  186.9 12.3 %collective-permute-start.1 = (bf16[24,2048]{1,0:T(8,128)(2,1)S(1)}, bf16[24,2048]{1,0:T(8,128)(2,1)S(1)}, u32[]{:S(2)}, u32[]{:S(2)}) collective-permute-start(bf16[24,2048]{1,0:T(8,128)(2,1)S(1)} %fusion), channel_id=1, source_target_pairs={{0,128},{64,192},{128,256},{192,320},{256,384},{320,448},{1,129},{... | collective-permute-start | bytes 294920
  188.2 11.0 %collective-permute-start = (bf16[24,2048]{1,0:T(8,128)(2,1)S(1)}, bf16[24,2048]{1,0:T(8,128)(2,1)S(1)}, u32[]{:S(2)}, u32[]{:S(2)}) collective-permute-start(bf16[24,2048]{1,0:T(8,128)(2,1)S(1)} %fusion), channel_id=1, source_target_pairs={{0,64},{64,128},{128,192},{192,256},{256,320},{320,384},{384,448},... | collective-permute-start | bytes 294920
  192.7 6.5 %collective-permute-start.2 = (bf16[1,2048]{1,0:T(2,128)(2,1)S(1)}, bf16[1,2048]{1,0:T(2,128)(2,1)S(1)}, u32[]{:S(2)}, u32[]{:S(2)}) collective-permute-start(bf16[1,2048]{1,0:T(2,128)(2,1)S(1)} %slice.81), channel_id=1, source_target_pairs={{0,192},{64,256},{128,320},{192,384},{256,448},{1,193},{65,257},{1... | collective-permute-start | bytes 12296
  412.6 7.3 %copy-start.10 = (bf16[1,2048,176]{1,2,0:T(8,128)(2,1)S(1)}, bf16[1,2048,176]{1,2,0:T(8,128)(2,1)}, u32[]{:S(2)}) copy-start(bf16[1,2048,176]{1,2,0:T(8,128)(2,1)} %param.34) | copy-start | bytes 2162692
  419.9 3.9 copy-start.1
  419.9 3.9 copy-start.11
  423.8 3.1 copy-start.5
  431.0 31.7 %all-to-all-start.2 = ((f32[64,1,16]{2,1,0:T(1,128)}), f32[64,1,16]{2,1,0:T(1,128)S(1)}, u32[]{:S(2)}, u32[]{:S(2)}) async-start(f32[64,1,16]{2,1,0:T(1,128)} %bitcast.28), calls=%async_computation.2 | async-start | bytes 65536 | tf_op jit(solution)/shard_map/all_to_all | solution.py:207
  462.8 52.5 %all-to-all-start.3 = ((bf16[64,16,256]{2,1,0:T(8,128)(2,1)}), bf16[64,16,256]{2,1,0:T(8,128)(2,1)S(1)}, u32[]{:S(2)}, u32[]{:S(2)}) async-start(bf16[64,16,256]{2,1,0:T(8,128)(2,1)} %bitcast.32), calls=%async_computation.3 | async-start | bytes 1048576 | tf_op jit(solution)/shard_map/all_to_all | solution.py:200
Sparse Core Ops, SparseCore 0:
  12.6 141.8 all-gather.5
  426.3 32.7 all-gather.7

commit v2 on v1

--- a/solution.py
+++ b/solution.py
@@ -164,15 +164,15 @@
     group_routes = lax.all_gather(routes, "dp", axis=0, tiled=True)
     routes_by_group = group_routes.reshape(groups, rows_dev, TOPK)
     slots_by_group = jax.vmap(partial(assign_slots, experts=members))(routes_by_group)
-    tokens_by_group = group_tokens.reshape(groups, rows_dev, D)
-    all_matrix = jax.vmap(partial(dispatch_matrix, experts=members, capacity=capacity))(
-        routes_by_group, slots_by_group
-    )
-    all_matrix = all_matrix.reshape(groups, rows_dev, members, capacity)
-    outgoing = jnp.einsum(
-        "grxc,grd->xgcd", all_matrix, tokens_by_group, preferred_element_type=jnp.bfloat16
-    )
-    expert_rows = lax.all_to_all(outgoing, "expert", split_axis=0, concat_axis=0, tiled=True)
+    own_slots = assign_slots(routes, members)
+    own_matrix = dispatch_matrix(routes, own_slots, members, capacity).reshape(
+        rows_dev, members, capacity
+    )
+    outgoing = jnp.einsum("rxc,rd->xcd", own_matrix, normed, preferred_element_type=jnp.bfloat16)
+    arrived = lax.all_to_all(outgoing, "expert", split_axis=0, concat_axis=0, tiled=True)
+    expert_rows = lax.all_gather(
+        arrived.reshape(members, 1, capacity, D), "dp", axis=1, tiled=True
+    )
     expert_rows = expert_rows.reshape(-1, D)
     gate_score = jax.nn.sigmoid(
         jnp.dot(expert_rows, router[:, 0], preferred_element_type=jnp.float32)

time: 539 us -> 408 us (0.76)
  blocking collectives: 265 us -> 112 us
  waiting for transfers between devices: 118 us -> 161 us
  local copies, waits for them, and re-layouts: 57.3 us -> 48.4 us
  starting transfers between devices: 49.7 us -> 41.7 us
    all_to_all x1, blocking collectives: 191 us -> 40 us  [shards(): lax.all_to_all(outgoing, 'expert', split_axis=0, concat_axis=0, tiled=True)]
    all_gather x0 -> x1, waiting for transfers between devices: none -> 30.7 us  [shards(): lax.all_gather(arrived.reshape(members, 1, capacity, D), 'dp', axis=1, ti...]
    all_gather x1, waiting for transfers between devices: 14.2 us -> 0.02 us  [shards(): routed_piece = lax.all_gather(expert_act, 'dp', axis=1, tiled=True)]
    all_gather x1, waiting for transfers between devices: 103 us -> 113 us  [gather_weights(): lax.all_gather(flat, 'expert', axis=0, tiled=True).reshape(members, padded)]
    all_to_all x1, starting transfers between devices: 15.3 us -> 5.25 us  [shards(): lax.all_to_all(expert_out.reshape(members, groups * capacity, col_width),...]
    all_to_all x1, waiting for transfers between devices: 0.01 us -> 9.54 us  [shards(): lax.all_to_all(gate_score.reshape(members, groups * capacity), 'expert',...]
    reshape x1 -> x0, local copies, waits for them, and re-layouts: 7.28 us -> none  [shards(): expert_rows = expert_rows.reshape(-1, D)]
    all_to_all x1, waiting for transfers between devices: 0.01 us -> 7.1 us  [shards(): lax.all_to_all(attention, 'dp', split_axis=1, concat_axis=0, tiled=True)]
  transfers between devices with their start and end apart: 8 -> 9, of which waited for: 2 -> 4; matrix products, arithmetic and copies ran while one was open for 9% -> 11% of each run, Pallas kernels for 0% -> 0%
where the time goes in v2:
time: 408 us; the launch traced here: 407 us
  waiting for transfers between devices  161 us (39%)
  blocking collectives  112 us (27%)
  local copies, waits for them, and re-layouts  48.4 us (12%)
  starting transfers between devices  41.7 us (10%)
  matrix products  22.4 us (5%)
  between operations  15.7 us (4%)
  other arithmetic  6.48 us (2%)
    all_gather x1, waiting for transfers between devices, gather_weights(): lax.all_gather(flat, 'expert', axis=0, tiled=True).reshape(members, padded)  113 us
    all_to_all x1, blocking collectives, shards(): lax.all_to_all(outgoing, 'expert', split_axis=0, concat_axis=0, tiled=True)  40 us
    all_gather x1, waiting for transfers between devices, shards(): lax.all_gather(arrived.reshape(members, 1, capacity, D), 'dp', axis=1, ti...  30.7 us
    unnamed x1, blocking collectives  23.4 us
    all_to_all x1, starting transfers between devices, shards(): lax.all_to_all(gate_score.reshape(members, groups * capacity), 'expert',...  15.3 us
    all_gather x1, blocking collectives, shards(): group_tokens = lax.all_gather(normed, 'dp', axis=0, tiled=True)  14.6 us
    all_gather x1, blocking collectives, shards(): shared_piece = lax.all_gather(shared_act, 'dp', axis=1, tiled=True)  13.1 us
    all_gather x1, blocking collectives, shards(): group_routes = lax.all_gather(routes, 'dp', axis=0, tiled=True)  12.9 us
  transfers between devices with their start and end apart: 9, of which 4 were waited for; matrix products, arithmetic and copies ran while one was open for 11% of the time, Pallas kernels for 0%

profile of v2, /device:TPU:1, one launch (start us, length us, event | category | flops | bytes accessed | tf_op | source)
XLA Modules:
  0.0 407.2 jit_solution(2359535582982337715)
XLA Ops:
  7.2 0.7 bitcast_dynamic-update-slice_fusion
  8.7 0.8 reshape.327
  9.5 0.8 reshape.328
  13.2 1.7 fusion.86
  14.9 0.9 convert_convert_fusion
  16.0 1.6 fusion.87
  19.7 1.6 fusion.21
  21.8 0.9 copy.90
  22.7 10.2 %all-to-all-start = ((bf16[17,16,512]{2,0,1:T(8,128)(2,1)}), bf16[17,16,512]{2,0,1:T(8,128)(2,1)S(1)}, u32[]{:S(2)}, u32[]{:S(2)}) async-start(bf16[17,16,512]{2,0,1:T(8,128)(2,1)} %copy.90), calls=%async_computation | async-start | bytes 786432 | tf_op jit(solution)/shard_map/all_to_all | solution.py:144
  33.9 7.1 %all-to-all-done = bf16[17,16,512]{2,0,1:T(8,128)(2,1)S(1)} async-done(((bf16[17,16,512]{2,0,1:T(8,128)(2,1)}), bf16[17,16,512]{2,0,1:T(8,128)(2,1)S(1)}, u32[]{:S(2)}, u32[]{:S(2)}) %all-to-all-start) | async-done | bytes 278560 | tf_op jit(solution)/shard_map/all_to_all | solution.py:144
  41.2 113.4 %all-gather.8.cloned.1.call-done = bf16[64,212,128]{2,1,0:T(8,128)(2,1)} async-done(((bf16[1,212,128]{2,1,0:T(8,128)(2,1)}), bf16[64,212,128]{2,1,0:T(8,128)(2,1)}) %all-gather.8.cloned.1.call-update) | async-done | bytes 3473424 | tf_op jit(solution)/shard_map/all_gather | solution.py:46
  154.6 2.4 copy.129
  157.1 1.7 copy-done.2
  158.8 0.8 reshape.338
  159.7 1.7 copy.93
  161.4 1.5 reshape.339
  163.4 23.4 %fusion = bf16[24,2048]{1,0:T(8,128)(2,1)S(1)} fusion(bf16[136,2048]{1,0:T(8,128)(2,1)S(1)} %fusion.1), kind=kCustom, calls=%all-reduce-scatter | all-reduce-scatter fusion | flops 393217 | bytes 657408
  186.8 3.5 collective-permute-start
  190.4 2.0 collective-permute-start.1
  192.4 5.1 %collective-permute-start.2 = (bf16[1,2048]{1,0:T(2,128)(2,1)S(1)}, bf16[1,2048]{1,0:T(2,128)(2,1)S(1)}, u32[]{:S(2)}, u32[]{:S(2)}) collective-permute-start(bf16[1,2048]{1,0:T(2,128)(2,1)S(1)} %slice.81), channel_id=1, source_target_pairs={{0,192},{64,256},{128,320},{192,384},{256,448},{1,193},{65,257},{1... | collective-permute-start | bytes 12296
  197.5 1.3 dynamic-slice.4
  201.3 40.0 %all_to_all.46 = bf16[64,2,2048]{2,1,0:T(2,128)(2,1)S(1)} all-to-all(bf16[64,2,2048]{2,1,0:T(2,128)(2,1)S(1)} %copy.102), channel_id=1, replica_groups=mesh['dp'=8,'expert'=64] {'expert'}, dimensions={0} | all-to-all | bytes 1048576 | tf_op jit(solution)/shard_map/all_to_all | solution.py:172
  241.3 1.0 copy.103
  242.5 30.7 %all-gather.12.cloned.1.call-done = bf16[64,16,2048]{2,0,1:T(8,128)(2,1)} async-done(((bf16[64,2,2048]{2,0,1:T(8,128)(2,1)}), bf16[64,16,2048]{2,0,1:T(8,128)(2,1)}) %all-gather.12.cloned.1.call-update) | async-done | bytes 4194320 | tf_op jit(solution)/shard_map/all_gather | solution.py:173
  273.2 4.5 %copy.104 = bf16[64,16,2048]{2,1,0:T(8,128)(2,1)S(1)} copy(bf16[64,16,2048]{2,0,1:T(8,128)(2,1)} %all-gather.12.cloned.1.call-done) | data formatting | bytes 8388608 | tf_op jit(solution)/shard_map/all_gather | solution.py:173
  277.7 1.6 fusion.27
  279.6 2.3 fusion.2
  282.0 12.9 %all-gather.3 = s32[8,17,6]{1,2,0:T(8,128)S(1)} all-gather(s32[1,17,6]{1,2,0:T(8,128)S(1)} %bitcast.151), channel_id=1, replica_groups=mesh['dp'=8,'expert'=64] {'dp'}, dimensions={0}, use_global_device_ids=true | all-gather | bytes 3672 | tf_op jit(solution)/shard_map/all_gather | solution.py:164
  295.0 2.0 select_reduce_fusion
  297.8 3.5 fusion.89
  302.1 15.3 %all-to-all-start.2 = ((f32[64,1,16]{2,1,0:T(1,128)}), f32[64,1,16]{2,1,0:T(1,128)S(1)}, u32[]{:S(2)}, u32[]{:S(2)}) async-start(f32[64,1,16]{2,1,0:T(1,128)} %bitcast.27), calls=%async_computation.2 | async-start | bytes 65536 | tf_op jit(solution)/shard_map/all_to_all | solution.py:207
  317.5 3.6 convolution_convert_fusion
  321.1 9.5 %all-to-all-done.2 = f32[64,1,16]{2,1,0:T(1,128)S(1)} async-done(((f32[64,1,16]{2,1,0:T(1,128)}), f32[64,1,16]{2,1,0:T(1,128)S(1)}, u32[]{:S(2)}, u32[]{:S(2)}) %all-to-all-start.2) | async-done | bytes 4128 | tf_op jit(solution)/shard_map/all_to_all | solution.py:207
  330.7 5.2 %all-to-all-start.3 = ((bf16[64,16,256]{2,1,0:T(8,128)(2,1)}), bf16[64,16,256]{2,1,0:T(8,128)(2,1)S(1)}, u32[]{:S(2)}, u32[]{:S(2)}) async-start(bf16[64,16,256]{2,1,0:T(8,128)(2,1)} %bitcast.31), calls=%async_computation.3 | async-start | bytes 1048576 | tf_op jit(solution)/shard_map/all_to_all | solution.py:200
  335.9 2.8 fusion.85
  338.7 3.0 reshape_reshape.10
  341.8 3.0 reshape_reshape.11
  344.8 2.7 reshape_reshape.12
  347.5 14.6 %all-gather.1 = bf16[8,17,2048]{2,1,0:T(8,128)(2,1)S(1)} all-gather(bf16[1,17,2048]{2,1,0:T(8,128)(2,1)S(1)} %fusion.58), channel_id=1, replica_groups=mesh['dp'=8,'expert'=64] {'dp'}, dimensions={0}, use_global_device_ids=true | all-gather | bytes 626688 | tf_op jit(solution)/shard_map/all_gather | solution.py:163
  362.1 1.0 reshape.371
  363.1 1.4 fusion.88
  364.5 1.7 fusion.11
  366.2 13.1 %all-gather.2 = bf16[8,176,136]{1,2,0:T(8,128)(2,1)S(1)} all-gather(bf16[1,176,136]{1,2,0:T(8,128)(2,1)S(1)} %fusion.11), channel_id=1, replica_groups=mesh['dp'=8,'expert'=64] {'dp'}, dimensions={0}, use_global_device_ids=true | all-gather | bytes 430848 | tf_op jit(solution)/shard_map/all_gather | solution.py:195
  379.5 1.3 reshape.373
  382.1 3.5 gather_fusion
  386.1 3.4 gather_fusion.1
  390.2 1.3 fusion.10
  391.5 7.7 %all_to_all.47 = bf16[8,17,256]{2,1,0:T(8,128)(2,1)S(1)} all-to-all(bf16[8,17,256]{2,1,0:T(8,128)(2,1)S(1)} %convert_element_type.167), channel_id=1, replica_groups=mesh['dp'=8,'expert'=64] {'dp'}, dimensions={0} | all-to-all | bytes 139264 | tf_op jit(solution)/shard_map/all_to_all | solution.py:224
  (115 shorter events, 15.6 us)
Async XLA Ops:
  7.2 310.3 %copy-start = (bf16[1,1408,256]{2,1,0:T(8,128)(2,1)S(1)}, bf16[1,1408,256]{2,1,0:T(8,128)(2,1)}, u32[]{:S(2)}) copy-start(bf16[1,1408,256]{2,1,0:T(8,128)(2,1)} %param.36) | copy-start | bytes 2162692
  7.2 14.1 %copy-start.9 = (f32[16]{0:T(128)S(1)}, f32[16]{0:T(128)}, u32[]{:S(2)}) copy-start(f32[16]{0:T(128)} %param.28) | copy-start | bytes 196
  7.2 14.2 %copy-start.13 = (bf16[16,576]{1,0:T(8,128)(2,1)S(1)}, bf16[16,576]{1,0:T(8,128)(2,1)}, u32[]{:S(2)}) copy-start(bf16[16,576]{1,0:T(8,128)(2,1)} %param.21) | copy-start | bytes 55300
  7.2 147.4 %all-gather.8.cloned.1.call-start = ((), (), s32[]{:S(2)}) async-start(), calls=%async_computation.5 | async-start | bytes 3594240 | tf_op jit(solution)/shard_map/all_gather | solution.py:46
  11.9 0.6 copy-start.5
  13.2 19.7 %copy-start.6 = (s32[17,6]{0,1:T(8,128)S(1)}, s32[17,6]{0,1:T(8,128)}, u32[]{:S(2)}) copy-start(s32[17,6]{0,1:T(8,128)} %param.33) | copy-start | bytes 1228
  22.7 18.3 %all-to-all-start = ((bf16[17,16,512]{2,0,1:T(8,128)(2,1)}), bf16[17,16,512]{2,0,1:T(8,128)(2,1)S(1)}, u32[]{:S(2)}, u32[]{:S(2)}) async-start(bf16[17,16,512]{2,0,1:T(8,128)(2,1)} %copy.90), calls=%async_computation | async-start | bytes 786432 | tf_op jit(solution)/shard_map/all_to_all | solution.py:144
  32.9 240.3 %all-gather.12.cloned.1.call-start = ((), (), s32[]{:S(2)}) async-start(), calls=%async_computation.7 | async-start | bytes 4718592 | tf_op jit(solution)/shard_map/all_gather | solution.py:173
  157.0 1.8 copy-start.2
  159.7 37.8 %copy-start.10 = (bf16[2048]{0:T(1024)(128)(2,1)S(1)}, bf16[2048]{0:T(1024)(128)(2,1)}, u32[]{:S(2)}) copy-start(bf16[2048]{0:T(1024)(128)(2,1)} %param.31) | copy-start | bytes 12292
  161.4 38.7 %copy-start.4 = (bf16[16,2048]{1,0:T(8,128)(2,1)S(1)}, bf16[16,2048]{1,0:T(8,128)(2,1)}, u32[]{:S(2)}) copy-start(bf16[16,2048]{1,0:T(8,128)(2,1)} %param.22) | copy-start | bytes 196612
  161.4 38.7 %copy-start.8 = (bf16[1,2048]{1,0:T(2,128)(2,1)S(1)}, bf16[1,2048]{1,0:T(2,128)(2,1)}, u32[]{:S(2)}) copy-start(bf16[1,2048]{1,0:T(2,128)(2,1)} %param.25) | copy-start | bytes 12292
  186.8 12.6 %collective-permute-start = (bf16[24,2048]{1,0:T(8,128)(2,1)S(1)}, bf16[24,2048]{1,0:T(8,128)(2,1)S(1)}, u32[]{:S(2)}, u32[]{:S(2)}) collective-permute-start(bf16[24,2048]{1,0:T(8,128)(2,1)S(1)} %fusion), channel_id=1, source_target_pairs={{0,64},{64,128},{128,192},{192,256},{256,320},{320,384},{384,448},... | collective-permute-start | bytes 294920
  190.4 9.1 %collective-permute-start.1 = (bf16[24,2048]{1,0:T(8,128)(2,1)S(1)}, bf16[24,2048]{1,0:T(8,128)(2,1)S(1)}, u32[]{:S(2)}, u32[]{:S(2)}) collective-permute-start(bf16[24,2048]{1,0:T(8,128)(2,1)S(1)} %fusion), channel_id=1, source_target_pairs={{0,128},{64,192},{128,256},{192,320},{256,384},{320,448},{1,129},{... | collective-permute-start | bytes 294920
  192.4 7.0 %collective-permute-start.2 = (bf16[1,2048]{1,0:T(2,128)(2,1)S(1)}, bf16[1,2048]{1,0:T(2,128)(2,1)S(1)}, u32[]{:S(2)}, u32[]{:S(2)}) collective-permute-start(bf16[1,2048]{1,0:T(2,128)(2,1)S(1)} %slice.81), channel_id=1, source_target_pairs={{0,192},{64,256},{128,320},{192,384},{256,448},{1,193},{65,257},{1... | collective-permute-start | bytes 12296
  242.2 35.5 %copy-start.11 = (bf16[1,2048,176]{1,2,0:T(8,128)(2,1)S(1)}, bf16[1,2048,176]{1,2,0:T(8,128)(2,1)}, u32[]{:S(2)}) copy-start(bf16[1,2048,176]{1,2,0:T(8,128)(2,1)} %param.34) | copy-start | bytes 2162692
  242.2 75.2 %all-gather.10.cloned.1.call-start = ((), (), s32[]{:S(2)}) async-start(), calls=%async_computation.6 | async-start | bytes 3244032 | tf_op jit(solution)/shard_map/all_gather | solution.py:194
  277.7 1.9 copy-start.1
  277.7 1.9 copy-start.12
  279.6 18.2 %copy-start.7 = (bf16[2048,1]{0,1:T(2,128)(2,1)S(1)}, bf16[2048,1]{0,1:T(2,128)(2,1)}, u32[]{:S(2)}) copy-start(bf16[2048,1]{0,1:T(2,128)(2,1)} %param.32) | copy-start | bytes 12292
  302.1 28.6 %all-to-all-start.2 = ((f32[64,1,16]{2,1,0:T(1,128)}), f32[64,1,16]{2,1,0:T(1,128)S(1)}, u32[]{:S(2)}, u32[]{:S(2)}) async-start(f32[64,1,16]{2,1,0:T(1,128)} %bitcast.27), calls=%async_computation.2 | async-start | bytes 65536 | tf_op jit(solution)/shard_map/all_to_all | solution.py:207
  330.7 55.4 %all-to-all-start.3 = ((bf16[64,16,256]{2,1,0:T(8,128)(2,1)}), bf16[64,16,256]{2,1,0:T(8,128)(2,1)S(1)}, u32[]{:S(2)}, u32[]{:S(2)}) async-start(bf16[64,16,256]{2,1,0:T(8,128)(2,1)} %bitcast.31), calls=%async_computation.3 | async-start | bytes 1048576 | tf_op jit(solution)/shard_map/all_to_all | solution.py:200
  385.9 4.3 %copy-start.3 = (bf16[1408,256]{1,0:T(8,128)(2,1)S(1)}, bf16[1408,256]{1,0:T(8,128)(2,1)}, u32[]{:S(2)}) copy-start(bf16[1408,256]{1,0:T(8,128)(2,1)} %reshape_reshape.12) | copy-start | bytes 2162692
Sparse Core Ops, SparseCore 0:
  12.7 141.8 all-gather.7
  242.4 30.8 all-gather.11
  282.1 34.3 all-gather.9

commit v3 on v2

--- a/solution.py
+++ b/solution.py
@@ -3,6 +3,8 @@
 import jax
 import jax.numpy as jnp
 from jax import lax
+from jax.experimental import pallas as pl
+from jax.experimental.pallas import tpu as pltpu
 from jax.sharding import PartitionSpec as P
 
 D = 2048
@@ -36,14 +38,128 @@
     return total
 
 
+MESH_ID = pl.DeviceIdType.MESH
+
+
+def gather_kernel(nx, nz, shard_ref, out_ref, xs_sem, xr_sem, own_sem, rs_sem, ls_sem, rr_sem):
+    d = lax.axis_index("dp")
+    e = lax.axis_index("expert")
+    x = e // nz
+    z = e % nz
+    right = x * nz + (z + 1) % nz
+    left = x * nz + (z + nz - 1) % nz
+    steps_r = nz // 2
+    steps_l = nz - 1 - steps_r
+
+    barrier = pltpu.get_barrier_semaphore()
+    for k in range(1, nx):
+        peer = ((x + k) % nx) * nz + z
+        pl.semaphore_signal(barrier, 1, device_id=(d, peer), device_id_type=MESH_ID)
+    greeted = nx - 1
+    if nz > 1:
+        pl.semaphore_signal(barrier, 1, device_id=(d, right), device_id_type=MESH_ID)
+        greeted += 1
+    if nz > 2:
+        pl.semaphore_signal(barrier, 1, device_id=(d, left), device_id_type=MESH_ID)
+        greeted += 1
+    if greeted:
+        pl.semaphore_wait(barrier, greeted)
+
+    own = pltpu.make_async_copy(shard_ref, out_ref.at[z, x], own_sem)
+    own.start()
+    x_copies = []
+    for k in range(1, nx):
+        px = (x + k) % nx
+        send = pltpu.make_async_remote_copy(
+            src_ref=shard_ref,
+            dst_ref=out_ref.at[z, x],
+            send_sem=xs_sem.at[k],
+            recv_sem=xr_sem.at[x],
+            device_id=(d, px * nz + z),
+            device_id_type=MESH_ID,
+        )
+        send.start()
+        x_copies.append(send)
+    own.wait()
+    for k in range(1, nx):
+        px = (x + k) % nx
+        incoming = pltpu.make_async_remote_copy(
+            src_ref=shard_ref,
+            dst_ref=out_ref.at[z, px],
+            send_sem=xs_sem.at[k],
+            recv_sem=xr_sem.at[px],
+            device_id=(d, px * nz + z),
+            device_id_type=MESH_ID,
+        )
+        incoming.wait_recv()
+
+    def ring_copy(group, sems, step, target):
+        return pltpu.make_async_remote_copy(
+            src_ref=out_ref.at[group],
+            dst_ref=out_ref.at[group],
+            send_sem=sems.at[step],
+            recv_sem=rr_sem.at[group],
+            device_id=(d, target),
+            device_id_type=MESH_ID,
+        )
+
+    sent = []
+    for s in range(max(steps_r, steps_l)):
+        if s < steps_r:
+            group = (z - s + nz) % nz
+            if s > 0:
+                ring_copy(group, rs_sem, s, right).wait_recv()
+            c = ring_copy(group, rs_sem, s, right)
+            c.start()
+            sent.append(c)
+        if s < steps_l:
+            group = (z + s) % nz
+            if s > 0:
+                ring_copy(group, ls_sem, s, left).wait_recv()
+            c = ring_copy(group, ls_sem, s, left)
+            c.start()
+            sent.append(c)
+    if steps_r > 0:
+        ring_copy((z - steps_r + nz) % nz, rs_sem, 0, right).wait_recv()
+    if steps_l > 0:
+        ring_copy((z + steps_l) % nz, ls_sem, 0, left).wait_recv()
+    for c in sent:
+        c.wait_send()
+    for c in x_copies:
+        c.wait_send()
+
+
+def expert_gather(flat, members):
+    nz = 16 if members % 16 == 0 else members
+    nx = members // nz
+    rows, lanes = flat.shape
+    steps = max(nz // 2, 1)
+    out = pl.pallas_call(
+        partial(gather_kernel, nx, nz),
+        out_shape=jax.ShapeDtypeStruct((nz, nx, rows, lanes), flat.dtype),
+        in_specs=[pl.BlockSpec(memory_space=pltpu.VMEM)],
+        out_specs=pl.BlockSpec(memory_space=pltpu.VMEM),
+        scratch_shapes=[
+            pltpu.SemaphoreType.DMA((max(nx, 1),)),
+            pltpu.SemaphoreType.DMA((max(nx, 1),)),
+            pltpu.SemaphoreType.DMA(()),
+            pltpu.SemaphoreType.DMA((steps,)),
+            pltpu.SemaphoreType.DMA((steps,)),
+            pltpu.SemaphoreType.DMA((nz,)),
+        ],
+        compiler_params=pltpu.CompilerParams(collective_id=0, has_side_effects=True),
+    )(flat)
+    return jnp.swapaxes(out, 0, 1).reshape(members, rows * lanes)
+
+
 def gather_weights(members, **parts):
     names = list(parts)
     flat = jnp.concatenate([parts[n][0].reshape(-1) for n in names])
     lanes = 128
     total = flat.shape[0]
-    padded = -(-total // lanes) * lanes
-    flat = jnp.pad(flat, (0, padded - total)).reshape(1, padded // lanes, lanes)
-    everyone = lax.all_gather(flat, "expert", axis=0, tiled=True).reshape(members, padded)
+    padded = -(-total // (lanes * 8)) * lanes * 8
+    flat = jnp.pad(flat, (0, padded - total)).reshape(padded // lanes, lanes)
+    everyone = expert_gather(flat, members)
     out = {}
     start = 0
     for n in names:

time: 408 us -> 337 us (0.83)
  waiting for transfers between devices: 161 us -> 40 us
  Pallas kernels: 0 us -> 58.5 us
  local copies, waits for them, and re-layouts: 48.4 us -> 42.8 us
    all_gather x1 -> x0, waiting for transfers between devices: 113 us -> none  [gather_weights(): lax.all_gather(flat, 'expert', axis=0, tiled=True).reshape(members, padded)]
    pallas_call x0 -> x1, Pallas kernels: none -> 58.5 us  [expert_gather(): pl.pallas_call(partial(gather_kernel, nx, nz), out_shape=jax.ShapeDtypeSt...]
    all_to_all x1, waiting for transfers between devices: 7.1 us -> 0.01 us  [shards(): lax.all_to_all(attention, 'dp', split_axis=1, concat_axis=0, tiled=True)]
    unnamed x44 -> x54, local copies, waits for them, and re-layouts: 11.8 us -> 7.75 us
  transfers between devices with their start and end apart: 9 -> 8, of which waited for: 4 -> 2; matrix products, arithmetic and copies ran while one was open for 11% -> 12% of each run, Pallas kernels for 0% -> 17%
where the time goes in v3:
time: 337 us; the launch traced here: 336 us
  blocking collectives  108 us (32%)
  Pallas kernels  58.5 us (17%)
  local copies, waits for them, and re-layouts  42.8 us (13%)
  starting transfers between devices  41.6 us (12%)
  waiting for transfers between devices  40 us (12%)
  matrix products  21.9 us (6%)
  between operations  16.3 us (5%)
  other arithmetic  6.49 us (2%)
    pallas_call x1, Pallas kernels, expert_gather(): pl.pallas_call(partial(gather_kernel, nx, nz), out_shape=jax.ShapeDtypeSt...  58.5 us
    all_to_all x1, blocking collectives, shards(): lax.all_to_all(outgoing, 'expert', split_axis=0, concat_axis=0, tiled=True)  38.8 us
    all_gather x1, waiting for transfers between devices, shards(): lax.all_gather(arrived.reshape(members, 1, capacity, D), 'dp', axis=1, ti...  30.4 us
    unnamed x1, blocking collectives  21.1 us
    all_to_all x1, starting transfers between devices, shards(): lax.all_to_all(gate_score.reshape(members, groups * capacity), 'expert',...  15.3 us
    all_gather x1, blocking collectives, shards(): group_tokens = lax.all_gather(normed, 'dp', axis=0, tiled=True)  14.4 us
    all_gather x1, blocking collectives, shards(): shared_piece = lax.all_gather(shared_act, 'dp', axis=1, tiled=True)  13.1 us
    all_gather x1, blocking collectives, shards(): group_routes = lax.all_gather(routes, 'dp', axis=0, tiled=True)  12.9 us
  transfers between devices with their start and end apart: 8, of which 2 were waited for; matrix products, arithmetic and copies ran while one was open for 12% of the time, Pallas kernels for 17%

profile of v3, /device:TPU:1, one launch (start us, length us, event | category | flops | bytes accessed | tf_op | source)
XLA Modules:
  0.0 335.6 jit_solution(10591870005080448376)
XLA Ops:
  8.0 0.7 slice_convert_fusion
  8.8 1.7 fusion.86
  10.4 0.9 convert_convert_fusion
  11.3 1.6 fusion.87
  13.7 0.7 exponential_add_fusion
  14.4 1.1 fusion.3
  16.1 0.9 copy.94
  17.0 10.2 %all-to-all-start = ((bf16[17,16,512]{2,0,1:T(8,128)(2,1)}), bf16[17,16,512]{2,0,1:T(8,128)(2,1)S(1)}, u32[]{:S(2)}, u32[]{:S(2)}) async-start(bf16[17,16,512]{2,0,1:T(8,128)(2,1)} %copy.94), calls=%async_computation | async-start | bytes 786432 | tf_op jit(solution)/shard_map/all_to_all | solution.py:260
  29.0 58.5 %shard_map.203 = bf16[16,4,216,128]{3,2,1,0:T(8,128)(2,1)} custom-call(bf16[216,128]{1,0:T(8,128)(2,1)} %pad_bitcast_fusion.shard_ref), custom_call_target="tpu_custom_call" | custom-call | tf_op jit(solution)/shard_map/pallas_call | solution.py:137
  87.5 2.3 copy.91
  90.3 1.7 copy-done.2
  92.1 0.8 reshape.338
  92.9 1.7 copy.97
  94.6 1.5 reshape.339
  96.1 0.8 copy.120
  98.1 1.4 fusion.1
  99.5 21.1 %fusion = bf16[24,2048]{1,0:T(8,128)(2,1)S(1)} fusion(bf16[136,2048]{1,0:T(8,128)(2,1)S(1)} %fusion.1), kind=kCustom, calls=%all-reduce-scatter | all-reduce-scatter fusion | flops 393217 | bytes 657408
  120.7 3.7 %collective-permute-start = (bf16[24,2048]{1,0:T(8,128)(2,1)S(1)}, bf16[24,2048]{1,0:T(8,128)(2,1)S(1)}, u32[]{:S(2)}, u32[]{:S(2)}) collective-permute-start(bf16[24,2048]{1,0:T(8,128)(2,1)S(1)} %fusion), channel_id=1, source_target_pairs={{0,64},{64,128},{128,192},{192,256},{256,320},{320,384},{384,448},... | collective-permute-start | bytes 294920
  124.3 2.0 collective-permute-start.1
  126.4 5.0 %collective-permute-start.2 = (bf16[1,2048]{1,0:T(2,128)(2,1)S(1)}, bf16[1,2048]{1,0:T(2,128)(2,1)S(1)}, u32[]{:S(2)}, u32[]{:S(2)}) collective-permute-start(bf16[1,2048]{1,0:T(2,128)(2,1)S(1)} %slice.81), channel_id=1, source_target_pairs={{0,192},{64,256},{128,320},{192,384},{256,448},{1,193},{65,257},{1... | collective-permute-start | bytes 12296
  131.5 1.3 dynamic-slice.4
  135.2 38.8 %all_to_all.46 = bf16[64,2,2048]{2,1,0:T(2,128)(2,1)S(1)} all-to-all(bf16[64,2,2048]{2,1,0:T(2,128)(2,1)S(1)} %copy.106), channel_id=1, replica_groups=mesh['dp'=8,'expert'=64] {'expert'}, dimensions={0} | all-to-all | bytes 1048576 | tf_op jit(solution)/shard_map/all_to_all | solution.py:288
  174.0 0.9 copy.107
  175.2 30.4 %all-gather.9.cloned.1.call-done = bf16[64,16,2048]{2,0,1:T(8,128)(2,1)} async-done(((bf16[64,2,2048]{2,0,1:T(8,128)(2,1)}), bf16[64,16,2048]{2,0,1:T(8,128)(2,1)}) %all-gather.9.cloned.1.call-update) | async-done | bytes 4194320 | tf_op jit(solution)/shard_map/all_gather | solution.py:289
  205.7 4.5 %copy.108 = bf16[64,16,2048]{2,1,0:T(8,128)(2,1)S(1)} copy(bf16[64,16,2048]{2,0,1:T(8,128)(2,1)} %all-gather.9.cloned.1.call-done) | data formatting | bytes 8388608 | tf_op jit(solution)/shard_map/all_gather | solution.py:289
  210.2 1.6 fusion.27
  212.1 2.3 fusion.2
  214.4 2.5 fusion.85
  217.0 2.0 reshape_reshape.10
  219.0 3.0 reshape_reshape.11
  222.0 12.9 %all-gather.3 = s32[8,17,6]{1,2,0:T(8,128)S(1)} all-gather(s32[1,17,6]{1,2,0:T(8,128)S(1)} %bitcast.155), channel_id=1, replica_groups=mesh['dp'=8,'expert'=64] {'dp'}, dimensions={0}, use_global_device_ids=true | all-gather | bytes 3672 | tf_op jit(solution)/shard_map/all_gather | solution.py:280
  235.0 2.0 select_reduce_fusion
  237.6 3.5 %fusion.89 = f32[1,1024]{1,0:T(1,128)S(1)} fusion(bf16[1024,2048]{1,0:T(8,128)(2,1)} %bitcast.138, bf16[2048,1]{0,1:T(2,128)(2,1)S(1)} %copy-done.12), kind=kOutput, calls=%fused_computation.146 | convolution fusion | flops 4194304 | bytes 4202496 | tf_op jit(solution)/shard_map/dot_general | solution.py:294
  241.0 0.7 all_to_all.37
  241.8 15.3 %all-to-all-start.2 = ((f32[64,1,16]{2,1,0:T(1,128)}), f32[64,1,16]{2,1,0:T(1,128)S(1)}, u32[]{:S(2)}, u32[]{:S(2)}) async-start(f32[64,1,16]{2,1,0:T(1,128)} %bitcast.28), calls=%async_computation.2 | async-start | bytes 65536 | tf_op jit(solution)/shard_map/all_to_all | solution.py:323
  257.1 3.7 %convolution_convert_fusion = bf16[1024,256]{1,0:T(8,128)(2,1)} fusion(bf16[1024,1408]{0,1:T(8,128)(2,1)} %all-gather.7.cloned.1.call-done, bf16[1,1408,256]{2,1,0:T(8,128)(2,1)S(1)} %copy-done), kind=kOutput, calls=%fused_computation.5 | convolution fusion | flops 738459648 | bytes 4128768 | tf_op jit(solution)/shard_map/dot_general | solution.py:312
  260.9 9.5 %all-to-all-done.2 = f32[64,1,16]{2,1,0:T(1,128)S(1)} async-done(((f32[64,1,16]{2,1,0:T(1,128)}), f32[64,1,16]{2,1,0:T(1,128)S(1)}, u32[]{:S(2)}, u32[]{:S(2)}) %all-to-all-start.2) | async-done | bytes 4128 | tf_op jit(solution)/shard_map/all_to_all | solution.py:323
  270.3 5.1 %all-to-all-start.3 = ((bf16[64,16,256]{2,1,0:T(8,128)(2,1)}), bf16[64,16,256]{2,1,0:T(8,128)(2,1)S(1)}, u32[]{:S(2)}, u32[]{:S(2)}) async-start(bf16[64,16,256]{2,1,0:T(8,128)(2,1)} %bitcast.151), calls=%async_computation.3 | async-start | bytes 1048576 | tf_op jit(solution)/shard_map/all_to_all | solution.py:316
  275.7 1.7 reshape_reshape.12
  277.5 14.4 %all-gather.1 = bf16[8,17,2048]{2,1,0:T(8,128)(2,1)S(1)} all-gather(bf16[1,17,2048]{2,1,0:T(8,128)(2,1)S(1)} %fusion.58), channel_id=1, replica_groups=mesh['dp'=8,'expert'=64] {'dp'}, dimensions={0}, use_global_device_ids=true | all-gather | bytes 626688 | tf_op jit(solution)/shard_map/all_gather | solution.py:279
  292.0 1.0 reshape.371
  293.0 1.4 fusion.88
  294.4 1.7 fusion.11
  296.1 13.1 %all-gather.2 = bf16[8,176,136]{1,2,0:T(8,128)(2,1)S(1)} all-gather(bf16[1,176,136]{1,2,0:T(8,128)(2,1)S(1)} %fusion.11), channel_id=1, replica_groups=mesh['dp'=8,'expert'=64] {'dp'}, dimensions={0}, use_global_device_ids=true | all-gather | bytes 430848 | tf_op jit(solution)/shard_map/all_gather | solution.py:311
  310.4 0.7 reduce.19
  311.2 3.5 %gather_fusion = f32[816]{0:T(1024)S(1)} fusion(f32[1024]{0:T(1024)S(1)} %reshape.342, s32[1024]{0:T(1024)S(1)} %pad_clamp_fusion), kind=kCustom, calls=%fused_computation | custom fusion | bytes 9792 | tf_op jit(solution)/shard_map/jit(_take)/gather | solution.py:335
  315.2 3.4 %gather_fusion.1 = bf16[816,256]{1,0:T(8,128)(2,1)S(1)} fusion(bf16[1024,256]{1,0:T(8,128)(2,1)S(1)} %bitcast.135, s32[1024]{0:T(1024)S(1)} %pad_clamp_fusion), kind=kCustom, calls=%fused_computation.1 | custom fusion | bytes 838848 | tf_op jit(solution)/shard_map/jit(_take)/gather | solution.py:334
  319.6 7.7 %all_to_all.47 = bf16[8,17,256]{2,1,0:T(8,128)(2,1)S(1)} all-to-all(bf16[8,17,256]{2,1,0:T(8,128)(2,1)S(1)} %convert_element_type.169), channel_id=1, replica_groups=mesh['dp'=8,'expert'=64] {'dp'}, dimensions={0} | all-to-all | bytes 139264 | tf_op jit(solution)/shard_map/all_to_all | solution.py:340
  (125 shorter events, 12.3 us)
Async XLA Ops:
  7.2 250.0 %copy-start = (bf16[1,1408,256]{2,1,0:T(8,128)(2,1)S(1)}, bf16[1,1408,256]{2,1,0:T(8,128)(2,1)}, u32[]{:S(2)}) copy-start(bf16[1,1408,256]{2,1,0:T(8,128)(2,1)} %param.36) | copy-start | bytes 2162692
  7.2 8.5 %copy-start.5 = (bf16[1,1024,576]{1,2,0:T(8,128)(2,1)S(1)}, bf16[1,1024,576]{1,2,0:T(8,128)(2,1)}, u32[]{:S(2)}) copy-start(bf16[1,1024,576]{1,2,0:T(8,128)(2,1)} %param.27) | copy-start | bytes 3538948
  7.2 8.5 %copy-start.14 = (f32[16]{0:T(128)S(1)}, f32[16]{0:T(128)}, u32[]{:S(2)}) copy-start(f32[16]{0:T(128)} %param.28) | copy-start | bytes 196
  8.7 18.6 %copy-start.16 = (bf16[2,8,128]{2,1,0:T(8,128)(2,1)S(1)}, bf16[2,8,128]{2,1,0:T(8,128)(2,1)}, u32[]{:S(2)}) copy-start(bf16[2,8,128]{2,1,0:T(8,128)(2,1)} %param.29) | copy-start | bytes 12292
  8.7 18.6 %copy-start.9 = (bf16[2,2,2048]{2,1,0:T(2,128)(2,1)S(1)}, bf16[2,2,2048]{2,1,0:T(2,128)(2,1)}, u32[]{:S(2)}) copy-start(bf16[2,2,2048]{2,1,0:T(2,128)(2,1)} %param.30) | copy-start | bytes 49156
  8.7 18.6 %copy-start.7 = (bf16[32,176]{1,0:T(8,128)(2,1)S(1)}, bf16[32,176]{1,0:T(8,128)(2,1)}, u32[]{:S(2)}) copy-start(bf16[32,176]{1,0:T(8,128)(2,1)} %param.37) | copy-start | bytes 33796
  8.7 18.7 %copy-start.8 = (bf16[32,176]{1,0:T(8,128)(2,1)S(1)}, bf16[32,176]{1,0:T(8,128)(2,1)}, u32[]{:S(2)}) copy-start(bf16[32,176]{1,0:T(8,128)(2,1)} %param.38) | copy-start | bytes 33796
  8.7 18.8 %copy-start.11 = (bf16[22,256]{1,0:T(8,128)(2,1)S(1)}, bf16[22,256]{1,0:T(8,128)(2,1)}, u32[]{:S(2)}) copy-start(bf16[22,256]{1,0:T(8,128)(2,1)} %param.39) | copy-start | bytes 33796
  17.0 80.8 %all-to-all-start = ((bf16[17,16,512]{2,0,1:T(8,128)(2,1)}), bf16[17,16,512]{2,0,1:T(8,128)(2,1)S(1)}, u32[]{:S(2)}, u32[]{:S(2)}) async-start(bf16[17,16,512]{2,0,1:T(8,128)(2,1)} %copy.94), calls=%async_computation | async-start | bytes 786432 | tf_op jit(solution)/shard_map/all_to_all | solution.py:260
  27.2 178.4 %all-gather.9.cloned.1.call-start = ((), (), s32[]{:S(2)}) async-start(), calls=%async_computation.6 | async-start | bytes 4718592 | tf_op jit(solution)/shard_map/all_gather | solution.py:289
  90.2 1.8 copy-start.2
  92.1 4.8 %copy-start.10 = (s32[17,6]{0,1:T(8,128)S(1)}, s32[17,6]{0,1:T(8,128)}, u32[]{:S(2)}) copy-start(s32[17,6]{0,1:T(8,128)} %param.33) | copy-start | bytes 1228
  94.6 36.8 %copy-start.15 = (bf16[2048]{0:T(1024)(128)(2,1)S(1)}, bf16[2048]{0:T(1024)(128)(2,1)}, u32[]{:S(2)}) copy-start(bf16[2048]{0:T(1024)(128)(2,1)} %param.31) | copy-start | bytes 12292
  94.6 39.4 %copy-start.6 = (bf16[16,2048]{1,0:T(8,128)(2,1)S(1)}, bf16[16,2048]{1,0:T(8,128)(2,1)}, u32[]{:S(2)}) copy-start(bf16[16,2048]{1,0:T(8,128)(2,1)} %param.22) | copy-start | bytes 196612
  94.6 39.4 %copy-start.13 = (bf16[1,2048]{1,0:T(2,128)(2,1)S(1)}, bf16[1,2048]{1,0:T(2,128)(2,1)}, u32[]{:S(2)}) copy-start(bf16[1,2048]{1,0:T(2,128)(2,1)} %param.25) | copy-start | bytes 12292
  120.7 12.7 %collective-permute-start = (bf16[24,2048]{1,0:T(8,128)(2,1)S(1)}, bf16[24,2048]{1,0:T(8,128)(2,1)S(1)}, u32[]{:S(2)}, u32[]{:S(2)}) collective-permute-start(bf16[24,2048]{1,0:T(8,128)(2,1)S(1)} %fusion), channel_id=1, source_target_pairs={{0,64},{64,128},{128,192},{192,256},{256,320},{320,384},{384,448},... | collective-permute-start | bytes 294920
  124.3 9.1 %collective-permute-start.1 = (bf16[24,2048]{1,0:T(8,128)(2,1)S(1)}, bf16[24,2048]{1,0:T(8,128)(2,1)S(1)}, u32[]{:S(2)}, u32[]{:S(2)}) collective-permute-start(bf16[24,2048]{1,0:T(8,128)(2,1)S(1)} %fusion), channel_id=1, source_target_pairs={{0,128},{64,192},{128,256},{192,320},{256,384},{320,448},{1,129},{... | collective-permute-start | bytes 294920
  126.4 7.0 %collective-permute-start.2 = (bf16[1,2048]{1,0:T(2,128)(2,1)S(1)}, bf16[1,2048]{1,0:T(2,128)(2,1)S(1)}, u32[]{:S(2)}, u32[]{:S(2)}) collective-permute-start(bf16[1,2048]{1,0:T(2,128)(2,1)S(1)} %slice.81), channel_id=1, source_target_pairs={{0,192},{64,256},{128,320},{192,384},{256,448},{1,193},{65,257},{1... | collective-permute-start | bytes 12296
  175.0 35.2 %copy-start.17 = (bf16[1,2048,176]{1,2,0:T(8,128)(2,1)S(1)}, bf16[1,2048,176]{1,2,0:T(8,128)(2,1)}, u32[]{:S(2)}) copy-start(bf16[1,2048,176]{1,2,0:T(8,128)(2,1)} %param.34) | copy-start | bytes 2162692
  175.0 82.1 %all-gather.7.cloned.1.call-start = ((), (), s32[]{:S(2)}) async-start(), calls=%async_computation.5 | async-start | bytes 3244032 | tf_op jit(solution)/shard_map/all_gather | solution.py:310
  210.1 1.9 copy-start.1
  210.2 1.9 copy-start.18
  214.4 23.1 %copy-start.12 = (bf16[2048,1]{0,1:T(2,128)(2,1)S(1)}, bf16[2048,1]{0,1:T(2,128)(2,1)}, u32[]{:S(2)}) copy-start(bf16[2048,1]{0,1:T(2,128)(2,1)} %param.32) | copy-start | bytes 12292
  241.8 28.6 %all-to-all-start.2 = ((f32[64,1,16]{2,1,0:T(1,128)}), f32[64,1,16]{2,1,0:T(1,128)S(1)}, u32[]{:S(2)}, u32[]{:S(2)}) async-start(f32[64,1,16]{2,1,0:T(1,128)} %bitcast.28), calls=%async_computation.2 | async-start | bytes 65536 | tf_op jit(solution)/shard_map/all_to_all | solution.py:323
  257.1 18.6 %copy-start.4 = (bf16[64,5632]{1,0:T(8,128)(2,1)S(1)}, bf16[64,5632]{1,0:T(8,128)(2,1)}, u32[]{:S(2)}) copy-start(bf16[64,5632]{1,0:T(8,128)(2,1)} %get-tuple-element.12) | copy-start | bytes 2162692
  270.3 44.8 %all-to-all-start.3 = ((bf16[64,16,256]{2,1,0:T(8,128)(2,1)}), bf16[64,16,256]{2,1,0:T(8,128)(2,1)S(1)}, u32[]{:S(2)}, u32[]{:S(2)}) async-start(bf16[64,16,256]{2,1,0:T(8,128)(2,1)} %bitcast.151), calls=%async_computation.3 | async-start | bytes 1048576 | tf_op jit(solution)/shard_map/all_to_all | solution.py:316
  314.8 4.5 %copy-start.3 = (bf16[1408,256]{1,0:T(8,128)(2,1)S(1)}, bf16[1408,256]{1,0:T(8,128)(2,1)}, u32[]{:S(2)}) copy-start(bf16[1408,256]{1,0:T(8,128)(2,1)} %reshape_reshape.12) | copy-start | bytes 2162692
Sparse Core Ops, SparseCore 0:
  175.1 30.4 all-gather.8
  214.5 34.3 all-gather.6

commit v4 on v3

--- a/solution.py
+++ b/solution.py
@@ -152,14 +152,18 @@
     return jnp.swapaxes(out, 0, 1).reshape(members, rows * lanes)
 
 
-def gather_weights(members, **parts):
+def gather_weights(members, by_kernel, **parts):
     names = list(parts)
     flat = jnp.concatenate([parts[n][0].reshape(-1) for n in names])
     lanes = 128
     total = flat.shape[0]
     padded = -(-total // (lanes * 8)) * lanes * 8
     flat = jnp.pad(flat, (0, padded - total)).reshape(padded // lanes, lanes)
-    everyone = expert_gather(flat, members)
+    if by_kernel:
+        everyone = expert_gather(flat, members)
+    else:
+        everyone = lax.all_gather(flat[None], "expert", axis=0, tiled=True)
+        everyone = everyone.reshape(members, padded)
     out = {}
     start = 0
     for n in names:
@@ -203,11 +207,18 @@
     scale_qk = (QK_NOPE + ROPE) ** (-0.5)
     weights = gather_weights(
         members,
+        True,
         uv=(uv_weight, 1),
         out=(out_weight, 1),
-        shared_gate=(shared_gate, 0),
-        shared_up=(shared_up, 0),
-        shared_down=(shared_down, 0),
+    )
+    weights.update(
+        gather_weights(
+            members,
+            False,
+            shared_gate=(shared_gate, 0),
+            shared_up=(shared_up, 0),
+            shared_down=(shared_down, 0),
+        )
     )
     pre_scores = (
         jnp.einsum("thc,uc->thu", pre_query, pre_latent, preferred_element_type=jnp.float32)
@@ -286,6 +297,8 @@
     )
     outgoing = jnp.einsum("rxc,rd->xcd", own_matrix, normed, preferred_element_type=jnp.bfloat16)
     arrived = lax.all_to_all(outgoing, "expert", split_axis=0, concat_axis=0, tiled=True)
+    shared_ready = (weights["shared_gate"], weights["shared_up"], weights["shared_down"])
+    arrived, shared_ready = lax.optimization_barrier((arrived, shared_ready))
     expert_rows = lax.all_gather(
         arrived.reshape(members, 1, capacity, D), "dp", axis=1, tiled=True
     )
@@ -296,11 +309,7 @@
     gate_proj = jnp.dot(expert_rows, gate_weight[0], preferred_element_type=jnp.float32)
     up_proj = jnp.dot(expert_rows, up_weight[0], preferred_element_type=jnp.float32)
     expert_act = (jax.nn.silu(gate_proj) * up_proj).astype(jnp.bfloat16)
-    shared_gate_full, shared_up_full, shared_down_full = (
-        weights["shared_gate"],
-        weights["shared_up"],
-        weights["shared_down"],
-    )
+    shared_gate_full, shared_up_full, shared_down_full = shared_ready
     shared_act = (
         jax.nn.silu(jnp.dot(group_tokens, shared_gate_full, preferred_element_type=jnp.float32))
         * jnp.dot(group_tokens, shared_up_full, preferred_element_type=jnp.float32)

time: 337 us -> 335 us (level)
  waiting for transfers between devices: 40 us -> 88.5 us
  blocking collectives: 108 us -> 71.5 us
  Pallas kernels: 58.5 us -> 36.7 us
  starting transfers between devices: 41.6 us -> 48.3 us
    all_to_all x1 -> x0, blocking collectives: 38.8 us -> none  [shards(): lax.all_to_all(outgoing, 'expert', split_axis=0, concat_axis=0, tiled=True)]
    all_gather x0 -> x1, waiting for transfers between devices: none -> 37.4 us  [gather_weights(): everyone = lax.all_gather(flat[None], 'expert', axis=0, tiled=True)]
    pallas_call x1, Pallas kernels: 58.5 us -> 36.7 us  [expert_gather(): pl.pallas_call(partial(gather_kernel, nx, nz), out_shape=jax.ShapeDtypeSt...]
    all_gather x1, waiting for transfers between devices: 30.4 us -> 41.5 us  [shards(): lax.all_gather(arrived.reshape(members, 1, capacity, D), 'dp', axis=1, ti...]
    all_to_all x0 -> x1, starting transfers between devices: none -> 7.85 us  [shards(): lax.all_to_all(outgoing, 'expert', split_axis=0, concat_axis=0, tiled=True)]
    unnamed x54 -> x45, local copies, waits for them, and re-layouts: 7.75 us -> 6.39 us
  transfers between devices with their start and end apart: 8 -> 10, of which waited for: 2 -> 3; matrix products, arithmetic and copies ran while one was open for 12% -> 23% of each run, Pallas kernels for 17% -> 11%
where the time goes in v4:
time: 335 us; the launch traced here: 333 us
  waiting for transfers between devices  88.5 us (26%)
  blocking collectives  71.5 us (21%)
  starting transfers between devices  48.3 us (14%)
  local copies, waits for them, and re-layouts  44.6 us (13%)
  Pallas kernels  36.7 us (11%)
  matrix products  20.3 us (6%)
  between operations  15.8 us (5%)
  other arithmetic  7.71 us (2%)
    all_gather x1, waiting for transfers between devices, shards(): lax.all_gather(arrived.reshape(members, 1, capacity, D), 'dp', axis=1, ti...  41.5 us
    all_gather x1, waiting for transfers between devices, gather_weights(): everyone = lax.all_gather(flat[None], 'expert', axis=0, tiled=True)  37.4 us
    pallas_call x1, Pallas kernels, expert_gather(): pl.pallas_call(partial(gather_kernel, nx, nz), out_shape=jax.ShapeDtypeSt...  36.7 us
    unnamed x1, blocking collectives  23.2 us
    all_to_all x1, starting transfers between devices, shards(): lax.all_to_all(gate_score.reshape(members, groups * capacity), 'expert',...  15.3 us
    all_gather x1, blocking collectives, shards(): group_tokens = lax.all_gather(normed, 'dp', axis=0, tiled=True)  14.4 us
    all_gather x1, blocking collectives, shards(): shared_piece = lax.all_gather(shared_act, 'dp', axis=1, tiled=True)  13.1 us
    all_gather x1, blocking collectives, shards(): group_routes = lax.all_gather(routes, 'dp', axis=0, tiled=True)  13.1 us
  transfers between devices with their start and end apart: 10, of which 3 were waited for; matrix products, arithmetic and copies ran while one was open for 23% of the time, Pallas kernels for 11%

profile of v4, /device:TPU:1, one launch (start us, length us, event | category | flops | bytes accessed | tf_op | source)
XLA Modules:
  0.0 333.4 jit_solution(6287355768068209861)
XLA Ops:
  7.3 0.9 reshape.340
  8.2 0.8 reshape.341
  9.0 0.7 reshape.342
  11.8 1.7 fusion.92
  13.4 0.9 convert_convert_fusion
  14.3 1.6 fusion.93
  18.4 0.9 copy.94
  19.3 10.2 %all-to-all-start = ((bf16[17,16,512]{2,0,1:T(8,128)(2,1)}), bf16[17,16,512]{2,0,1:T(8,128)(2,1)S(1)}, u32[]{:S(2)}, u32[]{:S(2)}) async-start(bf16[17,16,512]{2,0,1:T(8,128)(2,1)} %copy.94), calls=%async_computation | async-start | bytes 786432 | tf_op jit(solution)/shard_map/all_to_all | solution.py:271
  30.2 36.7 %shard_map.203 = bf16[16,4,80,128]{3,2,1,0:T(8,128)(2,1)} custom-call(bf16[80,128]{1,0:T(8,128)(2,1)} %maximum_bitcast_fusion.shard_ref), custom_call_target="tpu_custom_call" | custom-call | tf_op jit(solution)/shard_map/pallas_call | solution.py:137
  66.9 1.4 copy.91
  68.7 1.1 slice.69
  69.7 1.8 reshape.338
  71.6 1.7 copy.97
  73.3 1.5 reshape.339
  76.6 23.2 %fusion = bf16[24,2048]{1,0:T(8,128)(2,1)S(1)} fusion(bf16[136,2048]{1,0:T(8,128)(2,1)S(1)} %fusion.1), kind=kCustom, calls=%all-reduce-scatter | all-reduce-scatter fusion | flops 393217 | bytes 657408
  99.8 2.7 collective-permute-start
  102.4 3.3 collective-permute-start.1
  105.8 3.5 %collective-permute-start.2 = (bf16[1,2048]{1,0:T(2,128)(2,1)S(1)}, bf16[1,2048]{1,0:T(2,128)(2,1)S(1)}, u32[]{:S(2)}, u32[]{:S(2)}) collective-permute-start(bf16[1,2048]{1,0:T(2,128)(2,1)S(1)} %slice.81), channel_id=1, source_target_pairs={{0,192},{64,256},{128,320},{192,384},{256,448},{1,193},{65,257},{1... | collective-permute-start | bytes 12296
  109.3 1.3 dynamic-slice.4
  112.5 1.3 copy.100
  113.9 7.9 %all-to-all-start.1 = ((bf16[64,2,2048]{2,1,0:T(2,128)(2,1)}), bf16[64,2,2048]{2,1,0:T(2,128)(2,1)}, u32[]{:S(2)}, u32[]{:S(2)}) async-start(bf16[64,2,2048]{2,1,0:T(2,128)(2,1)} %copy.100), calls=%async_computation.1 | async-start | bytes 1048576 | tf_op jit(solution)/shard_map/all_to_all | solution.py:299
  122.0 37.4 %all-gather.8.cloned.1.call-done = bf16[64,136,128]{2,1,0:T(8,128)(2,1)} async-done(((bf16[1,136,128]{2,1,0:T(8,128)(2,1)}), bf16[64,136,128]{2,1,0:T(8,128)(2,1)}) %all-gather.8.cloned.1.call-update) | async-done | bytes 2228240 | tf_op jit(solution)/shard_map/all_gather | solution.py:165
  159.4 2.0 copy.135
  161.4 1.0 fusion.91
  162.4 2.0 reshape_reshape.10
  164.4 3.0 reshape_reshape.11
  167.4 1.8 reshape_reshape.12
  169.2 2.0 copy.107
  171.3 41.5 %all-gather.12.cloned.1.call-done = bf16[64,16,2048]{2,0,1:T(8,128)(2,1)} async-done(((bf16[64,2,2048]{2,0,1:T(8,128)(2,1)}), bf16[64,16,2048]{2,0,1:T(8,128)(2,1)}) %all-gather.12.cloned.1.call-update) | async-done | bytes 4194320 | tf_op jit(solution)/shard_map/all_gather | solution.py:302
  212.7 4.5 %copy.108 = bf16[64,16,2048]{2,1,0:T(8,128)(2,1)S(1)} copy(bf16[64,16,2048]{2,0,1:T(8,128)(2,1)} %all-gather.12.cloned.1.call-done) | data formatting | bytes 8388608 | tf_op jit(solution)/shard_map/all_gather | solution.py:302
  217.3 1.6 fusion.27
  219.2 2.4 fusion.2
  221.6 13.1 %all-gather.3 = s32[8,17,6]{1,2,0:T(8,128)S(1)} all-gather(s32[1,17,6]{1,2,0:T(8,128)S(1)} %bitcast.160), channel_id=1, replica_groups=mesh['dp'=8,'expert'=64] {'dp'}, dimensions={0}, use_global_device_ids=true | all-gather | bytes 3672 | tf_op jit(solution)/shard_map/all_gather | solution.py:291
  234.8 2.0 select_reduce_fusion
  237.3 3.6 %fusion.95 = f32[1,1024]{1,0:T(1,128)S(1)} fusion(bf16[1024,2048]{1,0:T(8,128)(2,1)} %bitcast.143, bf16[2048,1]{0,1:T(2,128)(2,1)S(1)} %copy-done.8), kind=kOutput, calls=%fused_computation.151 | convolution fusion | flops 4194304 | bytes 4202496 | tf_op jit(solution)/shard_map/dot_general | solution.py:307
  241.6 15.3 %all-to-all-start.2 = ((f32[64,1,16]{2,1,0:T(1,128)}), f32[64,1,16]{2,1,0:T(1,128)S(1)}, u32[]{:S(2)}, u32[]{:S(2)}) async-start(f32[64,1,16]{2,1,0:T(1,128)} %bitcast.29), calls=%async_computation.2 | async-start | bytes 65536 | tf_op jit(solution)/shard_map/all_to_all | solution.py:332
  257.0 3.6 %convolution_convert_fusion = bf16[1024,256]{1,0:T(8,128)(2,1)} fusion(bf16[1024,1408]{0,1:T(8,128)(2,1)} %all-gather.10.cloned.1.call-done, bf16[1,1408,256]{2,1,0:T(8,128)(2,1)S(1)} %copy-done), kind=kOutput, calls=%fused_computation.6 | convolution fusion | flops 738459648 | bytes 4128768 | tf_op jit(solution)/shard_map/dot_general | solution.py:321
  260.7 9.5 %all-to-all-done.2 = f32[64,1,16]{2,1,0:T(1,128)S(1)} async-done(((f32[64,1,16]{2,1,0:T(1,128)}), f32[64,1,16]{2,1,0:T(1,128)S(1)}, u32[]{:S(2)}, u32[]{:S(2)}) %all-to-all-start.2) | async-done | bytes 4128 | tf_op jit(solution)/shard_map/all_to_all | solution.py:332
  270.2 5.0 %all-to-all-start.3 = ((bf16[64,16,256]{2,1,0:T(8,128)(2,1)}), bf16[64,16,256]{2,1,0:T(8,128)(2,1)S(1)}, u32[]{:S(2)}, u32[]{:S(2)}) async-start(bf16[64,16,256]{2,1,0:T(8,128)(2,1)} %bitcast.33), calls=%async_computation.3 | async-start | bytes 1048576 | tf_op jit(solution)/shard_map/all_to_all | solution.py:325
  275.6 14.4 %all-gather.1 = bf16[8,17,2048]{2,1,0:T(8,128)(2,1)S(1)} all-gather(bf16[1,17,2048]{2,1,0:T(8,128)(2,1)S(1)} %fusion.64), channel_id=1, replica_groups=mesh['dp'=8,'expert'=64] {'dp'}, dimensions={0}, use_global_device_ids=true | all-gather | bytes 626688 | tf_op jit(solution)/shard_map/all_gather | solution.py:290
  290.1 1.0 reshape.375
  291.1 1.4 fusion.94
  292.5 1.7 fusion.11
  294.2 13.1 %all-gather.2 = bf16[8,176,136]{1,2,0:T(8,128)(2,1)S(1)} all-gather(bf16[1,176,136]{1,2,0:T(8,128)(2,1)S(1)} %fusion.11), channel_id=1, replica_groups=mesh['dp'=8,'expert'=64] {'dp'}, dimensions={0}, use_global_device_ids=true | all-gather | bytes 430848 | tf_op jit(solution)/shard_map/all_gather | solution.py:320
  308.5 0.7 reduce.19
  309.3 3.5 %gather_fusion = f32[816]{0:T(1024)S(1)} fusion(f32[1024]{0:T(1024)S(1)} %reshape.346, s32[1024]{0:T(1024)S(1)} %pad_clamp_fusion), kind=kCustom, calls=%fused_computation | custom fusion | bytes 9792 | tf_op jit(solution)/shard_map/jit(_take)/gather | solution.py:344
  313.3 3.4 %gather_fusion.1 = bf16[816,256]{1,0:T(8,128)(2,1)S(1)} fusion(bf16[1024,256]{1,0:T(8,128)(2,1)S(1)} %bitcast.140, s32[1024]{0:T(1024)S(1)} %pad_clamp_fusion), kind=kCustom, calls=%fused_computation.1 | custom fusion | bytes 838848 | tf_op jit(solution)/shard_map/jit(_take)/gather | solution.py:343
  317.7 7.7 %all_to_all.46 = bf16[8,17,256]{2,1,0:T(8,128)(2,1)S(1)} all-to-all(bf16[8,17,256]{2,1,0:T(8,128)(2,1)S(1)} %convert_element_type.169), channel_id=1, replica_groups=mesh['dp'=8,'expert'=64] {'dp'}, dimensions={0} | all-to-all | bytes 139264 | tf_op jit(solution)/shard_map/all_to_all | solution.py:349
  (120 shorter events, 14.2 us)
Async XLA Ops:
  7.2 249.9 %copy-start = (bf16[1,1408,256]{2,1,0:T(8,128)(2,1)S(1)}, bf16[1,1408,256]{2,1,0:T(8,128)(2,1)}, u32[]{:S(2)}) copy-start(bf16[1,1408,256]{2,1,0:T(8,128)(2,1)} %param.36) | copy-start | bytes 2162692
  7.2 10.4 %copy-start.4 = (bf16[1,1024,576]{1,2,0:T(8,128)(2,1)S(1)}, bf16[1,1024,576]{1,2,0:T(8,128)(2,1)}, u32[]{:S(2)}) copy-start(bf16[1,1024,576]{1,2,0:T(8,128)(2,1)} %param.27) | copy-start | bytes 3538948
  7.2 10.4 %copy-start.10 = (f32[16]{0:T(128)S(1)}, f32[16]{0:T(128)}, u32[]{:S(2)}) copy-start(f32[16]{0:T(128)} %param.28) | copy-start | bytes 196
  7.2 10.8 %copy-start.15 = (bf16[16,576]{1,0:T(8,128)(2,1)S(1)}, bf16[16,576]{1,0:T(8,128)(2,1)}, u32[]{:S(2)}) copy-start(bf16[16,576]{1,0:T(8,128)(2,1)} %param.21) | copy-start | bytes 55300
  7.2 152.1 %all-gather.8.cloned.1.call-start = ((), (), s32[]{:S(2)}) async-start(), calls=%async_computation.5 | async-start | bytes 2263040 | tf_op jit(solution)/shard_map/all_gather | solution.py:165
  18.0 11.6 %copy-start.6 = (bf16[2,2,2048]{2,1,0:T(2,128)(2,1)S(1)}, bf16[2,2,2048]{2,1,0:T(2,128)(2,1)}, u32[]{:S(2)}) copy-start(bf16[2,2,2048]{2,1,0:T(2,128)(2,1)} %param.30) | copy-start | bytes 49156
  18.0 11.6 %copy-start.11 = (bf16[2,8,128]{2,1,0:T(8,128)(2,1)S(1)}, bf16[2,8,128]{2,1,0:T(8,128)(2,1)}, u32[]{:S(2)}) copy-start(bf16[2,8,128]{2,1,0:T(8,128)(2,1)} %param.29) | copy-start | bytes 12292
  19.3 56.5 %all-to-all-start = ((bf16[17,16,512]{2,0,1:T(8,128)(2,1)}), bf16[17,16,512]{2,0,1:T(8,128)(2,1)S(1)}, u32[]{:S(2)}, u32[]{:S(2)}) async-start(bf16[17,16,512]{2,0,1:T(8,128)(2,1)} %copy.94), calls=%async_computation | async-start | bytes 786432 | tf_op jit(solution)/shard_map/all_to_all | solution.py:271
  71.6 3.3 copy-start.7
  74.8 34.6 %copy-start.12 = (bf16[2048]{0:T(1024)(128)(2,1)S(1)}, bf16[2048]{0:T(1024)(128)(2,1)}, u32[]{:S(2)}) copy-start(bf16[2048]{0:T(1024)(128)(2,1)} %param.31) | copy-start | bytes 12292
  75.1 36.8 %copy-start.5 = (bf16[16,2048]{1,0:T(8,128)(2,1)S(1)}, bf16[16,2048]{1,0:T(8,128)(2,1)}, u32[]{:S(2)}) copy-start(bf16[16,2048]{1,0:T(8,128)(2,1)} %param.22) | copy-start | bytes 196612
  75.1 36.8 %copy-start.9 = (bf16[1,2048]{1,0:T(2,128)(2,1)S(1)}, bf16[1,2048]{1,0:T(2,128)(2,1)}, u32[]{:S(2)}) copy-start(bf16[1,2048]{1,0:T(2,128)(2,1)} %param.25) | copy-start | bytes 12292
  99.8 11.5 %collective-permute-start = (bf16[24,2048]{1,0:T(8,128)(2,1)S(1)}, bf16[24,2048]{1,0:T(8,128)(2,1)S(1)}, u32[]{:S(2)}, u32[]{:S(2)}) collective-permute-start(bf16[24,2048]{1,0:T(8,128)(2,1)S(1)} %fusion), channel_id=1, source_target_pairs={{0,64},{64,128},{128,192},{192,256},{256,320},{320,384},{384,448},... | collective-permute-start | bytes 294920
  102.4 8.9 %collective-permute-start.1 = (bf16[24,2048]{1,0:T(8,128)(2,1)S(1)}, bf16[24,2048]{1,0:T(8,128)(2,1)S(1)}, u32[]{:S(2)}, u32[]{:S(2)}) collective-permute-start(bf16[24,2048]{1,0:T(8,128)(2,1)S(1)} %fusion), channel_id=1, source_target_pairs={{0,128},{64,192},{128,256},{192,320},{256,384},{320,448},{1,129},{... | collective-permute-start | bytes 294920
  105.8 5.5 %collective-permute-start.2 = (bf16[1,2048]{1,0:T(2,128)(2,1)S(1)}, bf16[1,2048]{1,0:T(2,128)(2,1)S(1)}, u32[]{:S(2)}, u32[]{:S(2)}) collective-permute-start(bf16[1,2048]{1,0:T(2,128)(2,1)S(1)} %slice.81), channel_id=1, source_target_pairs={{0,192},{64,256},{128,320},{192,384},{256,448},{1,193},{65,257},{1... | collective-permute-start | bytes 12296
  113.9 55.3 %all-to-all-start.1 = ((bf16[64,2,2048]{2,1,0:T(2,128)(2,1)}), bf16[64,2,2048]{2,1,0:T(2,128)(2,1)}, u32[]{:S(2)}, u32[]{:S(2)}) async-start(bf16[64,2,2048]{2,1,0:T(2,128)(2,1)} %copy.100), calls=%async_computation.1 | async-start | bytes 1048576 | tf_op jit(solution)/shard_map/all_to_all | solution.py:299
  121.8 91.0 %all-gather.12.cloned.1.call-start = ((), (), s32[]{:S(2)}) async-start(), calls=%async_computation.7 | async-start | bytes 4718592 | tf_op jit(solution)/shard_map/all_gather | solution.py:302
  164.4 3.0 copy-start.3
  171.2 46.0 %copy-start.13 = (bf16[1,2048,176]{1,2,0:T(8,128)(2,1)S(1)}, bf16[1,2048,176]{1,2,0:T(8,128)(2,1)}, u32[]{:S(2)}) copy-start(bf16[1,2048,176]{1,2,0:T(8,128)(2,1)} %param.34) | copy-start | bytes 2162692
  171.2 85.8 %all-gather.10.cloned.1.call-start = ((), (), s32[]{:S(2)}) async-start(), calls=%async_computation.6 | async-start | bytes 3244032 | tf_op jit(solution)/shard_map/all_gather | solution.py:319
  217.2 1.9 copy-start.1
  217.3 1.9 copy-start.14
  219.2 18.2 %copy-start.8 = (bf16[2048,1]{0,1:T(2,128)(2,1)S(1)}, bf16[2048,1]{0,1:T(2,128)(2,1)}, u32[]{:S(2)}) copy-start(bf16[2048,1]{0,1:T(2,128)(2,1)} %param.32) | copy-start | bytes 12292
  241.6 28.6 %all-to-all-start.2 = ((f32[64,1,16]{2,1,0:T(1,128)}), f32[64,1,16]{2,1,0:T(1,128)S(1)}, u32[]{:S(2)}, u32[]{:S(2)}) async-start(f32[64,1,16]{2,1,0:T(1,128)} %bitcast.29), calls=%async_computation.2 | async-start | bytes 65536 | tf_op jit(solution)/shard_map/all_to_all | solution.py:332
  270.2 43.1 %all-to-all-start.3 = ((bf16[64,16,256]{2,1,0:T(8,128)(2,1)}), bf16[64,16,256]{2,1,0:T(8,128)(2,1)S(1)}, u32[]{:S(2)}, u32[]{:S(2)}) async-start(bf16[64,16,256]{2,1,0:T(8,128)(2,1)} %bitcast.33), calls=%async_computation.3 | async-start | bytes 1048576 | tf_op jit(solution)/shard_map/all_to_all | solution.py:325
  313.3 4.1 %copy-start.2 = (bf16[1408,256]{1,0:T(8,128)(2,1)S(1)}, bf16[1408,256]{1,0:T(8,128)(2,1)}, u32[]{:S(2)}) copy-start(bf16[1408,256]{1,0:T(8,128)(2,1)} %reshape_reshape.12) | copy-start | bytes 2162692
Sparse Core Ops, SparseCore 0:
  11.6 147.7 all-gather.7
  171.4 41.3 all-gather.11
  221.7 34.4 all-gather.9

commit v5 on v4

--- a/solution.py
+++ b/solution.py
@@ -218,6 +218,7 @@
             shared_gate=(shared_gate, 0),
             shared_up=(shared_up, 0),
             shared_down=(shared_down, 0),
+            router=(router, 1),
         )
     )
     pre_scores = (
@@ -287,8 +288,15 @@
         hidden_up * lax.rsqrt(mean_square + NORM_EPS) * norm_gain.astype(jnp.float32)[None, :]
     ).astype(jnp.bfloat16)
     capacity = max(2, (rows_dev * TOPK + members - 1) // members)
-    group_tokens = lax.all_gather(normed, "dp", axis=0, tiled=True)
-    group_routes = lax.all_gather(routes, "dp", axis=0, tiled=True)
+    route_row = routes.astype(jnp.bfloat16).reshape(1, rows_dev * TOPK)
+    route_row = jnp.pad(route_row, ((0, 0), (0, D - rows_dev * TOPK)))
+    group_both = lax.all_gather(
+        jnp.concatenate([normed, route_row], axis=0)[None], "dp", axis=0, tiled=True
+    )
+    group_tokens = group_both[:, :rows_dev].reshape(groups * rows_dev, D)
+    group_routes = (
+        group_both[:, rows_dev, : rows_dev * TOPK].astype(jnp.int32).reshape(-1, TOPK)
+    )
     routes_by_group = group_routes.reshape(groups, rows_dev, TOPK)
     slots_by_group = jax.vmap(partial(assign_slots, experts=members))(routes_by_group)
     own_slots = assign_slots(routes, members)
@@ -297,19 +305,21 @@
     )
     outgoing = jnp.einsum("rxc,rd->xcd", own_matrix, normed, preferred_element_type=jnp.bfloat16)
     arrived = lax.all_to_all(outgoing, "expert", split_axis=0, concat_axis=0, tiled=True)
-    shared_ready = (weights["shared_gate"], weights["shared_up"], weights["shared_down"])
+    shared_ready = (
+        weights["shared_gate"],
+        weights["shared_up"],
+        weights["shared_down"],
+        weights["router"],
+    )
     arrived, shared_ready = lax.optimization_barrier((arrived, shared_ready))
     expert_rows = lax.all_gather(
         arrived.reshape(members, 1, capacity, D), "dp", axis=1, tiled=True
     )
     expert_rows = expert_rows.reshape(-1, D)
-    gate_score = jax.nn.sigmoid(
-        jnp.dot(expert_rows, router[:, 0], preferred_element_type=jnp.float32)
-    )
     gate_proj = jnp.dot(expert_rows, gate_weight[0], preferred_element_type=jnp.float32)
     up_proj = jnp.dot(expert_rows, up_weight[0], preferred_element_type=jnp.float32)
     expert_act = (jax.nn.silu(gate_proj) * up_proj).astype(jnp.bfloat16)
-    shared_gate_full, shared_up_full, shared_down_full = shared_ready
+    shared_gate_full, shared_up_full, shared_down_full, router_full = shared_ready
     shared_act = (
         jax.nn.silu(jnp.dot(group_tokens, shared_gate_full, preferred_element_type=jnp.float32))
         * jnp.dot(group_tokens, shared_up_full, preferred_element_type=jnp.float32)
@@ -329,19 +339,15 @@
         concat_axis=0,
         tiled=True,
     )
-    returned_scores = lax.all_to_all(
-        gate_score.reshape(members, groups * capacity),
-        "expert",
-        split_axis=0,
-        concat_axis=0,
-        tiled=True,
-    )
     group_offset = (jnp.arange(groups, dtype=jnp.int32) * capacity)[:, None, None]
     lookup = (routes_by_group * (groups * capacity) + group_offset + slots_by_group).reshape(
         groups * rows_dev, TOPK
     )
     picked = jnp.take(returned.reshape(-1, col_width), lookup, axis=0)
-    picked_scores = jnp.take(returned_scores.reshape(-1), lookup, axis=0)
+    group_logits = jnp.dot(group_tokens, router_full, preferred_element_type=jnp.float32)
+    picked_scores = jax.nn.sigmoid(
+        jnp.take_along_axis(group_logits, group_routes.reshape(-1, TOPK), axis=1)
+    )
     route_weight = ROUTE_SCALE * picked_scores / jnp.sum(picked_scores, axis=1, keepdims=True)
     moe_cols = shared_out.astype(jnp.float32) + jnp.sum(
         route_weight[:, :, None] * picked.astype(jnp.float32), axis=1

time: 335 us -> 337 us (level)
  blocking collectives: 71.5 us -> 58.5 us
  local copies, waits for them, and re-layouts: 44.6 us -> 56.3 us
  waiting for transfers between devices: 88.5 us -> 96.5 us
  starting transfers between devices: 48.3 us -> 44.2 us
    all_gather x1, waiting for transfers between devices: 0.02 us -> 18.1 us  [shards(): routed_piece = lax.all_gather(expert_act, 'dp', axis=1, tiled=True)]
    all_to_all x1 -> x0, starting transfers between devices: 15.3 us -> none  [shards(): lax.all_to_all(gate_score.reshape(members, groups * capacity), 'expert',...]
    all_gather x2 -> x1, blocking collectives: 27.5 us -> 13.8 us  [shards(): lax.all_gather(jnp.concatenate([normed, route_row], axis=0)[None], 'dp',...]
    all_to_all x1, starting transfers between devices: 5.04 us -> 15.5 us  [shards(): lax.all_to_all(expert_out.reshape(members, groups * capacity, col_width),...]
    all_to_all x1 -> x0, waiting for transfers between devices: 9.54 us -> none  [shards(): lax.all_to_all(gate_score.reshape(members, groups * capacity), 'expert',...]
    gather x3 -> x4, local copies, waits for them, and re-layouts: 3.67 us -> 11 us  [shards(): jnp.take_along_axis(group_logits, group_routes.reshape(-1, TOPK), axis=1)]
    another operation x3, local copies, waits for them, and re-layouts: 6.83 us -> 10.2 us  [gather_weights(): out[n] = piece.reshape(shape)]
  transfers between devices with their start and end apart: 10 -> 9, of which waited for: 3 -> 3; matrix products, arithmetic and copies ran while one was open for 23% -> 24% of each run, Pallas kernels for 11% -> 11%
where the time goes in v5:
time: 337 us; the launch traced here: 335 us
  waiting for transfers between devices  96.5 us (29%)
  blocking collectives  58.5 us (17%)
  local copies, waits for them, and re-layouts  56.3 us (17%)
  starting transfers between devices  44.2 us (13%)
  Pallas kernels  38.5 us (11%)
  matrix products  17 us (5%)
  between operations  15.8 us (5%)
  other arithmetic  8.58 us (3%)
    all_gather x1, waiting for transfers between devices, shards(): lax.all_gather(arrived.reshape(members, 1, capacity, D), 'dp', axis=1, ti...  41.9 us
    pallas_call x1, Pallas kernels, expert_gather(): pl.pallas_call(partial(gather_kernel, nx, nz), out_shape=jax.ShapeDtypeSt...  38.5 us
    all_gather x1, waiting for transfers between devices, gather_weights(): everyone = lax.all_gather(flat[None], 'expert', axis=0, tiled=True)  36.5 us
    unnamed x1, blocking collectives  21.4 us
    all_gather x1, waiting for transfers between devices, shards(): routed_piece = lax.all_gather(expert_act, 'dp', axis=1, tiled=True)  18.1 us
    all_to_all x1, starting transfers between devices, shards(): lax.all_to_all(expert_out.reshape(members, groups * capacity, col_width),...  15.5 us
    all_gather x1, blocking collectives, shards(): lax.all_gather(jnp.concatenate([normed, route_row], axis=0)[None], 'dp',...  13.8 us
    all_gather x1, blocking collectives, shards(): shared_piece = lax.all_gather(shared_act, 'dp', axis=1, tiled=True)  13.5 us
  transfers between devices with their start and end apart: 9, of which 3 were waited for; matrix products, arithmetic and copies ran while one was open for 24% of the time, Pallas kernels for 11%

profile of v5, /device:TPU:1, one launch (start us, length us, event | category | flops | bytes accessed | tf_op | source)
XLA Modules:
  0.0 335.4 jit_solution(2461574808513663527)
XLA Ops:
  7.2 0.9 reshape.479
  8.1 0.8 reshape.480
  8.9 0.7 reshape.481
  9.7 0.7 reduce.10
  11.7 1.6 fusion.101
  14.0 1.7 fusion.100
  15.6 0.9 convert_convert_fusion
  18.2 1.6 fusion.21
  20.3 0.9 copy.78
  21.2 10.2 %all-to-all-start = ((bf16[17,16,512]{2,0,1:T(8,128)(2,1)}), bf16[17,16,512]{2,0,1:T(8,128)(2,1)S(1)}, u32[]{:S(2)}, u32[]{:S(2)}) async-start(bf16[17,16,512]{2,0,1:T(8,128)(2,1)} %copy.78), calls=%async_computation | async-start | bytes 786432 | tf_op jit(solution)/shard_map/all_to_all | solution.py:272
  32.1 38.5 %shard_map.203 = bf16[16,4,80,128]{3,2,1,0:T(8,128)(2,1)} custom-call(bf16[80,128]{1,0:T(8,128)(2,1)} %maximum_bitcast_fusion.shard_ref), custom_call_target="tpu_custom_call" | custom-call | tf_op jit(solution)/shard_map/pallas_call | solution.py:137
  70.6 1.4 copy.75
  72.3 1.1 slice.81
  73.4 1.8 reshape.475
  75.2 1.7 copy.81
  76.9 1.5 reshape.476
  80.2 21.4 %fusion = bf16[24,2048]{1,0:T(8,128)(2,1)S(1)} fusion(bf16[136,2048]{1,0:T(8,128)(2,1)S(1)} %fusion.1), kind=kCustom, calls=%all-reduce-scatter | all-reduce-scatter fusion | flops 393217 | bytes 657408
  101.7 2.9 collective-permute-start
  104.6 2.7 collective-permute-start.1
  107.3 4.4 %collective-permute-start.2 = (bf16[1,2048]{1,0:T(2,128)(2,1)S(1)}, bf16[1,2048]{1,0:T(2,128)(2,1)S(1)}, u32[]{:S(2)}, u32[]{:S(2)}) collective-permute-start(bf16[1,2048]{1,0:T(2,128)(2,1)S(1)} %slice.96), channel_id=1, source_target_pairs={{0,192},{64,256},{128,320},{192,384},{256,448},{1,193},{65,257},{1... | collective-permute-start | bytes 12296
  111.7 1.3 dynamic-slice.4
  115.0 1.3 copy.85
  116.4 8.2 %all-to-all-start.1 = ((bf16[64,2,2048]{2,1,0:T(2,128)(2,1)}), bf16[64,2,2048]{2,1,0:T(2,128)(2,1)}, u32[]{:S(2)}, u32[]{:S(2)}) async-start(bf16[64,2,2048]{2,1,0:T(2,128)(2,1)} %copy.85), calls=%async_computation.1 | async-start | bytes 1048576 | tf_op jit(solution)/shard_map/all_to_all | solution.py:307
  124.8 36.5 %all-gather.8.cloned.1.call-done = bf16[64,152,128]{2,1,0:T(8,128)(2,1)} async-done(((bf16[1,152,128]{2,1,0:T(8,128)(2,1)}), bf16[64,152,128]{2,1,0:T(8,128)(2,1)}) %all-gather.8.cloned.1.call-update) | async-done | bytes 2490384 | tf_op jit(solution)/shard_map/all_gather | solution.py:165
  161.3 2.1 copy.117
  163.4 1.4 fusion.99
  164.8 3.8 %reshape_reshape.10 = bf16[2048,176]{1,0:T(8,128)(2,1)} reshape(bf16[64,5632]{1,0:T(8,128)(2,1)} %get-tuple-element.24) | data formatting | bytes 1441792 | tf_op jit(solution)/shard_map/reshape;reshape | solution.py:176
  168.6 3.8 %reshape_reshape.11 = bf16[2048,176]{1,0:T(8,128)(2,1)} reshape(bf16[64,5632]{1,0:T(8,128)(2,1)} %get-tuple-element.23) | data formatting | bytes 1441792 | tf_op jit(solution)/shard_map/reshape;reshape | solution.py:176
  172.4 2.7 reshape_reshape.12
  175.0 0.7 slice_bitcast_fusion
  175.7 2.0 copy.97
  177.8 41.9 %all-gather.12.cloned.1.call-done = bf16[64,16,2048]{2,0,1:T(8,128)(2,1)} async-done(((bf16[64,2,2048]{2,0,1:T(8,128)(2,1)}), bf16[64,16,2048]{2,0,1:T(8,128)(2,1)}) %all-gather.12.cloned.1.call-update) | async-done | bytes 4194320 | tf_op jit(solution)/shard_map/all_gather | solution.py:315
  219.7 4.5 %copy.98 = bf16[64,16,2048]{2,1,0:T(8,128)(2,1)S(1)} copy(bf16[64,16,2048]{2,0,1:T(8,128)(2,1)} %all-gather.12.cloned.1.call-done) | data formatting | bytes 8388608 | tf_op jit(solution)/shard_map/all_gather | solution.py:315
  224.2 1.5 fusion.27
  225.8 2.3 fusion.2
  228.5 13.8 %all-gather.2 = bf16[8,18,2048]{2,1,0:T(8,128)(2,1)S(1)} all-gather(bf16[1,18,2048]{2,1,0:T(8,128)(2,1)S(1)} %fusion.46), channel_id=2, replica_groups=mesh['dp'=8,'expert'=64] {'dp'}, dimensions={0}, use_global_device_ids=true | all-gather | bytes 663552 | tf_op jit(solution)/shard_map/all_gather | solution.py:293
  242.5 2.0 select_reduce_fusion
  244.5 18.1 %all-gather.10.cloned.1.call-done = bf16[1024,1408]{0,1:T(8,128)(2,1)} async-done(((bf16[1024,176]{0,1:T(8,128)(2,1)}), bf16[1024,1408]{0,1:T(8,128)(2,1)}) %all-gather.10.cloned.1.call-update) | async-done | bytes 2883600 | tf_op jit(solution)/shard_map/all_gather | solution.py:329
  262.7 3.7 %convolution_convert_fusion = bf16[1024,256]{1,0:T(8,128)(2,1)} fusion(bf16[1024,1408]{0,1:T(8,128)(2,1)} %all-gather.10.cloned.1.call-done, bf16[1,1408,256]{2,1,0:T(8,128)(2,1)S(1)} %copy-done), kind=kOutput, calls=%fused_computation.6 | convolution fusion | flops 738459648 | bytes 4128768 | tf_op jit(solution)/shard_map/dot_general | solution.py:331
  266.3 15.5 %all-to-all-start.2 = ((bf16[64,16,256]{2,1,0:T(8,128)(2,1)}), bf16[64,16,256]{2,1,0:T(8,128)(2,1)S(1)}, u32[]{:S(2)}, u32[]{:S(2)}) async-start(bf16[64,16,256]{2,1,0:T(8,128)(2,1)} %bitcast.164), calls=%async_computation.2 | async-start | bytes 1048576 | tf_op jit(solution)/shard_map/all_to_all | solution.py:335
  282.1 1.3 reshape.478
  283.6 0.7 fusion.97
  285.3 1.6 fusion.11
  286.9 13.5 %all-gather.3 = bf16[8,176,136]{1,2,0:T(8,128)(2,1)S(1)} all-gather(bf16[1,176,136]{1,2,0:T(8,128)(2,1)S(1)} %fusion.11), channel_id=1, replica_groups=mesh['dp'=8,'expert'=64] {'dp'}, dimensions={0}, use_global_device_ids=true | all-gather | bytes 430848 | tf_op jit(solution)/shard_map/all_gather | solution.py:330
  300.5 1.3 reshape.517
  302.1 10.7 %gather_fusion.1 = f32[816]{0:T(1024)S(1)} fusion(f32[136,64]{0,1:T(8,128)S(1)} %fusion.103, s32[816]{0:T(1024)S(1)} %reshape.504), kind=kCustom, calls=%fused_computation.1 | custom fusion | bytes 13056 | tf_op jit(solution)/shard_map/jit(take_along_axis)/gather | solution.py:349
  313.2 3.4 %gather_fusion = bf16[816,256]{1,0:T(8,128)(2,1)S(1)} fusion(bf16[1024,256]{1,0:T(8,128)(2,1)S(1)} %bitcast.146, s32[1024]{0:T(1024)S(1)} %pad_clamp_fusion), kind=kCustom, calls=%fused_computation | custom fusion | bytes 838848 | tf_op jit(solution)/shard_map/jit(_take)/gather | solution.py:346
  317.7 9.7 %all_to_all.37 = bf16[8,17,256]{2,1,0:T(8,128)(2,1)S(1)} all-to-all(bf16[8,17,256]{2,1,0:T(8,128)(2,1)S(1)} %convert_element_type.222), channel_id=1, replica_groups=mesh['dp'=8,'expert'=64] {'dp'}, dimensions={0} | all-to-all | bytes 139264 | tf_op jit(solution)/shard_map/all_to_all | solution.py:355
  (122 shorter events, 12.9 us)
Async XLA Ops:
  7.2 255.5 %copy-start = (bf16[1,1408,256]{2,1,0:T(8,128)(2,1)S(1)}, bf16[1,1408,256]{2,1,0:T(8,128)(2,1)}, u32[]{:S(2)}) copy-start(bf16[1,1408,256]{2,1,0:T(8,128)(2,1)} %param.36) | copy-start | bytes 2162692
  7.2 12.7 %copy-start.15 = (bf16[16,576]{1,0:T(8,128)(2,1)S(1)}, bf16[16,576]{1,0:T(8,128)(2,1)}, u32[]{:S(2)}) copy-start(bf16[16,576]{1,0:T(8,128)(2,1)} %param.21) | copy-start | bytes 55300
  7.2 12.7 %copy-start.10 = (f32[16]{0:T(128)S(1)}, f32[16]{0:T(128)}, u32[]{:S(2)}) copy-start(f32[16]{0:T(128)} %param.28) | copy-start | bytes 196
  7.2 154.1 %all-gather.8.cloned.1.call-start = ((), (), s32[]{:S(2)}) async-start(), calls=%async_computation.4 | async-start | bytes 2529280 | tf_op jit(solution)/shard_map/all_gather | solution.py:165
  18.2 13.3 %copy-start.7 = (bf16[2,2,2048]{2,1,0:T(2,128)(2,1)S(1)}, bf16[2,2,2048]{2,1,0:T(2,128)(2,1)}, u32[]{:S(2)}) copy-start(bf16[2,2,2048]{2,1,0:T(2,128)(2,1)} %param.30) | copy-start | bytes 49156
  18.2 13.3 %copy-start.11 = (bf16[2,8,128]{2,1,0:T(8,128)(2,1)S(1)}, bf16[2,8,128]{2,1,0:T(8,128)(2,1)}, u32[]{:S(2)}) copy-start(bf16[2,8,128]{2,1,0:T(8,128)(2,1)} %param.29) | copy-start | bytes 12292
  21.2 58.3 %all-to-all-start = ((bf16[17,16,512]{2,0,1:T(8,128)(2,1)}), bf16[17,16,512]{2,0,1:T(8,128)(2,1)S(1)}, u32[]{:S(2)}, u32[]{:S(2)}) async-start(bf16[17,16,512]{2,0,1:T(8,128)(2,1)} %copy.78), calls=%async_computation | async-start | bytes 786432 | tf_op jit(solution)/shard_map/all_to_all | solution.py:272
  75.2 3.3 copy-start.8
  78.4 33.3 %copy-start.12 = (bf16[2048]{0:T(1024)(128)(2,1)S(1)}, bf16[2048]{0:T(1024)(128)(2,1)}, u32[]{:S(2)}) copy-start(bf16[2048]{0:T(1024)(128)(2,1)} %param.31) | copy-start | bytes 12292
  78.4 35.9 %copy-start.6 = (bf16[16,2048]{1,0:T(8,128)(2,1)S(1)}, bf16[16,2048]{1,0:T(8,128)(2,1)}, u32[]{:S(2)}) copy-start(bf16[16,2048]{1,0:T(8,128)(2,1)} %param.22) | copy-start | bytes 196612
  78.4 35.9 %copy-start.9 = (bf16[1,2048]{1,0:T(2,128)(2,1)S(1)}, bf16[1,2048]{1,0:T(2,128)(2,1)}, u32[]{:S(2)}) copy-start(bf16[1,2048]{1,0:T(2,128)(2,1)} %param.25) | copy-start | bytes 12292
  101.7 12.0 %collective-permute-start = (bf16[24,2048]{1,0:T(8,128)(2,1)S(1)}, bf16[24,2048]{1,0:T(8,128)(2,1)S(1)}, u32[]{:S(2)}, u32[]{:S(2)}) collective-permute-start(bf16[24,2048]{1,0:T(8,128)(2,1)S(1)} %fusion), channel_id=1, source_target_pairs={{0,64},{64,128},{128,192},{192,256},{256,320},{320,384},{384,448},... | collective-permute-start | bytes 294920
  104.6 9.1 %collective-permute-start.1 = (bf16[24,2048]{1,0:T(8,128)(2,1)S(1)}, bf16[24,2048]{1,0:T(8,128)(2,1)S(1)}, u32[]{:S(2)}, u32[]{:S(2)}) collective-permute-start(bf16[24,2048]{1,0:T(8,128)(2,1)S(1)} %fusion), channel_id=1, source_target_pairs={{0,128},{64,192},{128,256},{192,320},{256,384},{320,448},{1,129},{... | collective-permute-start | bytes 294920
  107.3 6.3 %collective-permute-start.2 = (bf16[1,2048]{1,0:T(2,128)(2,1)S(1)}, bf16[1,2048]{1,0:T(2,128)(2,1)S(1)}, u32[]{:S(2)}, u32[]{:S(2)}) collective-permute-start(bf16[1,2048]{1,0:T(2,128)(2,1)S(1)} %slice.96), channel_id=1, source_target_pairs={{0,192},{64,256},{128,320},{192,384},{256,448},{1,193},{65,257},{1... | collective-permute-start | bytes 12296
  116.4 59.4 %all-to-all-start.1 = ((bf16[64,2,2048]{2,1,0:T(2,128)(2,1)}), bf16[64,2,2048]{2,1,0:T(2,128)(2,1)}, u32[]{:S(2)}, u32[]{:S(2)}) async-start(bf16[64,2,2048]{2,1,0:T(2,128)(2,1)} %copy.85), calls=%async_computation.1 | async-start | bytes 1048576 | tf_op jit(solution)/shard_map/all_to_all | solution.py:307
  124.6 95.1 %all-gather.12.cloned.1.call-start = ((), (), s32[]{:S(2)}) async-start(), calls=%async_computation.6 | async-start | bytes 4718592 | tf_op jit(solution)/shard_map/all_gather | solution.py:315
  177.8 46.4 %copy-start.13 = (bf16[1,2048,176]{1,2,0:T(8,128)(2,1)S(1)}, bf16[1,2048,176]{1,2,0:T(8,128)(2,1)}, u32[]{:S(2)}) copy-start(bf16[1,2048,176]{1,2,0:T(8,128)(2,1)} %param.34) | copy-start | bytes 2162692
  177.8 84.9 %all-gather.10.cloned.1.call-start = ((), (), s32[]{:S(2)}) async-start(), calls=%async_computation.5 | async-start | bytes 3244032 | tf_op jit(solution)/shard_map/all_gather | solution.py:329
  224.2 1.6 copy-start.14
  242.3 24.0 %copy-start.2 = (bf16[8,18,2048]{2,1,0:T(8,128)(2,1)}, bf16[8,18,2048]{2,1,0:T(8,128)(2,1)S(1)}, u32[]{:S(2)}) copy-start(bf16[8,18,2048]{2,1,0:T(8,128)(2,1)S(1)} %all-gather.2) | copy-start | bytes 1769476
  266.3 18.6 %copy-start.1 = (bf16[2048,176]{1,0:T(8,128)(2,1)S(1)}, bf16[2048,176]{1,0:T(8,128)(2,1)}, u32[]{:S(2)}) copy-start(bf16[2048,176]{1,0:T(8,128)(2,1)} %reshape_reshape.10) | copy-start | bytes 2162692
  266.3 46.9 %all-to-all-start.2 = ((bf16[64,16,256]{2,1,0:T(8,128)(2,1)}), bf16[64,16,256]{2,1,0:T(8,128)(2,1)S(1)}, u32[]{:S(2)}, u32[]{:S(2)}) async-start(bf16[64,16,256]{2,1,0:T(8,128)(2,1)} %bitcast.164), calls=%async_computation.2 | async-start | bytes 1048576 | tf_op jit(solution)/shard_map/all_to_all | solution.py:335
  285.3 16.5 %copy-start.5 = (bf16[2048,64]{0,1:T(8,128)(2,1)S(1)}, bf16[2048,64]{0,1:T(8,128)(2,1)}, u32[]{:S(2)}) copy-start(bf16[2048,64]{0,1:T(8,128)(2,1)} %slice_bitcast_fusion) | copy-start | bytes 786436
  313.2 4.1 %copy-start.3 = (bf16[1408,256]{1,0:T(8,128)(2,1)S(1)}, bf16[1408,256]{1,0:T(8,128)(2,1)}, u32[]{:S(2)}) copy-start(bf16[1408,256]{1,0:T(8,128)(2,1)} %reshape_reshape.12) | copy-start | bytes 2162692
  313.2 4.1 %copy-start.4 = (bf16[1408,136]{0,1:T(8,128)(2,1)S(1)}, bf16[1408,136]{0,1:T(8,128)(2,1)}, u32[]{:S(2)}) copy-start(bf16[1408,136]{0,1:T(8,128)(2,1)} %reshape.517) | copy-start | bytes 1148932
Sparse Core Ops, SparseCore 0:
  11.6 149.6 all-gather.7
  177.9 41.7 all-gather.11
  228.2 34.3 all-gather.9

commit v6 on v5

--- a/solution.py
+++ b/solution.py
@@ -210,16 +210,10 @@
         True,
         uv=(uv_weight, 1),
         out=(out_weight, 1),
-    )
-    weights.update(
-        gather_weights(
-            members,
-            False,
-            shared_gate=(shared_gate, 0),
-            shared_up=(shared_up, 0),
-            shared_down=(shared_down, 0),
-            router=(router, 1),
-        )
+        shared_gate=(shared_gate, 0),
+        shared_up=(shared_up, 0),
+        shared_down=(shared_down, 0),
+        router=(router, 1),
     )
     pre_scores = (
         jnp.einsum("thc,uc->thu", pre_query, pre_latent, preferred_element_type=jnp.float32)
@@ -311,7 +305,6 @@
         weights["shared_down"],
         weights["router"],
     )
-    arrived, shared_ready = lax.optimization_barrier((arrived, shared_ready))
     expert_rows = lax.all_gather(
         arrived.reshape(members, 1, capacity, D), "dp", axis=1, tiled=True
     )

time: 337 us -> 330 us (0.979)
  waiting for transfers between devices: 96.5 us -> 37.3 us
  blocking collectives: 58.5 us -> 97.3 us
  Pallas kernels: 38.5 us -> 61.4 us
  starting transfers between devices: 44.2 us -> 34.9 us
    all_to_all x0 -> x1, blocking collectives: none -> 39.1 us  [shards(): lax.all_to_all(outgoing, 'expert', split_axis=0, concat_axis=0, tiled=True)]
    all_gather x1 -> x0, waiting for transfers between devices: 36.5 us -> none  [gather_weights(): everyone = lax.all_gather(flat[None], 'expert', axis=0, tiled=True)]
    pallas_call x1, Pallas kernels: 38.5 us -> 61.4 us  [expert_gather(): pl.pallas_call(partial(gather_kernel, nx, nz), out_shape=jax.ShapeDtypeSt...]
    all_gather x1, waiting for transfers between devices: 18.1 us -> 6.52 us  [shards(): routed_piece = lax.all_gather(expert_act, 'dp', axis=1, tiled=True)]
    all_gather x1, waiting for transfers between devices: 41.9 us -> 30.7 us  [shards(): lax.all_gather(arrived.reshape(members, 1, capacity, D), 'dp', axis=1, ti...]
    all_to_all x1 -> x0, starting transfers between devices: 8.22 us -> none  [shards(): lax.all_to_all(outgoing, 'expert', split_axis=0, concat_axis=0, tiled=True)]
    unnamed x44 -> x54, local copies, waits for them, and re-layouts: 5.93 us -> 7.51 us
  transfers between devices with their start and end apart: 9 -> 7, of which waited for: 3 -> 2; matrix products, arithmetic and copies ran while one was open for 24% -> 15% of each run, Pallas kernels for 11% -> 19%
where the time goes in v6:
time: 330 us; the launch traced here: 329 us
  blocking collectives  97.3 us (29%)
  Pallas kernels  61.4 us (19%)
  local copies, waits for them, and re-layouts  55.8 us (17%)
  waiting for transfers between devices  37.3 us (11%)
  starting transfers between devices  34.9 us (11%)
  matrix products  18.4 us (6%)
  between operations  16.2 us (5%)
  other arithmetic  7.59 us (2%)
    pallas_call x1, Pallas kernels, expert_gather(): pl.pallas_call(partial(gather_kernel, nx, nz), out_shape=jax.ShapeDtypeSt...  61.4 us
    all_to_all x1, blocking collectives, shards(): lax.all_to_all(outgoing, 'expert', split_axis=0, concat_axis=0, tiled=True)  39.1 us
    all_gather x1, waiting for transfers between devices, shards(): lax.all_gather(arrived.reshape(members, 1, capacity, D), 'dp', axis=1, ti...  30.7 us
    unnamed x1, blocking collectives  21.8 us
    all_to_all x1, starting transfers between devices, shards(): lax.all_to_all(expert_out.reshape(members, groups * capacity, col_width),...  15.3 us
    all_gather x1, blocking collectives, shards(): lax.all_gather(jnp.concatenate([normed, route_row], axis=0)[None], 'dp',...  14.8 us
    all_gather x1, blocking collectives, shards(): shared_piece = lax.all_gather(shared_act, 'dp', axis=1, tiled=True)  13.5 us
    gather x4, local copies, waits for them, and re-layouts, shards(): jnp.take_along_axis(group_logits, group_routes.reshape(-1, TOPK), axis=1)  11 us
  transfers between devices with their start and end apart: 7, of which 2 were waited for; matrix products, arithmetic and copies ran while one was open for 15% of the time, Pallas kernels for 19%

profile of v6, /device:TPU:1, one launch (start us, length us, event | category | flops | bytes accessed | tf_op | source)
XLA Modules:
  0.0 329.0 jit_solution(17073230092430418575)
XLA Ops:
  8.7 1.7 fusion.93
  10.4 0.9 convert_convert_fusion
  11.3 1.6 fusion.94
  14.3 1.1 fusion.3
  16.1 0.9 copy.78
  17.0 10.2 %all-to-all-start = ((bf16[17,16,512]{2,0,1:T(8,128)(2,1)}), bf16[17,16,512]{2,0,1:T(8,128)(2,1)S(1)}, u32[]{:S(2)}, u32[]{:S(2)}) async-start(bf16[17,16,512]{2,0,1:T(8,128)(2,1)} %copy.78), calls=%async_computation | async-start | bytes 786432 | tf_op jit(solution)/shard_map/all_to_all | solution.py:266
  29.6 61.4 %shard_map.203 = bf16[16,4,232,128]{3,2,1,0:T(8,128)(2,1)} custom-call(bf16[232,128]{1,0:T(8,128)(2,1)} %pad_bitcast_fusion.shard_ref), custom_call_target="tpu_custom_call" | custom-call | tf_op jit(solution)/shard_map/pallas_call | solution.py:137
  91.0 2.3 copy.75
  94.0 1.7 copy-done.1
  95.7 0.8 reshape.476
  96.5 1.7 copy.81
  98.2 1.5 reshape.477
  99.7 0.7 copy.103
  101.7 1.4 fusion.1
  103.1 21.8 %fusion = bf16[24,2048]{1,0:T(8,128)(2,1)S(1)} fusion(bf16[136,2048]{1,0:T(8,128)(2,1)S(1)} %fusion.1), kind=kCustom, calls=%all-reduce-scatter | all-reduce-scatter fusion | flops 393217 | bytes 657408
  125.0 2.1 collective-permute-start
  127.1 2.4 collective-permute-start.1
  129.5 4.7 %collective-permute-start.2 = (bf16[1,2048]{1,0:T(2,128)(2,1)S(1)}, bf16[1,2048]{1,0:T(2,128)(2,1)S(1)}, u32[]{:S(2)}, u32[]{:S(2)}) collective-permute-start(bf16[1,2048]{1,0:T(2,128)(2,1)S(1)} %slice.96), channel_id=1, source_target_pairs={{0,192},{64,256},{128,320},{192,384},{256,448},{1,193},{65,257},{1... | collective-permute-start | bytes 12296
  134.2 1.3 dynamic-slice.4
  138.1 39.1 %all_to_all.37 = bf16[64,2,2048]{2,1,0:T(2,128)(2,1)S(1)} all-to-all(bf16[64,2,2048]{2,1,0:T(2,128)(2,1)S(1)} %copy.96), channel_id=1, replica_groups=mesh['dp'=8,'expert'=64] {'expert'}, dimensions={0} | all-to-all | bytes 1048576 | tf_op jit(solution)/shard_map/all_to_all | solution.py:301
  177.2 1.0 copy.97
  178.4 30.7 %all-gather.9.cloned.1.call-done = bf16[64,16,2048]{2,0,1:T(8,128)(2,1)} async-done(((bf16[64,2,2048]{2,0,1:T(8,128)(2,1)}), bf16[64,16,2048]{2,0,1:T(8,128)(2,1)}) %all-gather.9.cloned.1.call-update) | async-done | bytes 4194320 | tf_op jit(solution)/shard_map/all_gather | solution.py:308
  209.1 4.5 %copy.98 = bf16[64,16,2048]{2,1,0:T(8,128)(2,1)S(1)} copy(bf16[64,16,2048]{2,0,1:T(8,128)(2,1)} %all-gather.9.cloned.1.call-done) | data formatting | bytes 8388608 | tf_op jit(solution)/shard_map/all_gather | solution.py:308
  213.6 1.6 fusion.27
  215.2 2.3 fusion.2
  217.8 2.9 fusion.92
  220.6 3.0 reshape_reshape.10
  223.7 3.1 reshape_reshape.11
  226.9 2.7 reshape_reshape.12
  229.6 14.8 %all-gather.2 = bf16[8,18,2048]{2,1,0:T(8,128)(2,1)S(1)} all-gather(bf16[1,18,2048]{2,1,0:T(8,128)(2,1)S(1)} %fusion.47), channel_id=2, replica_groups=mesh['dp'=8,'expert'=64] {'dp'}, dimensions={0}, use_global_device_ids=true | all-gather | bytes 663552 | tf_op jit(solution)/shard_map/all_gather | solution.py:287
  244.5 2.0 select_reduce_fusion
  246.6 6.5 %all-gather.7.cloned.1.call-done = bf16[1024,1408]{0,1:T(8,128)(2,1)} async-done(((bf16[1024,176]{0,1:T(8,128)(2,1)}), bf16[1024,1408]{0,1:T(8,128)(2,1)}) %all-gather.7.cloned.1.call-update) | async-done | bytes 2883600 | tf_op jit(solution)/shard_map/all_gather | solution.py:322
  253.1 3.6 %convolution_convert_fusion = bf16[1024,256]{1,0:T(8,128)(2,1)} fusion(bf16[1024,1408]{0,1:T(8,128)(2,1)} %all-gather.7.cloned.1.call-done, bf16[1,1408,256]{2,1,0:T(8,128)(2,1)S(1)} %copy-done), kind=kOutput, calls=%fused_computation.5 | convolution fusion | flops 738459648 | bytes 4128768 | tf_op jit(solution)/shard_map/dot_general | solution.py:324
  256.8 15.3 %all-to-all-start.2 = ((bf16[64,16,256]{2,1,0:T(8,128)(2,1)}), bf16[64,16,256]{2,1,0:T(8,128)(2,1)S(1)}, u32[]{:S(2)}, u32[]{:S(2)}) async-start(bf16[64,16,256]{2,1,0:T(8,128)(2,1)} %bitcast.158), calls=%async_computation.2 | async-start | bytes 1048576 | tf_op jit(solution)/shard_map/all_to_all | solution.py:328
  272.1 0.7 sub.97
  272.8 0.7 sub.100
  273.5 0.7 reshape.488
  274.3 1.3 reshape.479
  275.9 1.5 fusion.11
  277.5 13.5 %all-gather.3 = bf16[8,176,136]{1,2,0:T(8,128)(2,1)S(1)} all-gather(bf16[1,176,136]{1,2,0:T(8,128)(2,1)S(1)} %fusion.11), channel_id=1, replica_groups=mesh['dp'=8,'expert'=64] {'dp'}, dimensions={0}, use_global_device_ids=true | all-gather | bytes 430848 | tf_op jit(solution)/shard_map/all_gather | solution.py:323
  291.1 1.2 reshape.513
  292.4 1.0 copy.92
  293.3 0.8 fusion.90
  294.4 1.0 fusion.52
  295.6 1.3 fusion.33
  296.8 10.7 %gather_fusion.1 = f32[816]{0:T(1024)S(1)} fusion(f32[136,64]{0,1:T(8,128)S(1)} %fusion.33, s32[816]{0:T(1024)S(1)} %reshape.500), kind=kCustom, calls=%fused_computation.1 | custom fusion | bytes 13056 | tf_op jit(solution)/shard_map/jit(take_along_axis)/gather | solution.py:342
  308.1 3.4 %gather_fusion = bf16[816,256]{1,0:T(8,128)(2,1)S(1)} fusion(bf16[1024,256]{1,0:T(8,128)(2,1)S(1)} %bitcast.141, s32[1024]{0:T(1024)S(1)} %pad_clamp_fusion), kind=kCustom, calls=%fused_computation | custom fusion | bytes 838848 | tf_op jit(solution)/shard_map/jit(_take)/gather | solution.py:339
  312.6 8.1 %all_to_all.38 = bf16[8,17,256]{2,1,0:T(8,128)(2,1)S(1)} all-to-all(bf16[8,17,256]{2,1,0:T(8,128)(2,1)S(1)} %convert_element_type.222), channel_id=1, replica_groups=mesh['dp'=8,'expert'=64] {'dp'}, dimensions={0} | all-to-all | bytes 139264 | tf_op jit(solution)/shard_map/all_to_all | solution.py:348
  (127 shorter events, 13.4 us)
Async XLA Ops:
  7.2 246.0 %copy-start = (bf16[1,1408,256]{2,1,0:T(8,128)(2,1)S(1)}, bf16[1,1408,256]{2,1,0:T(8,128)(2,1)}, u32[]{:S(2)}) copy-start(bf16[1,1408,256]{2,1,0:T(8,128)(2,1)} %param.36) | copy-start | bytes 2162692
  7.2 8.5 %copy-start.5 = (bf16[1,1024,576]{1,2,0:T(8,128)(2,1)S(1)}, bf16[1,1024,576]{1,2,0:T(8,128)(2,1)}, u32[]{:S(2)}) copy-start(bf16[1,1024,576]{1,2,0:T(8,128)(2,1)} %param.27) | copy-start | bytes 3538948
  7.2 8.4 %copy-start.14 = (f32[16]{0:T(128)S(1)}, f32[16]{0:T(128)}, u32[]{:S(2)}) copy-start(f32[16]{0:T(128)} %param.28) | copy-start | bytes 196
  7.2 20.0 %copy-start.16 = (bf16[2,8,128]{2,1,0:T(8,128)(2,1)S(1)}, bf16[2,8,128]{2,1,0:T(8,128)(2,1)}, u32[]{:S(2)}) copy-start(bf16[2,8,128]{2,1,0:T(8,128)(2,1)} %param.29) | copy-start | bytes 12292
  7.2 20.0 %copy-start.9 = (bf16[2,2,2048]{2,1,0:T(2,128)(2,1)S(1)}, bf16[2,2,2048]{2,1,0:T(2,128)(2,1)}, u32[]{:S(2)}) copy-start(bf16[2,2,2048]{2,1,0:T(2,128)(2,1)} %param.30) | copy-start | bytes 49156
  7.2 20.1 %copy-start.7 = (bf16[32,176]{1,0:T(8,128)(2,1)S(1)}, bf16[32,176]{1,0:T(8,128)(2,1)}, u32[]{:S(2)}) copy-start(bf16[32,176]{1,0:T(8,128)(2,1)} %param.37) | copy-start | bytes 33796
  7.2 20.2 %copy-start.8 = (bf16[32,176]{1,0:T(8,128)(2,1)S(1)}, bf16[32,176]{1,0:T(8,128)(2,1)}, u32[]{:S(2)}) copy-start(bf16[32,176]{1,0:T(8,128)(2,1)} %param.38) | copy-start | bytes 33796
  7.2 20.3 %copy-start.11 = (bf16[22,256]{1,0:T(8,128)(2,1)S(1)}, bf16[22,256]{1,0:T(8,128)(2,1)}, u32[]{:S(2)}) copy-start(bf16[22,256]{1,0:T(8,128)(2,1)} %param.39) | copy-start | bytes 33796
  7.3 20.3 %copy-start.13 = (bf16[2048,1]{0,1:T(2,128)(2,1)S(1)}, bf16[2048,1]{0,1:T(2,128)(2,1)}, u32[]{:S(2)}) copy-start(bf16[2048,1]{0,1:T(2,128)(2,1)} %param.32) | copy-start | bytes 12292
  17.0 84.4 %all-to-all-start = ((bf16[17,16,512]{2,0,1:T(8,128)(2,1)}), bf16[17,16,512]{2,0,1:T(8,128)(2,1)S(1)}, u32[]{:S(2)}, u32[]{:S(2)}) async-start(bf16[17,16,512]{2,0,1:T(8,128)(2,1)} %copy.78), calls=%async_computation | async-start | bytes 786432 | tf_op jit(solution)/shard_map/all_to_all | solution.py:266
  27.2 181.9 %all-gather.9.cloned.1.call-start = ((), (), s32[]{:S(2)}) async-start(), calls=%async_computation.5 | async-start | bytes 4718592 | tf_op jit(solution)/shard_map/all_gather | solution.py:308
  93.9 1.8 copy-start.1
  95.7 4.8 %copy-start.10 = (s32[17,6]{0,1:T(8,128)S(1)}, s32[17,6]{0,1:T(8,128)}, u32[]{:S(2)}) copy-start(s32[17,6]{0,1:T(8,128)} %param.33) | copy-start | bytes 1228
  96.5 37.7 %copy-start.15 = (bf16[2048]{0:T(1024)(128)(2,1)S(1)}, bf16[2048]{0:T(1024)(128)(2,1)}, u32[]{:S(2)}) copy-start(bf16[2048]{0:T(1024)(128)(2,1)} %param.31) | copy-start | bytes 12292
  98.2 38.6 %copy-start.6 = (bf16[16,2048]{1,0:T(8,128)(2,1)S(1)}, bf16[16,2048]{1,0:T(8,128)(2,1)}, u32[]{:S(2)}) copy-start(bf16[16,2048]{1,0:T(8,128)(2,1)} %param.22) | copy-start | bytes 196612
  98.2 38.6 %copy-start.12 = (bf16[1,2048]{1,0:T(2,128)(2,1)S(1)}, bf16[1,2048]{1,0:T(2,128)(2,1)}, u32[]{:S(2)}) copy-start(bf16[1,2048]{1,0:T(2,128)(2,1)} %param.25) | copy-start | bytes 12292
  125.0 11.2 %collective-permute-start = (bf16[24,2048]{1,0:T(8,128)(2,1)S(1)}, bf16[24,2048]{1,0:T(8,128)(2,1)S(1)}, u32[]{:S(2)}, u32[]{:S(2)}) collective-permute-start(bf16[24,2048]{1,0:T(8,128)(2,1)S(1)} %fusion), channel_id=1, source_target_pairs={{0,64},{64,128},{128,192},{192,256},{256,320},{320,384},{384,448},... | collective-permute-start | bytes 294920
  127.1 9.1 %collective-permute-start.1 = (bf16[24,2048]{1,0:T(8,128)(2,1)S(1)}, bf16[24,2048]{1,0:T(8,128)(2,1)S(1)}, u32[]{:S(2)}, u32[]{:S(2)}) collective-permute-start(bf16[24,2048]{1,0:T(8,128)(2,1)S(1)} %fusion), channel_id=1, source_target_pairs={{0,128},{64,192},{128,256},{192,320},{256,384},{320,448},{1,129},{... | collective-permute-start | bytes 294920
  129.5 6.7 %collective-permute-start.2 = (bf16[1,2048]{1,0:T(2,128)(2,1)S(1)}, bf16[1,2048]{1,0:T(2,128)(2,1)S(1)}, u32[]{:S(2)}, u32[]{:S(2)}) collective-permute-start(bf16[1,2048]{1,0:T(2,128)(2,1)S(1)} %slice.96), channel_id=1, source_target_pairs={{0,192},{64,256},{128,320},{192,384},{256,448},{1,193},{65,257},{1... | collective-permute-start | bytes 12296
  178.2 35.4 %copy-start.17 = (bf16[1,2048,176]{1,2,0:T(8,128)(2,1)S(1)}, bf16[1,2048,176]{1,2,0:T(8,128)(2,1)}, u32[]{:S(2)}) copy-start(bf16[1,2048,176]{1,2,0:T(8,128)(2,1)} %param.34) | copy-start | bytes 2162692
  178.2 74.9 %all-gather.7.cloned.1.call-start = ((), (), s32[]{:S(2)}) async-start(), calls=%async_computation.4 | async-start | bytes 3244032 | tf_op jit(solution)/shard_map/all_gather | solution.py:322
  213.6 1.6 copy-start.18
  244.4 12.4 %copy-start.2 = (bf16[8,18,2048]{2,1,0:T(8,128)(2,1)}, bf16[8,18,2048]{2,1,0:T(8,128)(2,1)S(1)}, u32[]{:S(2)}) copy-start(bf16[8,18,2048]{2,1,0:T(8,128)(2,1)S(1)} %all-gather.2) | copy-start | bytes 1769476
  256.8 51.3 %all-to-all-start.2 = ((bf16[64,16,256]{2,1,0:T(8,128)(2,1)}), bf16[64,16,256]{2,1,0:T(8,128)(2,1)S(1)}, u32[]{:S(2)}, u32[]{:S(2)}) async-start(bf16[64,16,256]{2,1,0:T(8,128)(2,1)} %bitcast.158), calls=%async_computation.2 | async-start | bytes 1048576 | tf_op jit(solution)/shard_map/all_to_all | solution.py:328
  307.5 4.7 %copy-start.3 = (bf16[1408,256]{1,0:T(8,128)(2,1)S(1)}, bf16[1408,256]{1,0:T(8,128)(2,1)}, u32[]{:S(2)}) copy-start(bf16[1408,256]{1,0:T(8,128)(2,1)} %reshape_reshape.12) | copy-start | bytes 2162692
  307.5 4.7 %copy-start.4 = (bf16[1408,136]{0,1:T(8,128)(2,1)S(1)}, bf16[1408,136]{0,1:T(8,128)(2,1)}, u32[]{:S(2)}) copy-start(bf16[1408,136]{0,1:T(8,128)(2,1)} %reshape.513) | copy-start | bytes 1148932
Sparse Core Ops, SparseCore 0:
  178.3 30.7 all-gather.8
  217.7 35.4 all-gather.6

commit v7 on v6

--- a/solution.py
+++ b/solution.py
@@ -298,13 +298,15 @@
         rows_dev, members, capacity
     )
     outgoing = jnp.einsum("rxc,rd->xcd", own_matrix, normed, preferred_element_type=jnp.bfloat16)
+    shared_gate_full, shared_up_full = weights["shared_gate"], weights["shared_up"]
+    shared_down_full, router_full = weights["shared_down"], weights["router"]
+    shared_act = (
+        jax.nn.silu(jnp.dot(group_tokens, shared_gate_full, preferred_element_type=jnp.float32))
+        * jnp.dot(group_tokens, shared_up_full, preferred_element_type=jnp.float32)
+    ).astype(jnp.bfloat16)
+    shared_piece = lax.all_gather(shared_act, "dp", axis=1, tiled=True)
     arrived = lax.all_to_all(outgoing, "expert", split_axis=0, concat_axis=0, tiled=True)
-    shared_ready = (
-        weights["shared_gate"],
-        weights["shared_up"],
-        weights["shared_down"],
-        weights["router"],
-    )
+    arrived, shared_piece = lax.optimization_barrier((arrived, shared_piece))
     expert_rows = lax.all_gather(
         arrived.reshape(members, 1, capacity, D), "dp", axis=1, tiled=True
     )
@@ -312,15 +314,9 @@
     gate_proj = jnp.dot(expert_rows, gate_weight[0], preferred_element_type=jnp.float32)
     up_proj = jnp.dot(expert_rows, up_weight[0], preferred_element_type=jnp.float32)
     expert_act = (jax.nn.silu(gate_proj) * up_proj).astype(jnp.bfloat16)
-    shared_gate_full, shared_up_full, shared_down_full, router_full = shared_ready
-    shared_act = (
-        jax.nn.silu(jnp.dot(group_tokens, shared_gate_full, preferred_element_type=jnp.float32))
-        * jnp.dot(group_tokens, shared_up_full, preferred_element_type=jnp.float32)
-    ).astype(jnp.bfloat16)
     down_local = down_weight[0]
     col_width = down_local.shape[1]
     routed_piece = lax.all_gather(expert_act, "dp", axis=1, tiled=True)
-    shared_piece = lax.all_gather(shared_act, "dp", axis=1, tiled=True)
     routed_cols = jnp.dot(routed_piece, down_local, preferred_element_type=jnp.float32)
     shared_cols = jnp.dot(shared_piece, shared_down_full, preferred_element_type=jnp.float32)
     expert_out = routed_cols.astype(jnp.bfloat16)

time: 330 us -> 345 us (1.045)
  waiting for transfers between devices: 37.3 us -> 85.9 us
  blocking collectives: 97.3 us -> 59.5 us
  starting transfers between devices: 34.9 us -> 43.2 us
    all_to_all x1 -> x0, blocking collectives: 39.1 us -> none  [shards(): lax.all_to_all(outgoing, 'expert', split_axis=0, concat_axis=0, tiled=True)]
    all_gather x1, waiting for transfers between devices: 6.52 us -> 32.6 us  [shards(): routed_piece = lax.all_gather(expert_act, 'dp', axis=1, tiled=True)]
    all_to_all x1, waiting for transfers between devices: 0.01 us -> 14.4 us  [shards(): lax.all_to_all(expert_out.reshape(members, groups * capacity, col_width),...]
    all_to_all x0 -> x1, starting transfers between devices: none -> 8.33 us  [shards(): lax.all_to_all(outgoing, 'expert', split_axis=0, concat_axis=0, tiled=True)]
    all_gather x1, waiting for transfers between devices: 30.7 us -> 38.9 us  [shards(): lax.all_gather(arrived.reshape(members, 1, capacity, D), 'dp', axis=1, ti...]
  transfers between devices with their start and end apart: 7 -> 8, of which waited for: 2 -> 3; matrix products, arithmetic and copies ran while one was open for 15% -> 13% of each run, Pallas kernels for 19% -> 18%
where the time goes in v7:
time: 345 us; the launch traced here: 344 us
  waiting for transfers between devices  85.9 us (25%)
  Pallas kernels  61.6 us (18%)
  blocking collectives  59.5 us (17%)
  local copies, waits for them, and re-layouts  53.4 us (15%)
  starting transfers between devices  43.2 us (13%)
  matrix products  17.5 us (5%)
  between operations  16.3 us (5%)
  other arithmetic  6.65 us (2%)
    pallas_call x1, Pallas kernels, expert_gather(): pl.pallas_call(partial(gather_kernel, nx, nz), out_shape=jax.ShapeDtypeSt...  61.6 us
    all_gather x1, waiting for transfers between devices, shards(): lax.all_gather(arrived.reshape(members, 1, capacity, D), 'dp', axis=1, ti...  38.9 us
    all_gather x1, waiting for transfers between devices, shards(): routed_piece = lax.all_gather(expert_act, 'dp', axis=1, tiled=True)  32.6 us
    unnamed x1, blocking collectives  22 us
    all_to_all x1, starting transfers between devices, shards(): lax.all_to_all(expert_out.reshape(members, groups * capacity, col_width),...  15.6 us
    all_to_all x1, waiting for transfers between devices, shards(): lax.all_to_all(expert_out.reshape(members, groups * capacity, col_width),...  14.4 us
    all_gather x1, blocking collectives, shards(): lax.all_gather(jnp.concatenate([normed, route_row], axis=0)[None], 'dp',...  13.6 us
    all_gather x1, blocking collectives, shards(): shared_piece = lax.all_gather(shared_act, 'dp', axis=1, tiled=True)  13.1 us
  transfers between devices with their start and end apart: 8, of which 3 were waited for; matrix products, arithmetic and copies ran while one was open for 13% of the time, Pallas kernels for 18%

profile of v7, /device:TPU:1, one launch (start us, length us, event | category | flops | bytes accessed | tf_op | source)
XLA Modules:
  0.0 344.0 jit_solution(7128314942737832224)
XLA Ops:
  8.0 0.7 slice_convert_fusion.1
  8.7 1.7 fusion.93
  10.4 0.9 convert_convert_fusion
  11.3 1.6 fusion.94
  12.9 0.7 broadcast_maximum_fusion
  13.7 0.7 exponential_add_fusion
  14.3 1.1 fusion.3
  16.1 0.9 copy.78
  17.0 10.2 %all-to-all-start = ((bf16[17,16,512]{2,0,1:T(8,128)(2,1)}), bf16[17,16,512]{2,0,1:T(8,128)(2,1)S(1)}, u32[]{:S(2)}, u32[]{:S(2)}) async-start(bf16[17,16,512]{2,0,1:T(8,128)(2,1)} %copy.78), calls=%async_computation | async-start | bytes 786432 | tf_op jit(solution)/shard_map/all_to_all | solution.py:266
  29.6 61.6 %shard_map.203 = bf16[16,4,232,128]{3,2,1,0:T(8,128)(2,1)} custom-call(bf16[232,128]{1,0:T(8,128)(2,1)} %pad_bitcast_fusion.shard_ref), custom_call_target="tpu_custom_call" | custom-call | tf_op jit(solution)/shard_map/pallas_call | solution.py:137
  91.2 2.3 copy.75
  94.1 1.8 copy-done.1
  96.6 0.7 sub.97
  97.4 0.8 reshape.476
  98.2 1.7 copy.81
  99.9 1.5 reshape.477
  101.4 0.7 multiply_add_fusion
  103.1 22.0 %fusion = bf16[24,2048]{1,0:T(8,128)(2,1)S(1)} fusion(bf16[136,2048]{1,0:T(8,128)(2,1)S(1)} %fusion.1), kind=kCustom, calls=%all-reduce-scatter | all-reduce-scatter fusion | flops 393217 | bytes 657408
  125.1 1.3 collective-permute-start.1
  126.4 3.4 collective-permute-start
  129.8 3.9 %collective-permute-start.2 = (bf16[1,2048]{1,0:T(2,128)(2,1)S(1)}, bf16[1,2048]{1,0:T(2,128)(2,1)S(1)}, u32[]{:S(2)}, u32[]{:S(2)}) collective-permute-start(bf16[1,2048]{1,0:T(2,128)(2,1)S(1)} %slice.96), channel_id=1, source_target_pairs={{0,192},{64,256},{128,320},{192,384},{256,448},{1,193},{65,257},{1... | collective-permute-start | bytes 12296
  133.9 1.3 dynamic-slice.4
  137.2 1.4 copy.84
  138.6 8.3 %all-to-all-start.1 = ((bf16[64,2,2048]{2,1,0:T(2,128)(2,1)}), bf16[64,2,2048]{2,1,0:T(2,128)(2,1)}, u32[]{:S(2)}, u32[]{:S(2)}) async-start(bf16[64,2,2048]{2,1,0:T(2,128)(2,1)} %copy.84), calls=%async_computation.1 | async-start | bytes 1048576 | tf_op jit(solution)/shard_map/all_to_all | solution.py:308
  147.1 2.6 fusion.92
  149.8 3.0 reshape_reshape.11
  152.8 2.0 reshape_reshape.10
  154.8 13.6 %all-gather.2 = bf16[8,18,2048]{2,1,0:T(8,128)(2,1)S(1)} all-gather(bf16[1,18,2048]{2,1,0:T(8,128)(2,1)S(1)} %fusion.47), channel_id=2, replica_groups=mesh['dp'=8,'expert'=64] {'dp'}, dimensions={0}, use_global_device_ids=true | all-gather | bytes 663552 | tf_op jit(solution)/shard_map/all_gather | solution.py:287
  168.9 1.5 fusion.11
  170.5 13.1 %all-gather.3 = bf16[8,176,136]{1,2,0:T(8,128)(2,1)S(1)} all-gather(bf16[1,176,136]{1,2,0:T(8,128)(2,1)S(1)} %fusion.11), channel_id=1, replica_groups=mesh['dp'=8,'expert'=64] {'dp'}, dimensions={0}, use_global_device_ids=true | all-gather | bytes 430848 | tf_op jit(solution)/shard_map/all_gather | solution.py:307
  183.6 0.9 copy.86
  184.5 2.4 reshape.513
  186.9 2.0 copy.97
  189.3 38.9 %all-gather.9.cloned.1.call-done = bf16[64,16,2048]{2,0,1:T(8,128)(2,1)} async-done(((bf16[64,2,2048]{2,0,1:T(8,128)(2,1)}), bf16[64,16,2048]{2,0,1:T(8,128)(2,1)}) %all-gather.9.cloned.1.call-update) | async-done | bytes 4194320 | tf_op jit(solution)/shard_map/all_gather | solution.py:310
  228.1 4.5 %copy.98 = bf16[64,16,2048]{2,1,0:T(8,128)(2,1)S(1)} copy(bf16[64,16,2048]{2,0,1:T(8,128)(2,1)} %all-gather.9.cloned.1.call-done) | data formatting | bytes 8388608 | tf_op jit(solution)/shard_map/all_gather | solution.py:310
  232.7 1.6 fusion.27
  234.2 2.4 fusion.2
  236.8 1.7 reshape_reshape.12
  238.6 32.6 %all-gather.7.cloned.1.call-done = bf16[1024,1408]{0,1:T(8,128)(2,1)} async-done(((bf16[1024,176]{0,1:T(8,128)(2,1)}), bf16[1024,1408]{0,1:T(8,128)(2,1)}) %all-gather.7.cloned.1.call-update) | async-done | bytes 2883600 | tf_op jit(solution)/shard_map/all_gather | solution.py:319
  271.2 3.6 %convolution_convert_fusion = bf16[1024,256]{1,0:T(8,128)(2,1)} fusion(bf16[1024,1408]{0,1:T(8,128)(2,1)} %all-gather.7.cloned.1.call-done, bf16[1,1408,256]{2,1,0:T(8,128)(2,1)S(1)} %copy-done), kind=kOutput, calls=%fused_computation.5 | convolution fusion | flops 738459648 | bytes 4128768 | tf_op jit(solution)/shard_map/dot_general | solution.py:320
  274.8 15.6 %all-to-all-start.2 = ((bf16[64,16,256]{2,1,0:T(8,128)(2,1)}), bf16[64,16,256]{2,1,0:T(8,128)(2,1)S(1)}, u32[]{:S(2)}, u32[]{:S(2)}) async-start(bf16[64,16,256]{2,1,0:T(8,128)(2,1)} %bitcast.34), calls=%async_computation.2 | async-start | bytes 1048576 | tf_op jit(solution)/shard_map/all_to_all | solution.py:324
  290.6 2.0 select_reduce_fusion
  293.7 1.3 fusion.33
  295.0 10.7 %gather_fusion.1 = f32[816]{0:T(1024)S(1)} fusion(f32[136,64]{0,1:T(8,128)S(1)} %fusion.33, s32[816]{0:T(1024)S(1)} %reshape.500), kind=kCustom, calls=%fused_computation.1 | custom fusion | bytes 13056 | tf_op jit(solution)/shard_map/jit(take_along_axis)/gather | solution.py:338
  306.1 14.4 %all-to-all-done.2 = bf16[64,16,256]{2,1,0:T(8,128)(2,1)S(1)} async-done(((bf16[64,16,256]{2,1,0:T(8,128)(2,1)}), bf16[64,16,256]{2,1,0:T(8,128)(2,1)S(1)}, u32[]{:S(2)}, u32[]{:S(2)}) %all-to-all-start.2) | async-done | bytes 524320 | tf_op jit(solution)/shard_map/all_to_all | solution.py:324
  320.5 3.4 gather_fusion
  325.0 10.8 %all_to_all.37 = bf16[8,17,256]{2,1,0:T(8,128)(2,1)S(1)} all-to-all(bf16[8,17,256]{2,1,0:T(8,128)(2,1)S(1)} %convert_element_type.222), channel_id=1, replica_groups=mesh['dp'=8,'expert'=64] {'dp'}, dimensions={0} | all-to-all | bytes 139264 | tf_op jit(solution)/shard_map/all_to_all | solution.py:344
  336.6 0.6 slice.94
  (128 shorter events, 11.4 us)
Async XLA Ops:
  7.2 264.0 %copy-start = (bf16[1,1408,256]{2,1,0:T(8,128)(2,1)S(1)}, bf16[1,1408,256]{2,1,0:T(8,128)(2,1)}, u32[]{:S(2)}) copy-start(bf16[1,1408,256]{2,1,0:T(8,128)(2,1)} %param.36) | copy-start | bytes 2162692
  7.2 8.5 %copy-start.5 = (bf16[1,1024,576]{1,2,0:T(8,128)(2,1)S(1)}, bf16[1,1024,576]{1,2,0:T(8,128)(2,1)}, u32[]{:S(2)}) copy-start(bf16[1,1024,576]{1,2,0:T(8,128)(2,1)} %param.27) | copy-start | bytes 3538948
  7.2 8.4 %copy-start.14 = (f32[16]{0:T(128)S(1)}, f32[16]{0:T(128)}, u32[]{:S(2)}) copy-start(f32[16]{0:T(128)} %param.28) | copy-start | bytes 196
  7.2 20.0 %copy-start.7 = (bf16[32,176]{1,0:T(8,128)(2,1)S(1)}, bf16[32,176]{1,0:T(8,128)(2,1)}, u32[]{:S(2)}) copy-start(bf16[32,176]{1,0:T(8,128)(2,1)} %param.37) | copy-start | bytes 33796
  7.2 20.1 %copy-start.8 = (bf16[32,176]{1,0:T(8,128)(2,1)S(1)}, bf16[32,176]{1,0:T(8,128)(2,1)}, u32[]{:S(2)}) copy-start(bf16[32,176]{1,0:T(8,128)(2,1)} %param.38) | copy-start | bytes 33796
  7.2 20.2 %copy-start.11 = (bf16[22,256]{1,0:T(8,128)(2,1)S(1)}, bf16[22,256]{1,0:T(8,128)(2,1)}, u32[]{:S(2)}) copy-start(bf16[22,256]{1,0:T(8,128)(2,1)} %param.39) | copy-start | bytes 33796
  7.2 20.3 %copy-start.9 = (bf16[2,2,2048]{2,1,0:T(2,128)(2,1)S(1)}, bf16[2,2,2048]{2,1,0:T(2,128)(2,1)}, u32[]{:S(2)}) copy-start(bf16[2,2,2048]{2,1,0:T(2,128)(2,1)} %param.30) | copy-start | bytes 49156
  7.2 20.3 %copy-start.16 = (bf16[2,8,128]{2,1,0:T(8,128)(2,1)S(1)}, bf16[2,8,128]{2,1,0:T(8,128)(2,1)}, u32[]{:S(2)}) copy-start(bf16[2,8,128]{2,1,0:T(8,128)(2,1)} %param.29) | copy-start | bytes 12292
  7.3 20.3 %copy-start.13 = (bf16[2048,1]{0,1:T(2,128)(2,1)S(1)}, bf16[2048,1]{0,1:T(2,128)(2,1)}, u32[]{:S(2)}) copy-start(bf16[2048,1]{0,1:T(2,128)(2,1)} %param.32) | copy-start | bytes 12292
  17.0 85.3 %all-to-all-start = ((bf16[17,16,512]{2,0,1:T(8,128)(2,1)}), bf16[17,16,512]{2,0,1:T(8,128)(2,1)S(1)}, u32[]{:S(2)}, u32[]{:S(2)}) async-start(bf16[17,16,512]{2,0,1:T(8,128)(2,1)} %copy.78), calls=%async_computation | async-start | bytes 786432 | tf_op jit(solution)/shard_map/all_to_all | solution.py:266
  93.6 2.4 copy-start.10
  94.1 1.8 copy-start.1
  98.2 38.3 %copy-start.6 = (bf16[16,2048]{1,0:T(8,128)(2,1)S(1)}, bf16[16,2048]{1,0:T(8,128)(2,1)}, u32[]{:S(2)}) copy-start(bf16[16,2048]{1,0:T(8,128)(2,1)} %param.22) | copy-start | bytes 196612
  99.9 34.0 %copy-start.15 = (bf16[2048]{0:T(1024)(128)(2,1)S(1)}, bf16[2048]{0:T(1024)(128)(2,1)}, u32[]{:S(2)}) copy-start(bf16[2048]{0:T(1024)(128)(2,1)} %param.31) | copy-start | bytes 12292
  99.9 36.6 %copy-start.12 = (bf16[1,2048]{1,0:T(2,128)(2,1)S(1)}, bf16[1,2048]{1,0:T(2,128)(2,1)}, u32[]{:S(2)}) copy-start(bf16[1,2048]{1,0:T(2,128)(2,1)} %param.25) | copy-start | bytes 12292
  125.1 10.8 %collective-permute-start.1 = (bf16[24,2048]{1,0:T(8,128)(2,1)S(1)}, bf16[24,2048]{1,0:T(8,128)(2,1)S(1)}, u32[]{:S(2)}, u32[]{:S(2)}) collective-permute-start(bf16[24,2048]{1,0:T(8,128)(2,1)S(1)} %fusion), channel_id=1, source_target_pairs={{0,128},{64,192},{128,256},{192,320},{256,384},{320,448},{1,129},{... | collective-permute-start | bytes 294920
  126.4 9.5 %collective-permute-start = (bf16[24,2048]{1,0:T(8,128)(2,1)S(1)}, bf16[24,2048]{1,0:T(8,128)(2,1)S(1)}, u32[]{:S(2)}, u32[]{:S(2)}) collective-permute-start(bf16[24,2048]{1,0:T(8,128)(2,1)S(1)} %fusion), channel_id=1, source_target_pairs={{0,64},{64,128},{128,192},{192,256},{256,320},{320,384},{384,448},... | collective-permute-start | bytes 294920
  129.8 6.1 %collective-permute-start.2 = (bf16[1,2048]{1,0:T(2,128)(2,1)S(1)}, bf16[1,2048]{1,0:T(2,128)(2,1)S(1)}, u32[]{:S(2)}, u32[]{:S(2)}) collective-permute-start(bf16[1,2048]{1,0:T(2,128)(2,1)S(1)} %slice.96), channel_id=1, source_target_pairs={{0,192},{64,256},{128,320},{192,384},{256,448},{1,193},{65,257},{1... | collective-permute-start | bytes 12296
  138.6 48.4 %all-to-all-start.1 = ((bf16[64,2,2048]{2,1,0:T(2,128)(2,1)}), bf16[64,2,2048]{2,1,0:T(2,128)(2,1)}, u32[]{:S(2)}, u32[]{:S(2)}) async-start(bf16[64,2,2048]{2,1,0:T(2,128)(2,1)} %copy.84), calls=%async_computation.1 | async-start | bytes 1048576 | tf_op jit(solution)/shard_map/all_to_all | solution.py:308
  146.9 81.2 %all-gather.9.cloned.1.call-start = ((), (), s32[]{:S(2)}) async-start(), calls=%async_computation.5 | async-start | bytes 4718592 | tf_op jit(solution)/shard_map/all_gather | solution.py:310
  189.0 43.6 %copy-start.17 = (bf16[1,2048,176]{1,2,0:T(8,128)(2,1)S(1)}, bf16[1,2048,176]{1,2,0:T(8,128)(2,1)}, u32[]{:S(2)}) copy-start(bf16[1,2048,176]{1,2,0:T(8,128)(2,1)} %param.34) | copy-start | bytes 2162692
  189.0 82.2 %all-gather.7.cloned.1.call-start = ((), (), s32[]{:S(2)}) async-start(), calls=%async_computation.4 | async-start | bytes 3244032 | tf_op jit(solution)/shard_map/all_gather | solution.py:319
  232.6 1.6 copy-start.18
  234.2 2.6 copy-start.3
  274.8 45.7 %all-to-all-start.2 = ((bf16[64,16,256]{2,1,0:T(8,128)(2,1)}), bf16[64,16,256]{2,1,0:T(8,128)(2,1)S(1)}, u32[]{:S(2)}, u32[]{:S(2)}) async-start(bf16[64,16,256]{2,1,0:T(8,128)(2,1)} %bitcast.34), calls=%async_computation.2 | async-start | bytes 1048576 | tf_op jit(solution)/shard_map/all_to_all | solution.py:324
  305.7 18.9 %copy-start.2 = (bf16[1408,256]{1,0:T(8,128)(2,1)S(1)}, bf16[1408,256]{1,0:T(8,128)(2,1)}, u32[]{:S(2)}) copy-start(bf16[1408,256]{1,0:T(8,128)(2,1)} %reshape_reshape.12) | copy-start | bytes 2162692
  305.7 18.9 %copy-start.4 = (bf16[1408,136]{0,1:T(8,128)(2,1)S(1)}, bf16[1408,136]{0,1:T(8,128)(2,1)}, u32[]{:S(2)}) copy-start(bf16[1408,136]{0,1:T(8,128)(2,1)} %reshape.513) | copy-start | bytes 1148932
Sparse Core Ops, SparseCore 0:
  189.1 38.9 all-gather.8
  236.8 34.3 all-gather.6

commit v8 on v6

--- a/solution.py
+++ b/solution.py
@@ -284,31 +284,28 @@
     capacity = max(2, (rows_dev * TOPK + members - 1) // members)
     route_row = routes.astype(jnp.bfloat16).reshape(1, rows_dev * TOPK)
     route_row = jnp.pad(route_row, ((0, 0), (0, D - rows_dev * TOPK)))
-    group_both = lax.all_gather(
-        jnp.concatenate([normed, route_row], axis=0)[None], "dp", axis=0, tiled=True
-    )
-    group_tokens = group_both[:, :rows_dev].reshape(groups * rows_dev, D)
-    group_routes = (
-        group_both[:, rows_dev, : rows_dev * TOPK].astype(jnp.int32).reshape(-1, TOPK)
-    )
-    routes_by_group = group_routes.reshape(groups, rows_dev, TOPK)
-    slots_by_group = jax.vmap(partial(assign_slots, experts=members))(routes_by_group)
     own_slots = assign_slots(routes, members)
     own_matrix = dispatch_matrix(routes, own_slots, members, capacity).reshape(
         rows_dev, members, capacity
     )
     outgoing = jnp.einsum("rxc,rd->xcd", own_matrix, normed, preferred_element_type=jnp.bfloat16)
     arrived = lax.all_to_all(outgoing, "expert", split_axis=0, concat_axis=0, tiled=True)
+    slots_in = members * capacity
+    combined = jnp.concatenate([arrived.reshape(slots_in, D), normed, route_row], axis=0)
+    group_all = lax.all_gather(combined[None], "dp", axis=0, tiled=True)
+    expert_rows = group_all[:, :slots_in].reshape(-1, D)
+    group_tokens = group_all[:, slots_in : slots_in + rows_dev].reshape(groups * rows_dev, D)
+    group_routes = (
+        group_all[:, slots_in + rows_dev, : rows_dev * TOPK].astype(jnp.int32).reshape(-1, TOPK)
+    )
+    routes_by_group = group_routes.reshape(groups, rows_dev, TOPK)
+    slots_by_group = jax.vmap(partial(assign_slots, experts=members))(routes_by_group)
     shared_ready = (
         weights["shared_gate"],
         weights["shared_up"],
         weights["shared_down"],
         weights["router"],
     )
-    expert_rows = lax.all_gather(
-        arrived.reshape(members, 1, capacity, D), "dp", axis=1, tiled=True
-    )
-    expert_rows = expert_rows.reshape(-1, D)
     gate_proj = jnp.dot(expert_rows, gate_weight[0], preferred_element_type=jnp.float32)
     up_proj = jnp.dot(expert_rows, up_weight[0], preferred_element_type=jnp.float32)
     expert_act = (jax.nn.silu(gate_proj) * up_proj).astype(jnp.bfloat16)
@@ -319,12 +316,15 @@
     ).astype(jnp.bfloat16)
     down_local = down_weight[0]
     col_width = down_local.shape[1]
-    routed_piece = lax.all_gather(expert_act, "dp", axis=1, tiled=True)
-    shared_piece = lax.all_gather(shared_act, "dp", axis=1, tiled=True)
+    both_acts = jnp.concatenate([expert_act, shared_act], axis=0)
+    both_pieces = lax.all_gather(both_acts, "dp", axis=1, tiled=True)
+    routed_piece = both_pieces[: expert_act.shape[0]]
+    shared_piece = both_pieces[expert_act.shape[0] :]
     routed_cols = jnp.dot(routed_piece, down_local, preferred_element_type=jnp.float32)
     shared_cols = jnp.dot(shared_piece, shared_down_full, preferred_element_type=jnp.float32)
     expert_out = routed_cols.astype(jnp.bfloat16)
     shared_out = shared_cols.astype(jnp.bfloat16)
+    expert_out = jnp.swapaxes(expert_out.reshape(groups, members, capacity, col_width), 0, 1)
     returned = lax.all_to_all(
         expert_out.reshape(members, groups * capacity, col_width),
         "expert",

time: 330 us -> 338 us (1.024)
  waiting for transfers between devices: 37.3 us -> 105 us
  blocking collectives: 97.3 us -> 32.2 us
  starting transfers between devices: 34.9 us -> 43 us
  local copies, waits for them, and re-layouts: 55.8 us -> 50.6 us
    all_to_all x1 -> x0, blocking collectives: 39.1 us -> none  [shards(): lax.all_to_all(outgoing, 'expert', split_axis=0, concat_axis=0, tiled=True)]
    all_to_all x0 -> x1, waiting for transfers between devices: none -> 31 us  [shards(): lax.all_to_all(outgoing, 'expert', split_axis=0, concat_axis=0, tiled=True)]
    all_gather x2 -> x0, blocking collectives: 28.3 us -> none  [the longest x1 14.8 us: shards(): lax.all_gather(jnp.concatenate([normed, route_row], axis=0)[None], 'dp',...]
    all_gather x2, waiting for transfers between devices: 37.2 us -> 61.5 us  [the longest x1 36.5 us: shards(): both_pieces = lax.all_gather(both_acts, 'dp', axis=1, tiled=True)]
    all_to_all x1, waiting for transfers between devices: 0.01 us -> 13 us  [shards(): lax.all_to_all(expert_out.reshape(members, groups * capacity, col_width),...]
    all_to_all x0 -> x1, starting transfers between devices: none -> 8.05 us  [shards(): lax.all_to_all(outgoing, 'expert', split_axis=0, concat_axis=0, tiled=True)]
    all_gather x2 -> x0, local copies, waits for them, and re-layouts: 4.59 us -> none  [the longest x1 4.49 us: shards(): lax.all_gather(arrived.reshape(members, 1, capacity, D), 'dp', axis=1, ti...]
    slice x0 -> x2, local copies, waits for them, and re-layouts: none -> 3.75 us  [the longest x1 2.57 us: shards(): expert_rows = group_all[:, :slots_in].reshape(-1, D)]
  transfers between devices with their start and end apart: 7 -> 8, of which waited for: 2 -> 4; matrix products, arithmetic and copies ran while one was open for 15% -> 12% of each run, Pallas kernels for 19% -> 18%
where the time goes in v8:
time: 338 us; the launch traced here: 337 us
  waiting for transfers between devices  105 us (31%)
  Pallas kernels  61.5 us (18%)
  local copies, waits for them, and re-layouts  50.6 us (15%)
  starting transfers between devices  43 us (13%)
  blocking collectives  32.2 us (10%)
  matrix products  18.9 us (6%)
  between operations  16.3 us (5%)
  other arithmetic  9.1 us (3%)
    pallas_call x1, Pallas kernels, expert_gather(): pl.pallas_call(partial(gather_kernel, nx, nz), out_shape=jax.ShapeDtypeSt...  61.5 us
    all_gather x1, waiting for transfers between devices, shards(): both_pieces = lax.all_gather(both_acts, 'dp', axis=1, tiled=True)  36.5 us
    all_to_all x1, waiting for transfers between devices, shards(): lax.all_to_all(outgoing, 'expert', split_axis=0, concat_axis=0, tiled=True)  31 us
    all_gather x1, waiting for transfers between devices, shards(): group_all = lax.all_gather(combined[None], 'dp', axis=0, tiled=True)  25 us
    unnamed x1, blocking collectives  21.9 us
    all_to_all x1, starting transfers between devices, shards(): lax.all_to_all(expert_out.reshape(members, groups * capacity, col_width),...  15.5 us
    all_to_all x1, waiting for transfers between devices, shards(): lax.all_to_all(expert_out.reshape(members, groups * capacity, col_width),...  13 us
    gather x4, local copies, waits for them, and re-layouts, shards(): jnp.take_along_axis(group_logits, group_routes.reshape(-1, TOPK), axis=1)  11 us
  transfers between devices with their start and end apart: 8, of which 4 were waited for; matrix products, arithmetic and copies ran while one was open for 12% of the time, Pallas kernels for 18%

profile of v8, /device:TPU:1, one launch (start us, length us, event | category | flops | bytes accessed | tf_op | source)
XLA Modules:
  0.0 337.1 jit_solution(11512275204503869182)
XLA Ops:
  8.8 1.7 fusion.98
  10.5 0.9 convert_convert_fusion
  11.3 1.6 fusion.99
  14.4 1.1 fusion.9
  16.1 0.9 copy.69
  17.1 10.2 %all-to-all-start = ((bf16[17,16,512]{2,0,1:T(8,128)(2,1)}), bf16[17,16,512]{2,0,1:T(8,128)(2,1)S(1)}, u32[]{:S(2)}, u32[]{:S(2)}) async-start(bf16[17,16,512]{2,0,1:T(8,128)(2,1)} %copy.69), calls=%async_computation | async-start | bytes 786432 | tf_op jit(solution)/shard_map/all_to_all | solution.py:266
  29.7 61.5 %shard_map.203 = bf16[16,4,232,128]{3,2,1,0:T(8,128)(2,1)} custom-call(bf16[232,128]{1,0:T(8,128)(2,1)} %pad_bitcast_fusion.shard_ref), custom_call_target="tpu_custom_call" | custom-call | tf_op jit(solution)/shard_map/pallas_call | solution.py:137
  91.2 2.3 copy.66
  94.2 1.8 copy-done.1
  96.0 0.8 reshape.479
  96.8 1.7 copy.72
  98.5 1.5 reshape.480
  100.0 0.7 copy.94
  102.0 1.4 fusion.3
  103.4 21.9 %fusion = bf16[24,2048]{1,0:T(8,128)(2,1)S(1)} fusion(bf16[136,2048]{1,0:T(8,128)(2,1)S(1)} %fusion.3), kind=kCustom, calls=%all-reduce-scatter | all-reduce-scatter fusion | flops 393217 | bytes 657408
  125.3 1.9 collective-permute-start
  127.3 2.6 collective-permute-start.1
  129.8 4.4 %collective-permute-start.2 = (bf16[1,2048]{1,0:T(2,128)(2,1)S(1)}, bf16[1,2048]{1,0:T(2,128)(2,1)S(1)}, u32[]{:S(2)}, u32[]{:S(2)}) collective-permute-start(bf16[1,2048]{1,0:T(2,128)(2,1)S(1)} %slice.111), channel_id=1, source_target_pairs={{0,192},{64,256},{128,320},{192,384},{256,448},{1,193},{65,257},{1... | collective-permute-start | bytes 12296
  134.3 1.3 dynamic-slice.4
  137.6 1.3 copy.75
  139.0 8.1 %all-to-all-start.1 = ((bf16[64,2,2048]{2,1,0:T(2,128)(2,1)}), bf16[64,2,2048]{2,1,0:T(2,128)(2,1)S(1)}, u32[]{:S(2)}, u32[]{:S(2)}) async-start(bf16[64,2,2048]{2,1,0:T(2,128)(2,1)} %copy.75), calls=%async_computation.1 | async-start | bytes 1048576 | tf_op jit(solution)/shard_map/all_to_all | solution.py:292
  147.3 31.0 %all-to-all-done.1 = bf16[64,2,2048]{2,1,0:T(2,128)(2,1)S(1)} async-done(((bf16[64,2,2048]{2,1,0:T(2,128)(2,1)}), bf16[64,2,2048]{2,1,0:T(2,128)(2,1)S(1)}, u32[]{:S(2)}, u32[]{:S(2)}) %all-to-all-start.1) | async-done | bytes 524320 | tf_op jit(solution)/shard_map/all_to_all | solution.py:292
  178.5 0.9 fusion.36
  179.6 2.9 fusion.97
  182.5 3.0 reshape_reshape.10
  185.5 3.1 reshape_reshape.11
  188.6 25.0 %all-gather.7.cloned.1.call-done = bf16[8,146,2048]{2,1,0:T(8,128)(2,1)} async-done(((bf16[1,146,2048]{2,1,0:T(8,128)(2,1)}), bf16[8,146,2048]{2,1,0:T(8,128)(2,1)}) %all-gather.7.cloned.1.call-update) | async-done | bytes 4784144 | tf_op jit(solution)/shard_map/all_gather | solution.py:295
  213.6 1.2 slice.101
  215.3 1.5 fusion.13
  217.0 2.6 slice.100
  219.6 1.6 fusion.33
  221.1 1.6 fusion.8
  222.8 0.9 pad_maximum_fusion
  223.8 0.9 reshape_reshape.12
  224.7 36.5 %all-gather.5.cloned.1.call-done = bf16[1160,1408]{0,1:T(8,128)(2,1)} async-done(((bf16[1160,176]{0,1:T(8,128)(2,1)}), bf16[1160,1408]{0,1:T(8,128)(2,1)}) %all-gather.5.cloned.1.call-update) | async-done | bytes 3266576 | tf_op jit(solution)/shard_map/all_gather | solution.py:320
  261.2 3.6 %fusion.4 = bf16[1024,256]{1,0:T(8,128)(2,1)} fusion(bf16[1160,1408]{0,1:T(8,128)(2,1)} %all-gather.5.cloned.1.call-done, bf16[1,1408,256]{2,1,0:T(8,128)(2,1)S(1)} %copy-done), kind=kOutput, calls=%fused_computation.7 | convolution fusion | flops 738459648 | bytes 4128768 | tf_op jit(solution)/shard_map/dot_general | solution.py:323
  264.9 1.2 reshape.487
  266.2 1.1 copy.89
  267.3 15.5 %all-to-all-start.2 = ((bf16[64,16,256]{2,1,0:T(8,128)(2,1)}), bf16[64,16,256]{2,1,0:T(8,128)(2,1)S(1)}, u32[]{:S(2)}, u32[]{:S(2)}) async-start(bf16[64,16,256]{2,1,0:T(8,128)(2,1)} %copy.89), calls=%async_computation.2 | async-start | bytes 1048576 | tf_op jit(solution)/shard_map/all_to_all | solution.py:328
  282.8 0.7 slice_convert_fusion
  283.7 2.0 select_reduce_fusion
  286.1 0.8 fusion.95
  287.5 1.3 fusion.41
  288.7 10.7 %gather_fusion.1 = f32[816]{0:T(1024)S(1)} fusion(f32[136,64]{0,1:T(8,128)S(1)} %fusion.41, s32[816]{0:T(1024)S(1)} %reshape.504), kind=kCustom, calls=%fused_computation.1 | custom fusion | bytes 13056 | tf_op jit(solution)/shard_map/jit(take_along_axis)/gather | solution.py:342
  300.0 13.0 %all-to-all-done.2 = bf16[64,16,256]{2,1,0:T(8,128)(2,1)S(1)} async-done(((bf16[64,16,256]{2,1,0:T(8,128)(2,1)}), bf16[64,16,256]{2,1,0:T(8,128)(2,1)S(1)}, u32[]{:S(2)}, u32[]{:S(2)}) %all-to-all-start.2) | async-done | bytes 524320 | tf_op jit(solution)/shard_map/all_to_all | solution.py:328
  312.9 3.4 %gather_fusion = bf16[816,256]{1,0:T(8,128)(2,1)S(1)} fusion(bf16[1024,256]{1,0:T(8,128)(2,1)S(1)} %bitcast.134, s32[1024]{0:T(1024)S(1)} %pad_clamp_fusion), kind=kCustom, calls=%fused_computation | custom fusion | bytes 838848 | tf_op jit(solution)/shard_map/jit(_take)/gather | solution.py:339
  317.0 1.5 fusion.16
  318.6 10.2 %all_to_all.37 = bf16[8,17,256]{2,1,0:T(8,128)(2,1)S(1)} all-to-all(bf16[8,17,256]{2,1,0:T(8,128)(2,1)S(1)} %convert_element_type.222), channel_id=1, replica_groups=mesh['dp'=8,'expert'=64] {'dp'}, dimensions={0} | all-to-all | bytes 139264 | tf_op jit(solution)/shard_map/all_to_all | solution.py:348
  (126 shorter events, 13.5 us)
Async XLA Ops:
  7.2 254.0 %copy-start = (bf16[1,1408,256]{2,1,0:T(8,128)(2,1)S(1)}, bf16[1,1408,256]{2,1,0:T(8,128)(2,1)}, u32[]{:S(2)}) copy-start(bf16[1,1408,256]{2,1,0:T(8,128)(2,1)} %param.36) | copy-start | bytes 2162692
  7.2 8.5 %copy-start.3 = (bf16[1,1024,576]{1,2,0:T(8,128)(2,1)S(1)}, bf16[1,1024,576]{1,2,0:T(8,128)(2,1)}, u32[]{:S(2)}) copy-start(bf16[1,1024,576]{1,2,0:T(8,128)(2,1)} %param.27) | copy-start | bytes 3538948
  7.2 8.5 %copy-start.12 = (f32[16]{0:T(128)S(1)}, f32[16]{0:T(128)}, u32[]{:S(2)}) copy-start(f32[16]{0:T(128)} %param.28) | copy-start | bytes 196
  8.7 18.6 %copy-start.14 = (bf16[2,8,128]{2,1,0:T(8,128)(2,1)S(1)}, bf16[2,8,128]{2,1,0:T(8,128)(2,1)}, u32[]{:S(2)}) copy-start(bf16[2,8,128]{2,1,0:T(8,128)(2,1)} %param.29) | copy-start | bytes 12292
  8.7 18.6 %copy-start.7 = (bf16[2,2,2048]{2,1,0:T(2,128)(2,1)S(1)}, bf16[2,2,2048]{2,1,0:T(2,128)(2,1)}, u32[]{:S(2)}) copy-start(bf16[2,2,2048]{2,1,0:T(2,128)(2,1)} %param.30) | copy-start | bytes 49156
  8.7 18.6 %copy-start.5 = (bf16[32,176]{1,0:T(8,128)(2,1)S(1)}, bf16[32,176]{1,0:T(8,128)(2,1)}, u32[]{:S(2)}) copy-start(bf16[32,176]{1,0:T(8,128)(2,1)} %param.37) | copy-start | bytes 33796
  8.7 18.7 %copy-start.6 = (bf16[32,176]{1,0:T(8,128)(2,1)S(1)}, bf16[32,176]{1,0:T(8,128)(2,1)}, u32[]{:S(2)}) copy-start(bf16[32,176]{1,0:T(8,128)(2,1)} %param.38) | copy-start | bytes 33796
  8.7 18.8 %copy-start.9 = (bf16[22,256]{1,0:T(8,128)(2,1)S(1)}, bf16[22,256]{1,0:T(8,128)(2,1)}, u32[]{:S(2)}) copy-start(bf16[22,256]{1,0:T(8,128)(2,1)} %param.39) | copy-start | bytes 33796
  8.8 18.8 %copy-start.11 = (bf16[2048,1]{0,1:T(2,128)(2,1)S(1)}, bf16[2048,1]{0,1:T(2,128)(2,1)}, u32[]{:S(2)}) copy-start(bf16[2048,1]{0,1:T(2,128)(2,1)} %param.32) | copy-start | bytes 12292
  17.1 84.7 %all-to-all-start = ((bf16[17,16,512]{2,0,1:T(8,128)(2,1)}), bf16[17,16,512]{2,0,1:T(8,128)(2,1)S(1)}, u32[]{:S(2)}, u32[]{:S(2)}) async-start(bf16[17,16,512]{2,0,1:T(8,128)(2,1)} %copy.69), calls=%async_computation | async-start | bytes 786432 | tf_op jit(solution)/shard_map/all_to_all | solution.py:266
  94.1 1.9 copy-start.1
  96.0 4.8 %copy-start.8 = (s32[17,6]{0,1:T(8,128)S(1)}, s32[17,6]{0,1:T(8,128)}, u32[]{:S(2)}) copy-start(s32[17,6]{0,1:T(8,128)} %param.33) | copy-start | bytes 1228
  98.5 35.8 %copy-start.13 = (bf16[2048]{0:T(1024)(128)(2,1)S(1)}, bf16[2048]{0:T(1024)(128)(2,1)}, u32[]{:S(2)}) copy-start(bf16[2048]{0:T(1024)(128)(2,1)} %param.31) | copy-start | bytes 12292
  98.5 38.4 %copy-start.4 = (bf16[16,2048]{1,0:T(8,128)(2,1)S(1)}, bf16[16,2048]{1,0:T(8,128)(2,1)}, u32[]{:S(2)}) copy-start(bf16[16,2048]{1,0:T(8,128)(2,1)} %param.22) | copy-start | bytes 196612
  98.5 38.4 %copy-start.10 = (bf16[1,2048]{1,0:T(2,128)(2,1)S(1)}, bf16[1,2048]{1,0:T(2,128)(2,1)}, u32[]{:S(2)}) copy-start(bf16[1,2048]{1,0:T(2,128)(2,1)} %param.25) | copy-start | bytes 12292
  125.3 10.9 %collective-permute-start = (bf16[24,2048]{1,0:T(8,128)(2,1)S(1)}, bf16[24,2048]{1,0:T(8,128)(2,1)S(1)}, u32[]{:S(2)}, u32[]{:S(2)}) collective-permute-start(bf16[24,2048]{1,0:T(8,128)(2,1)S(1)} %fusion), channel_id=1, source_target_pairs={{0,64},{64,128},{128,192},{192,256},{256,320},{320,384},{384,448},... | collective-permute-start | bytes 294920
  127.3 9.0 %collective-permute-start.1 = (bf16[24,2048]{1,0:T(8,128)(2,1)S(1)}, bf16[24,2048]{1,0:T(8,128)(2,1)S(1)}, u32[]{:S(2)}, u32[]{:S(2)}) collective-permute-start(bf16[24,2048]{1,0:T(8,128)(2,1)S(1)} %fusion), channel_id=1, source_target_pairs={{0,128},{64,192},{128,256},{192,320},{256,384},{320,448},{1,129},{... | collective-permute-start | bytes 294920
  129.8 6.4 %collective-permute-start.2 = (bf16[1,2048]{1,0:T(2,128)(2,1)S(1)}, bf16[1,2048]{1,0:T(2,128)(2,1)S(1)}, u32[]{:S(2)}, u32[]{:S(2)}) collective-permute-start(bf16[1,2048]{1,0:T(2,128)(2,1)S(1)} %slice.111), channel_id=1, source_target_pairs={{0,192},{64,256},{128,320},{192,384},{256,448},{1,193},{65,257},{1... | collective-permute-start | bytes 12296
  139.0 39.3 %all-to-all-start.1 = ((bf16[64,2,2048]{2,1,0:T(2,128)(2,1)}), bf16[64,2,2048]{2,1,0:T(2,128)(2,1)S(1)}, u32[]{:S(2)}, u32[]{:S(2)}) async-start(bf16[64,2,2048]{2,1,0:T(2,128)(2,1)} %copy.75), calls=%async_computation.1 | async-start | bytes 1048576 | tf_op jit(solution)/shard_map/all_to_all | solution.py:292
  147.0 66.5 %all-gather.7.cloned.1.call-start = ((), (), s32[]{:S(2)}) async-start(), calls=%async_computation.5 | async-start | bytes 5603328 | tf_op jit(solution)/shard_map/all_gather | solution.py:295
  179.4 81.8 %all-gather.5.cloned.1.call-start = ((), (), s32[]{:S(2)}) async-start(), calls=%async_computation.4 | async-start | bytes 4055040 | tf_op jit(solution)/shard_map/all_gather | solution.py:320
  217.0 2.6 copy-start.15
  219.5 1.6 copy-start.16
  221.1 2.7 copy-start.2
  267.3 45.6 %all-to-all-start.2 = ((bf16[64,16,256]{2,1,0:T(8,128)(2,1)}), bf16[64,16,256]{2,1,0:T(8,128)(2,1)S(1)}, u32[]{:S(2)}, u32[]{:S(2)}) async-start(bf16[64,16,256]{2,1,0:T(8,128)(2,1)} %copy.89), calls=%async_computation.2 | async-start | bytes 1048576 | tf_op jit(solution)/shard_map/all_to_all | solution.py:328
Sparse Core Ops, SparseCore 0:
  179.5 34.0 all-gather.6
  223.8 37.4 all-gather.4

commit v9 on v6

--- a/solution.py
+++ b/solution.py
@@ -271,9 +271,13 @@
     head_partial = jnp.einsum(
         "thv,hvd->td", head_values, out_full, preferred_element_type=jnp.float32
     )
-    attn_out = lax.psum_scatter(
-        head_partial.astype(jnp.bfloat16), "dp", scatter_dimension=0, tiled=True
-    ).astype(jnp.float32)
+    aligned = 32
+    padded_partial = jnp.pad(
+        head_partial.astype(jnp.bfloat16).reshape(groups, rows_dev, D),
+        ((0, 0), (0, aligned - rows_dev), (0, 0)),
+    ).reshape(groups * aligned, D)
+    attn_out = lax.psum_scatter(padded_partial, "dp", scatter_dimension=0, tiled=True)
+    attn_out = attn_out[:rows_dev].astype(jnp.float32)
     resid = jnp.concatenate([pre_resid, dec_resid], axis=0)
     hidden = (resid.astype(jnp.float32) + attn_out).astype(jnp.bfloat16)
     hidden_up = lax.optimization_barrier(hidden).astype(jnp.float32)

time: 330 us -> 342 us (1.036)
  waiting for transfers between devices: 37.3 us -> 81.2 us
  blocking collectives: 97.3 us -> 77.4 us
  starting transfers between devices: 34.9 us -> 25.8 us
    reduce_scatter x0 -> x1, waiting for transfers between devices: none -> 36.1 us  [shards(): lax.psum_scatter(padded_partial, 'dp', scatter_dimension=0, tiled=True)]
    unnamed x1 -> x0, blocking collectives: 21.8 us -> none
    unnamed x3 -> x0, starting transfers between devices: 9.16 us -> none
    all_gather x1, waiting for transfers between devices: 30.7 us -> 38.5 us  [shards(): lax.all_gather(arrived.reshape(members, 1, capacity, D), 'dp', axis=1, ti...]
    unnamed x54 -> x51, local copies, waits for them, and re-layouts: 7.51 us -> 5.96 us
  transfers between devices with their start and end apart: 7 -> 5, of which waited for: 2 -> 3; matrix products, arithmetic and copies ran while one was open for 15% -> 13% of each run, Pallas kernels for 19% -> 18%
where the time goes in v9:
time: 342 us; the launch traced here: 340 us
  waiting for transfers between devices  81.2 us (24%)
  blocking collectives  77.4 us (23%)
  Pallas kernels  61.4 us (18%)
  local copies, waits for them, and re-layouts  53.5 us (16%)
  starting transfers between devices  25.8 us (8%)
  matrix products  17.4 us (5%)
  between operations  15.3 us (4%)
  other arithmetic  8.46 us (2%)
    pallas_call x1, Pallas kernels, expert_gather(): pl.pallas_call(partial(gather_kernel, nx, nz), out_shape=jax.ShapeDtypeSt...  61.4 us
    all_to_all x1, blocking collectives, shards(): lax.all_to_all(outgoing, 'expert', split_axis=0, concat_axis=0, tiled=True)  41 us
    all_gather x1, waiting for transfers between devices, shards(): lax.all_gather(arrived.reshape(members, 1, capacity, D), 'dp', axis=1, ti...  38.5 us
    reduce_scatter x1, waiting for transfers between devices, shards(): lax.psum_scatter(padded_partial, 'dp', scatter_dimension=0, tiled=True)  36.1 us
    all_to_all x1, starting transfers between devices, shards(): lax.all_to_all(expert_out.reshape(members, groups * capacity, col_width),...  15.3 us
    all_gather x1, blocking collectives, shards(): lax.all_gather(jnp.concatenate([normed, route_row], axis=0)[None], 'dp',...  14.8 us
    all_gather x1, blocking collectives, shards(): shared_piece = lax.all_gather(shared_act, 'dp', axis=1, tiled=True)  13.5 us
    gather x4, local copies, waits for them, and re-layouts, shards(): jnp.take_along_axis(group_logits, group_routes.reshape(-1, TOPK), axis=1)  11 us
  transfers between devices with their start and end apart: 5, of which 3 were waited for; matrix products, arithmetic and copies ran while one was open for 13% of the time, Pallas kernels for 18%

profile of v9, /device:TPU:1, one launch (start us, length us, event | category | flops | bytes accessed | tf_op | source)
XLA Modules:
  0.0 340.5 jit_solution(13206415509760332040)
XLA Ops:
  8.0 0.7 slice_convert_fusion.1
  8.7 1.7 fusion.92
  10.4 0.9 convert_convert_fusion
  11.3 1.6 fusion.93
  12.9 0.7 broadcast_maximum_fusion
  13.7 0.7 exponential_add_fusion
  14.3 1.1 fusion.2
  16.1 0.9 copy.73
  17.0 10.2 %all-to-all-start = ((bf16[17,16,512]{2,0,1:T(8,128)(2,1)}), bf16[17,16,512]{2,0,1:T(8,128)(2,1)S(1)}, u32[]{:S(2)}, u32[]{:S(2)}) async-start(bf16[17,16,512]{2,0,1:T(8,128)(2,1)} %copy.73), calls=%async_computation | async-start | bytes 786432 | tf_op jit(solution)/shard_map/all_to_all | solution.py:266
  29.6 61.4 %shard_map.203 = bf16[16,4,232,128]{3,2,1,0:T(8,128)(2,1)} custom-call(bf16[232,128]{1,0:T(8,128)(2,1)} %pad_bitcast_fusion.shard_ref), custom_call_target="tpu_custom_call" | custom-call | tf_op jit(solution)/shard_map/pallas_call | solution.py:137
  91.0 2.3 copy.70
  93.9 1.8 copy-done.1
  95.8 0.8 reshape.482
  96.6 0.7 copy.76
  97.8 1.0 slice_bitcast_fusion.2
  99.8 1.1 pad.13
  102.0 36.1 %reduce-scatter.2.cloned.1.call-done = bf16[32,2048]{1,0:T(8,128)(2,1)} async-done(((bf16[256,2048]{1,0:T(8,128)(2,1)}), bf16[32,2048]{1,0:T(8,128)(2,1)}) %reduce-scatter.2.cloned.1.call-update) | async-done | bytes 131088 | tf_op jit(solution)/shard_map/reduce_scatter | solution.py:279
  138.1 0.9 add_convert_fusion
  140.2 41.0 %all_to_all.37 = bf16[64,2,2048]{2,1,0:T(2,128)(2,1)S(1)} all-to-all(bf16[64,2,2048]{2,1,0:T(2,128)(2,1)S(1)} %copy.91), channel_id=1, replica_groups=mesh['dp'=8,'expert'=64] {'expert'}, dimensions={0} | all-to-all | bytes 1048576 | tf_op jit(solution)/shard_map/all_to_all | solution.py:305
  181.2 1.0 copy.92
  182.4 38.5 %all-gather.9.cloned.1.call-done = bf16[64,16,2048]{2,0,1:T(8,128)(2,1)} async-done(((bf16[64,2,2048]{2,0,1:T(8,128)(2,1)}), bf16[64,16,2048]{2,0,1:T(8,128)(2,1)}) %all-gather.9.cloned.1.call-update) | async-done | bytes 4194320 | tf_op jit(solution)/shard_map/all_gather | solution.py:312
  220.9 4.5 %copy.93 = bf16[64,16,2048]{2,1,0:T(8,128)(2,1)S(1)} copy(bf16[64,16,2048]{2,0,1:T(8,128)(2,1)} %all-gather.9.cloned.1.call-done) | data formatting | bytes 8388608 | tf_op jit(solution)/shard_map/all_gather | solution.py:312
  225.4 1.5 fusion.26
  227.0 2.4 fusion.1
  229.6 2.9 fusion.91
  232.4 3.0 reshape_reshape.10
  235.5 3.1 reshape_reshape.11
  238.7 2.7 reshape_reshape.12
  241.4 14.8 %all-gather.2 = bf16[8,18,2048]{2,1,0:T(8,128)(2,1)S(1)} all-gather(bf16[1,18,2048]{2,1,0:T(8,128)(2,1)S(1)} %fusion.46), channel_id=2, replica_groups=mesh['dp'=8,'expert'=64] {'dp'}, dimensions={0}, use_global_device_ids=true | all-gather | bytes 663552 | tf_op jit(solution)/shard_map/all_gather | solution.py:291
  256.3 2.0 select_reduce_fusion
  258.4 6.5 %all-gather.7.cloned.1.call-done = bf16[1024,1408]{0,1:T(8,128)(2,1)} async-done(((bf16[1024,176]{0,1:T(8,128)(2,1)}), bf16[1024,1408]{0,1:T(8,128)(2,1)}) %all-gather.7.cloned.1.call-update) | async-done | bytes 2883600 | tf_op jit(solution)/shard_map/all_gather | solution.py:326
  264.9 3.6 %convolution_convert_fusion = bf16[1024,256]{1,0:T(8,128)(2,1)} fusion(bf16[1024,1408]{0,1:T(8,128)(2,1)} %all-gather.7.cloned.1.call-done, bf16[1,1408,256]{2,1,0:T(8,128)(2,1)S(1)} %copy-done), kind=kOutput, calls=%fused_computation.5 | convolution fusion | flops 738459648 | bytes 4128768 | tf_op jit(solution)/shard_map/dot_general | solution.py:328
  268.6 15.3 %all-to-all-start.2 = ((bf16[64,16,256]{2,1,0:T(8,128)(2,1)}), bf16[64,16,256]{2,1,0:T(8,128)(2,1)S(1)}, u32[]{:S(2)}, u32[]{:S(2)}) async-start(bf16[64,16,256]{2,1,0:T(8,128)(2,1)} %bitcast.157), calls=%async_computation.3 | async-start | bytes 1048576 | tf_op jit(solution)/shard_map/all_to_all | solution.py:332
  283.9 0.7 sub.97
  284.6 0.7 sub.100
  285.4 0.7 reshape.496
  286.1 1.3 reshape.487
  287.7 1.5 fusion.10
  289.3 13.5 %all-gather.3 = bf16[8,176,136]{1,2,0:T(8,128)(2,1)S(1)} all-gather(bf16[1,176,136]{1,2,0:T(8,128)(2,1)S(1)} %fusion.10), channel_id=1, replica_groups=mesh['dp'=8,'expert'=64] {'dp'}, dimensions={0}, use_global_device_ids=true | all-gather | bytes 430848 | tf_op jit(solution)/shard_map/all_gather | solution.py:327
  302.9 1.2 reshape.521
  304.2 1.0 copy.87
  305.1 0.8 fusion.89
  306.2 1.0 fusion.51
  307.4 1.3 fusion.32
  308.6 10.7 %gather_fusion.1 = f32[816]{0:T(1024)S(1)} fusion(f32[136,64]{0,1:T(8,128)S(1)} %fusion.32, s32[816]{0:T(1024)S(1)} %reshape.508), kind=kCustom, calls=%fused_computation.1 | custom fusion | bytes 13056 | tf_op jit(solution)/shard_map/jit(take_along_axis)/gather | solution.py:346
  319.9 3.4 %gather_fusion = bf16[816,256]{1,0:T(8,128)(2,1)S(1)} fusion(bf16[1024,256]{1,0:T(8,128)(2,1)S(1)} %bitcast.139, s32[1024]{0:T(1024)S(1)} %pad_clamp_fusion), kind=kCustom, calls=%fused_computation | custom fusion | bytes 838848 | tf_op jit(solution)/shard_map/jit(_take)/gather | solution.py:343
  324.4 8.1 %all_to_all.38 = bf16[8,17,256]{2,1,0:T(8,128)(2,1)S(1)} all-to-all(bf16[8,17,256]{2,1,0:T(8,128)(2,1)S(1)} %convert_element_type.224), channel_id=1, replica_groups=mesh['dp'=8,'expert'=64] {'dp'}, dimensions={0} | all-to-all | bytes 139264 | tf_op jit(solution)/shard_map/all_to_all | solution.py:352
  332.7 0.6 slice.99
  (122 shorter events, 11.2 us)
Async XLA Ops:
  7.2 257.8 %copy-start = (bf16[1,1408,256]{2,1,0:T(8,128)(2,1)S(1)}, bf16[1,1408,256]{2,1,0:T(8,128)(2,1)}, u32[]{:S(2)}) copy-start(bf16[1,1408,256]{2,1,0:T(8,128)(2,1)} %param.36) | copy-start | bytes 2162692
  7.2 8.5 %copy-start.5 = (bf16[1,1024,576]{1,2,0:T(8,128)(2,1)S(1)}, bf16[1,1024,576]{1,2,0:T(8,128)(2,1)}, u32[]{:S(2)}) copy-start(bf16[1,1024,576]{1,2,0:T(8,128)(2,1)} %param.27) | copy-start | bytes 3538948
  7.2 8.4 %copy-start.14 = (f32[16]{0:T(128)S(1)}, f32[16]{0:T(128)}, u32[]{:S(2)}) copy-start(f32[16]{0:T(128)} %param.28) | copy-start | bytes 196
  7.2 20.0 %copy-start.16 = (bf16[2,8,128]{2,1,0:T(8,128)(2,1)S(1)}, bf16[2,8,128]{2,1,0:T(8,128)(2,1)}, u32[]{:S(2)}) copy-start(bf16[2,8,128]{2,1,0:T(8,128)(2,1)} %param.29) | copy-start | bytes 12292
  7.2 20.0 %copy-start.9 = (bf16[2,2,2048]{2,1,0:T(2,128)(2,1)S(1)}, bf16[2,2,2048]{2,1,0:T(2,128)(2,1)}, u32[]{:S(2)}) copy-start(bf16[2,2,2048]{2,1,0:T(2,128)(2,1)} %param.30) | copy-start | bytes 49156
  7.2 20.1 %copy-start.7 = (bf16[32,176]{1,0:T(8,128)(2,1)S(1)}, bf16[32,176]{1,0:T(8,128)(2,1)}, u32[]{:S(2)}) copy-start(bf16[32,176]{1,0:T(8,128)(2,1)} %param.37) | copy-start | bytes 33796
  7.2 20.2 %copy-start.8 = (bf16[32,176]{1,0:T(8,128)(2,1)S(1)}, bf16[32,176]{1,0:T(8,128)(2,1)}, u32[]{:S(2)}) copy-start(bf16[32,176]{1,0:T(8,128)(2,1)} %param.38) | copy-start | bytes 33796
  7.2 20.3 %copy-start.11 = (bf16[22,256]{1,0:T(8,128)(2,1)S(1)}, bf16[22,256]{1,0:T(8,128)(2,1)}, u32[]{:S(2)}) copy-start(bf16[22,256]{1,0:T(8,128)(2,1)} %param.39) | copy-start | bytes 33796
  7.3 20.3 %copy-start.13 = (bf16[2048,1]{0,1:T(2,128)(2,1)S(1)}, bf16[2048,1]{0,1:T(2,128)(2,1)}, u32[]{:S(2)}) copy-start(bf16[2048,1]{0,1:T(2,128)(2,1)} %param.32) | copy-start | bytes 12292
  17.0 81.8 %all-to-all-start = ((bf16[17,16,512]{2,0,1:T(8,128)(2,1)}), bf16[17,16,512]{2,0,1:T(8,128)(2,1)S(1)}, u32[]{:S(2)}, u32[]{:S(2)}) async-start(bf16[17,16,512]{2,0,1:T(8,128)(2,1)} %copy.73), calls=%async_computation | async-start | bytes 786432 | tf_op jit(solution)/shard_map/all_to_all | solution.py:266
  27.2 110.8 %reduce-scatter.2.cloned.1.call-start = ((), (), s32[]{:S(2)}) async-start(), calls=%async_computation.5 | async-start | bytes 1179648 | tf_op jit(solution)/shard_map/reduce_scatter | solution.py:279
  93.9 1.8 copy-start.1
  98.7 2.2 copy-start.15
  98.7 2.2 copy-start.10
  98.8 39.3 %copy-start.6 = (bf16[16,2048]{1,0:T(8,128)(2,1)S(1)}, bf16[16,2048]{1,0:T(8,128)(2,1)}, u32[]{:S(2)}) copy-start(bf16[16,2048]{1,0:T(8,128)(2,1)} %param.22) | copy-start | bytes 196612
  98.8 39.3 %copy-start.12 = (bf16[1,2048]{1,0:T(2,128)(2,1)S(1)}, bf16[1,2048]{1,0:T(2,128)(2,1)}, u32[]{:S(2)}) copy-start(bf16[1,2048]{1,0:T(2,128)(2,1)} %param.25) | copy-start | bytes 12292
  100.9 120.0 %all-gather.9.cloned.1.call-start = ((), (), s32[]{:S(2)}) async-start(), calls=%async_computation.7 | async-start | bytes 4718592 | tf_op jit(solution)/shard_map/all_gather | solution.py:312
  182.2 43.2 %copy-start.17 = (bf16[1,2048,176]{1,2,0:T(8,128)(2,1)S(1)}, bf16[1,2048,176]{1,2,0:T(8,128)(2,1)}, u32[]{:S(2)}) copy-start(bf16[1,2048,176]{1,2,0:T(8,128)(2,1)} %param.34) | copy-start | bytes 2162692
  182.2 82.7 %all-gather.7.cloned.1.call-start = ((), (), s32[]{:S(2)}) async-start(), calls=%async_computation.6 | async-start | bytes 3244032 | tf_op jit(solution)/shard_map/all_gather | solution.py:326
  225.4 1.6 copy-start.18
  256.2 12.4 %copy-start.2 = (bf16[8,18,2048]{2,1,0:T(8,128)(2,1)}, bf16[8,18,2048]{2,1,0:T(8,128)(2,1)S(1)}, u32[]{:S(2)}) copy-start(bf16[8,18,2048]{2,1,0:T(8,128)(2,1)S(1)} %all-gather.2) | copy-start | bytes 1769476
  268.6 51.3 %all-to-all-start.2 = ((bf16[64,16,256]{2,1,0:T(8,128)(2,1)}), bf16[64,16,256]{2,1,0:T(8,128)(2,1)S(1)}, u32[]{:S(2)}, u32[]{:S(2)}) async-start(bf16[64,16,256]{2,1,0:T(8,128)(2,1)} %bitcast.157), calls=%async_computation.3 | async-start | bytes 1048576 | tf_op jit(solution)/shard_map/all_to_all | solution.py:332
  319.3 4.7 %copy-start.3 = (bf16[1408,256]{1,0:T(8,128)(2,1)S(1)}, bf16[1408,256]{1,0:T(8,128)(2,1)}, u32[]{:S(2)}) copy-start(bf16[1408,256]{1,0:T(8,128)(2,1)} %reshape_reshape.12) | copy-start | bytes 2162692
  319.3 4.7 %copy-start.4 = (bf16[1408,136]{0,1:T(8,128)(2,1)S(1)}, bf16[1408,136]{0,1:T(8,128)(2,1)}, u32[]{:S(2)}) copy-start(bf16[1408,136]{0,1:T(8,128)(2,1)} %reshape.521) | copy-start | bytes 1148932
Sparse Core Ops, SparseCore 0:
  101.0 37.0 reduce-scatter.1
  182.3 38.5 all-gather.8
  229.5 35.4 all-gather.6

commit v10 on v6

--- a/solution.py
+++ b/solution.py
@@ -284,15 +284,6 @@
     capacity = max(2, (rows_dev * TOPK + members - 1) // members)
     route_row = routes.astype(jnp.bfloat16).reshape(1, rows_dev * TOPK)
     route_row = jnp.pad(route_row, ((0, 0), (0, D - rows_dev * TOPK)))
-    group_both = lax.all_gather(
-        jnp.concatenate([normed, route_row], axis=0)[None], "dp", axis=0, tiled=True
-    )
-    group_tokens = group_both[:, :rows_dev].reshape(groups * rows_dev, D)
-    group_routes = (
-        group_both[:, rows_dev, : rows_dev * TOPK].astype(jnp.int32).reshape(-1, TOPK)
-    )
-    routes_by_group = group_routes.reshape(groups, rows_dev, TOPK)
-    slots_by_group = jax.vmap(partial(assign_slots, experts=members))(routes_by_group)
     own_slots = assign_slots(routes, members)
     own_matrix = dispatch_matrix(routes, own_slots, members, capacity).reshape(
         rows_dev, members, capacity
@@ -309,6 +300,17 @@
         arrived.reshape(members, 1, capacity, D), "dp", axis=1, tiled=True
     )
     expert_rows = expert_rows.reshape(-1, D)
+    own_both, _ = lax.optimization_barrier(
+        (jnp.concatenate([normed, route_row], axis=0), arrived)
+    )
+    group_both = lax.all_gather(own_both[None], "dp", axis=0, tiled=True)
+    expert_rows, group_both = lax.optimization_barrier((expert_rows, group_both))
+    group_tokens = group_both[:, :rows_dev].reshape(groups * rows_dev, D)
+    group_routes = (
+        group_both[:, rows_dev, : rows_dev * TOPK].astype(jnp.int32).reshape(-1, TOPK)
+    )
+    routes_by_group = group_routes.reshape(groups, rows_dev, TOPK)
+    slots_by_group = jax.vmap(partial(assign_slots, experts=members))(routes_by_group)
     gate_proj = jnp.dot(expert_rows, gate_weight[0], preferred_element_type=jnp.float32)
     up_proj = jnp.dot(expert_rows, up_weight[0], preferred_element_type=jnp.float32)
     expert_act = (jax.nn.silu(gate_proj) * up_proj).astype(jnp.bfloat16)

time: 330 us -> 327 us (level)
  local copies, waits for them, and re-layouts: 55.8 us -> 51.7 us
    all_gather x1, waiting for transfers between devices: 6.52 us -> 21.8 us  [shards(): routed_piece = lax.all_gather(expert_act, 'dp', axis=1, tiled=True)]
    all_gather x1, waiting for transfers between devices: 30.7 us -> 18.1 us  [shards(): lax.all_gather(arrived.reshape(members, 1, capacity, D), 'dp', axis=1, ti...]
    unnamed x54 -> x52, local copies, waits for them, and re-layouts: 7.51 us -> 6.87 us
  transfers between devices with their start and end apart: 7 -> 7, of which waited for: 2 -> 2; matrix products, arithmetic and copies ran while one was open for 15% -> 13% of each run, Pallas kernels for 19% -> 19%
where the time goes in v10:
time: 327 us; the launch traced here: 326 us
  blocking collectives  97.2 us (30%)
  Pallas kernels  61.4 us (19%)
  local copies, waits for them, and re-layouts  51.7 us (16%)
  waiting for transfers between devices  39.9 us (12%)
  starting transfers between devices  34.5 us (11%)
  matrix products  18.5 us (6%)
  between operations  16.3 us (5%)
  other arithmetic  6.65 us (2%)
    pallas_call x1, Pallas kernels, expert_gather(): pl.pallas_call(partial(gather_kernel, nx, nz), out_shape=jax.ShapeDtypeSt...  61.4 us
    all_to_all x1, blocking collectives, shards(): lax.all_to_all(outgoing, 'expert', split_axis=0, concat_axis=0, tiled=True)  39.6 us
    unnamed x1, blocking collectives  21.8 us
    all_gather x1, waiting for transfers between devices, shards(): routed_piece = lax.all_gather(expert_act, 'dp', axis=1, tiled=True)  21.8 us
    all_gather x1, waiting for transfers between devices, shards(): lax.all_gather(arrived.reshape(members, 1, capacity, D), 'dp', axis=1, ti...  18.1 us
    all_to_all x1, starting transfers between devices, shards(): lax.all_to_all(expert_out.reshape(members, groups * capacity, col_width),...  15.3 us
    all_gather x1, blocking collectives, shards(): shared_piece = lax.all_gather(shared_act, 'dp', axis=1, tiled=True)  13.5 us
    all_gather x1, blocking collectives, shards(): group_both = lax.all_gather(own_both[None], 'dp', axis=0, tiled=True)  12.6 us
  transfers between devices with their start and end apart: 7, of which 2 were waited for; matrix products, arithmetic and copies ran while one was open for 13% of the time, Pallas kernels for 19%

profile of v10, /device:TPU:1, one launch (start us, length us, event | category | flops | bytes accessed | tf_op | source)
XLA Modules:
  0.0 326.1 jit_solution(14209380936051630203)
XLA Ops:
  8.0 0.7 slice_convert_fusion.1
  8.7 1.7 fusion.92
  10.4 0.9 convert_convert_fusion
  11.3 1.6 fusion.93
  12.9 0.7 broadcast_maximum_fusion
  13.7 0.7 exponential_add_fusion
  14.3 1.1 fusion.3
  16.1 0.9 copy.78
  17.0 10.2 %all-to-all-start = ((bf16[17,16,512]{2,0,1:T(8,128)(2,1)}), bf16[17,16,512]{2,0,1:T(8,128)(2,1)S(1)}, u32[]{:S(2)}, u32[]{:S(2)}) async-start(bf16[17,16,512]{2,0,1:T(8,128)(2,1)} %copy.78), calls=%async_computation | async-start | bytes 786432 | tf_op jit(solution)/shard_map/all_to_all | solution.py:266
  29.0 0.6 pad_bitcast_fusion.shard_ref
  29.6 61.4 %shard_map.203 = bf16[16,4,232,128]{3,2,1,0:T(8,128)(2,1)} custom-call(bf16[232,128]{1,0:T(8,128)(2,1)} %pad_bitcast_fusion.shard_ref), custom_call_target="tpu_custom_call" | custom-call | tf_op jit(solution)/shard_map/pallas_call | solution.py:137
  91.0 2.3 copy.75
  93.9 1.8 copy-done.1
  96.4 0.7 sub.97
  97.1 0.8 reshape.476
  98.0 1.7 copy.81
  99.7 1.5 reshape.477
  101.1 0.7 multiply_add_fusion
  102.9 21.8 %fusion = bf16[24,2048]{1,0:T(8,128)(2,1)S(1)} fusion(bf16[136,2048]{1,0:T(8,128)(2,1)S(1)} %fusion.1), kind=kCustom, calls=%all-reduce-scatter | all-reduce-scatter fusion | flops 393217 | bytes 657408
  124.7 1.3 collective-permute-start.1
  126.0 3.5 %collective-permute-start = (bf16[24,2048]{1,0:T(8,128)(2,1)S(1)}, bf16[24,2048]{1,0:T(8,128)(2,1)S(1)}, u32[]{:S(2)}, u32[]{:S(2)}) collective-permute-start(bf16[24,2048]{1,0:T(8,128)(2,1)S(1)} %fusion), channel_id=1, source_target_pairs={{0,64},{64,128},{128,192},{192,256},{256,320},{320,384},{384,448},... | collective-permute-start | bytes 294920
  129.5 4.1 %collective-permute-start.2 = (bf16[1,2048]{1,0:T(2,128)(2,1)S(1)}, bf16[1,2048]{1,0:T(2,128)(2,1)S(1)}, u32[]{:S(2)}, u32[]{:S(2)}) collective-permute-start(bf16[1,2048]{1,0:T(2,128)(2,1)S(1)} %slice.94), channel_id=1, source_target_pairs={{0,192},{64,256},{128,320},{192,384},{256,448},{1,193},{65,257},{1... | collective-permute-start | bytes 12296
  133.7 1.3 dynamic-slice.4
  137.5 39.6 %all_to_all.37 = bf16[64,2,2048]{2,1,0:T(2,128)(2,1)S(1)} all-to-all(bf16[64,2,2048]{2,1,0:T(2,128)(2,1)S(1)} %copy.84), channel_id=1, replica_groups=mesh['dp'=8,'expert'=64] {'expert'}, dimensions={0} | all-to-all | bytes 1048576 | tf_op jit(solution)/shard_map/all_to_all | solution.py:292
  177.2 1.0 copy.85
  178.5 12.6 %all-gather.2 = bf16[8,18,2048]{2,1,0:T(8,128)(2,1)S(1)} all-gather(bf16[1,18,2048]{2,1,0:T(8,128)(2,1)S(1)} %bitcast.158), channel_id=3, replica_groups=mesh['dp'=8,'expert'=64] {'dp'}, dimensions={0}, use_global_device_ids=true | all-gather | bytes 663552 | tf_op jit(solution)/shard_map/all_gather | solution.py:306
  191.1 18.1 %all-gather.9.cloned.1.call-done = bf16[64,16,2048]{2,0,1:T(8,128)(2,1)} async-done(((bf16[64,2,2048]{2,0,1:T(8,128)(2,1)}), bf16[64,16,2048]{2,0,1:T(8,128)(2,1)}) %all-gather.9.cloned.1.call-update) | async-done | bytes 4194320 | tf_op jit(solution)/shard_map/all_gather | solution.py:299
  209.2 4.5 %copy.86 = bf16[64,16,2048]{2,1,0:T(8,128)(2,1)S(1)} copy(bf16[64,16,2048]{2,0,1:T(8,128)(2,1)} %all-gather.9.cloned.1.call-done) | data formatting | bytes 8388608 | tf_op jit(solution)/shard_map/all_gather | solution.py:299
  213.7 1.6 fusion.27
  215.3 2.4 fusion.2
  217.8 2.5 fusion.91
  220.4 1.8 reshape_reshape.12
  222.1 3.0 reshape_reshape.11
  225.2 3.0 reshape_reshape.10
  228.3 2.0 select_reduce_fusion
  230.4 21.8 %all-gather.7.cloned.1.call-done = bf16[1024,1408]{0,1:T(8,128)(2,1)} async-done(((bf16[1024,176]{0,1:T(8,128)(2,1)}), bf16[1024,1408]{0,1:T(8,128)(2,1)}) %all-gather.7.cloned.1.call-update) | async-done | bytes 2883600 | tf_op jit(solution)/shard_map/all_gather | solution.py:324
  252.2 3.7 %convolution_convert_fusion = bf16[1024,256]{1,0:T(8,128)(2,1)} fusion(bf16[1024,1408]{0,1:T(8,128)(2,1)} %all-gather.7.cloned.1.call-done, bf16[1,1408,256]{2,1,0:T(8,128)(2,1)S(1)} %copy-done), kind=kOutput, calls=%fused_computation.5 | convolution fusion | flops 738459648 | bytes 4128768 | tf_op jit(solution)/shard_map/dot_general | solution.py:326
  255.9 15.3 %all-to-all-start.2 = ((bf16[64,16,256]{2,1,0:T(8,128)(2,1)}), bf16[64,16,256]{2,1,0:T(8,128)(2,1)S(1)}, u32[]{:S(2)}, u32[]{:S(2)}) async-start(bf16[64,16,256]{2,1,0:T(8,128)(2,1)} %bitcast.157), calls=%async_computation.2 | async-start | bytes 1048576 | tf_op jit(solution)/shard_map/all_to_all | solution.py:330
  272.3 1.3 reshape.481
  273.6 1.3 fusion.33
  274.9 10.7 %gather_fusion.1 = f32[816]{0:T(1024)S(1)} fusion(f32[136,64]{0,1:T(8,128)S(1)} %fusion.33, s32[816]{0:T(1024)S(1)} %reshape.500), kind=kCustom, calls=%fused_computation.1 | custom fusion | bytes 13056 | tf_op jit(solution)/shard_map/jit(take_along_axis)/gather | solution.py:344
  286.3 1.5 fusion.11
  287.9 13.5 %all-gather.3 = bf16[8,176,136]{1,2,0:T(8,128)(2,1)S(1)} all-gather(bf16[1,176,136]{1,2,0:T(8,128)(2,1)S(1)} %fusion.11), channel_id=1, replica_groups=mesh['dp'=8,'expert'=64] {'dp'}, dimensions={0}, use_global_device_ids=true | all-gather | bytes 430848 | tf_op jit(solution)/shard_map/all_gather | solution.py:325
  301.5 1.3 reshape.513
  302.8 3.4 %gather_fusion = bf16[816,256]{1,0:T(8,128)(2,1)S(1)} fusion(bf16[1024,256]{1,0:T(8,128)(2,1)S(1)} %bitcast.140, s32[1024]{0:T(1024)S(1)} %pad_clamp_fusion), kind=kCustom, calls=%fused_computation | custom fusion | bytes 838848 | tf_op jit(solution)/shard_map/jit(_take)/gather | solution.py:341
  306.9 1.3 fusion.10
  308.2 9.6 %all_to_all.38 = bf16[8,17,256]{2,1,0:T(8,128)(2,1)S(1)} all-to-all(bf16[8,17,256]{2,1,0:T(8,128)(2,1)S(1)} %convert_element_type.222), channel_id=1, replica_groups=mesh['dp'=8,'expert'=64] {'dp'}, dimensions={0} | all-to-all | bytes 139264 | tf_op jit(solution)/shard_map/all_to_all | solution.py:350
  318.6 0.6 slice.92
  (125 shorter events, 10.5 us)
Async XLA Ops:
  7.2 245.0 %copy-start = (bf16[1,1408,256]{2,1,0:T(8,128)(2,1)S(1)}, bf16[1,1408,256]{2,1,0:T(8,128)(2,1)}, u32[]{:S(2)}) copy-start(bf16[1,1408,256]{2,1,0:T(8,128)(2,1)} %param.36) | copy-start | bytes 2162692
  7.2 8.5 %copy-start.4 = (bf16[1,1024,576]{1,2,0:T(8,128)(2,1)S(1)}, bf16[1,1024,576]{1,2,0:T(8,128)(2,1)}, u32[]{:S(2)}) copy-start(bf16[1,1024,576]{1,2,0:T(8,128)(2,1)} %param.27) | copy-start | bytes 3538948
  7.2 8.4 %copy-start.13 = (f32[16]{0:T(128)S(1)}, f32[16]{0:T(128)}, u32[]{:S(2)}) copy-start(f32[16]{0:T(128)} %param.28) | copy-start | bytes 196
  7.2 20.0 %copy-start.6 = (bf16[32,176]{1,0:T(8,128)(2,1)S(1)}, bf16[32,176]{1,0:T(8,128)(2,1)}, u32[]{:S(2)}) copy-start(bf16[32,176]{1,0:T(8,128)(2,1)} %param.37) | copy-start | bytes 33796
  7.2 20.1 %copy-start.7 = (bf16[32,176]{1,0:T(8,128)(2,1)S(1)}, bf16[32,176]{1,0:T(8,128)(2,1)}, u32[]{:S(2)}) copy-start(bf16[32,176]{1,0:T(8,128)(2,1)} %param.38) | copy-start | bytes 33796
  7.2 20.2 %copy-start.10 = (bf16[22,256]{1,0:T(8,128)(2,1)S(1)}, bf16[22,256]{1,0:T(8,128)(2,1)}, u32[]{:S(2)}) copy-start(bf16[22,256]{1,0:T(8,128)(2,1)} %param.39) | copy-start | bytes 33796
  7.2 20.3 %copy-start.8 = (bf16[2,2,2048]{2,1,0:T(2,128)(2,1)S(1)}, bf16[2,2,2048]{2,1,0:T(2,128)(2,1)}, u32[]{:S(2)}) copy-start(bf16[2,2,2048]{2,1,0:T(2,128)(2,1)} %param.30) | copy-start | bytes 49156
  7.2 20.3 %copy-start.15 = (bf16[2,8,128]{2,1,0:T(8,128)(2,1)S(1)}, bf16[2,8,128]{2,1,0:T(8,128)(2,1)}, u32[]{:S(2)}) copy-start(bf16[2,8,128]{2,1,0:T(8,128)(2,1)} %param.29) | copy-start | bytes 12292
  7.3 20.3 %copy-start.12 = (bf16[2048,1]{0,1:T(2,128)(2,1)S(1)}, bf16[2048,1]{0,1:T(2,128)(2,1)}, u32[]{:S(2)}) copy-start(bf16[2048,1]{0,1:T(2,128)(2,1)} %param.32) | copy-start | bytes 12292
  17.0 85.1 %all-to-all-start = ((bf16[17,16,512]{2,0,1:T(8,128)(2,1)}), bf16[17,16,512]{2,0,1:T(8,128)(2,1)S(1)}, u32[]{:S(2)}, u32[]{:S(2)}) async-start(bf16[17,16,512]{2,0,1:T(8,128)(2,1)} %copy.78), calls=%async_computation | async-start | bytes 786432 | tf_op jit(solution)/shard_map/all_to_all | solution.py:266
  27.2 182.0 %all-gather.9.cloned.1.call-start = ((), (), s32[]{:S(2)}) async-start(), calls=%async_computation.5 | async-start | bytes 4718592 | tf_op jit(solution)/shard_map/all_gather | solution.py:299
  93.4 2.4 copy-start.9
  93.9 1.8 copy-start.1
  97.9 38.3 %copy-start.5 = (bf16[16,2048]{1,0:T(8,128)(2,1)S(1)}, bf16[16,2048]{1,0:T(8,128)(2,1)}, u32[]{:S(2)}) copy-start(bf16[16,2048]{1,0:T(8,128)(2,1)} %param.22) | copy-start | bytes 196612
  99.7 34.0 %copy-start.14 = (bf16[2048]{0:T(1024)(128)(2,1)S(1)}, bf16[2048]{0:T(1024)(128)(2,1)}, u32[]{:S(2)}) copy-start(bf16[2048]{0:T(1024)(128)(2,1)} %param.31) | copy-start | bytes 12292
  99.7 36.6 %copy-start.11 = (bf16[1,2048]{1,0:T(2,128)(2,1)S(1)}, bf16[1,2048]{1,0:T(2,128)(2,1)}, u32[]{:S(2)}) copy-start(bf16[1,2048]{1,0:T(2,128)(2,1)} %param.25) | copy-start | bytes 12292
  124.7 10.9 %collective-permute-start.1 = (bf16[24,2048]{1,0:T(8,128)(2,1)S(1)}, bf16[24,2048]{1,0:T(8,128)(2,1)S(1)}, u32[]{:S(2)}, u32[]{:S(2)}) collective-permute-start(bf16[24,2048]{1,0:T(8,128)(2,1)S(1)} %fusion), channel_id=1, source_target_pairs={{0,128},{64,192},{128,256},{192,320},{256,384},{320,448},{1,129},{... | collective-permute-start | bytes 294920
  126.0 9.6 %collective-permute-start = (bf16[24,2048]{1,0:T(8,128)(2,1)S(1)}, bf16[24,2048]{1,0:T(8,128)(2,1)S(1)}, u32[]{:S(2)}, u32[]{:S(2)}) collective-permute-start(bf16[24,2048]{1,0:T(8,128)(2,1)S(1)} %fusion), channel_id=1, source_target_pairs={{0,64},{64,128},{128,192},{192,256},{256,320},{320,384},{384,448},... | collective-permute-start | bytes 294920
  129.5 6.1 %collective-permute-start.2 = (bf16[1,2048]{1,0:T(2,128)(2,1)S(1)}, bf16[1,2048]{1,0:T(2,128)(2,1)S(1)}, u32[]{:S(2)}, u32[]{:S(2)}) collective-permute-start(bf16[1,2048]{1,0:T(2,128)(2,1)S(1)} %slice.94), channel_id=1, source_target_pairs={{0,192},{64,256},{128,320},{192,384},{256,448},{1,193},{65,257},{1... | collective-permute-start | bytes 12296
  178.2 74.0 %all-gather.7.cloned.1.call-start = ((), (), s32[]{:S(2)}) async-start(), calls=%async_computation.4 | async-start | bytes 3244032 | tf_op jit(solution)/shard_map/all_gather | solution.py:324
  191.1 80.4 %copy-start.2 = (bf16[8,18,2048]{2,1,0:T(8,128)(2,1)}, bf16[8,18,2048]{2,1,0:T(8,128)(2,1)S(1)}, u32[]{:S(2)}) copy-start(bf16[8,18,2048]{2,1,0:T(8,128)(2,1)S(1)} %all-gather.2) | copy-start | bytes 1769476
  191.1 22.6 %copy-start.16 = (bf16[1,2048,176]{1,2,0:T(8,128)(2,1)S(1)}, bf16[1,2048,176]{1,2,0:T(8,128)(2,1)}, u32[]{:S(2)}) copy-start(bf16[1,2048,176]{1,2,0:T(8,128)(2,1)} %param.34) | copy-start | bytes 2162692
  213.7 1.6 copy-start.17
  255.9 46.9 %all-to-all-start.2 = ((bf16[64,16,256]{2,1,0:T(8,128)(2,1)}), bf16[64,16,256]{2,1,0:T(8,128)(2,1)S(1)}, u32[]{:S(2)}, u32[]{:S(2)}) async-start(bf16[64,16,256]{2,1,0:T(8,128)(2,1)} %bitcast.157), calls=%async_computation.2 | async-start | bytes 1048576 | tf_op jit(solution)/shard_map/all_to_all | solution.py:330
  301.5 5.4 %copy-start.3 = (bf16[1408,256]{1,0:T(8,128)(2,1)S(1)}, bf16[1408,256]{1,0:T(8,128)(2,1)}, u32[]{:S(2)}) copy-start(bf16[1408,256]{1,0:T(8,128)(2,1)} %reshape_reshape.12) | copy-start | bytes 2162692
Sparse Core Ops, SparseCore 0:
  178.3 30.8 all-gather.8
  217.8 34.3 all-gather.6

commit v11 on v10

--- a/solution.py
+++ b/solution.py
@@ -127,6 +127,58 @@
         c.wait_send()
     for c in x_copies:
         c.wait_send()
+
+
+def exchange_kernel(members, send_ref, recv_ref, send_sem, recv_sem, own_sem):
+    d = lax.axis_index("dp")
+    e = lax.axis_index("expert")
+    barrier = pltpu.get_barrier_semaphore()
+    for k in range(1, members):
+        peer = (e + k) % members
+        pl.semaphore_signal(barrier, 1, device_id=(d, peer), device_id_type=MESH_ID)
+    pl.semaphore_wait(barrier, members - 1)
+
+    def remote(peer, slot):
+        return pltpu.make_async_remote_copy(
+            src_ref=send_ref.at[peer],
+            dst_ref=recv_ref.at[slot],
+            send_sem=send_sem.at[peer],
+            recv_sem=recv_sem.at[slot],
+            device_id=(d, peer),
+            device_id_type=MESH_ID,
+        )
+
+    own = pltpu.make_async_copy(send_ref.at[e], recv_ref.at[e], own_sem)
+    own.start()
+
+    def start(k, carry):
+        remote((e + k) % members, e).start()
+        return carry
+
+    lax.fori_loop(1, members, start, 0)
+    own.wait()
+
+    def finish(k, carry):
+        remote((e + members - k) % members, (e + members - k) % members).wait_recv()
+        remote((e + k) % members, e).wait_send()
+        return carry
+
+    lax.fori_loop(1, members, finish, 0)
+
+
+def expert_exchange(outgoing, members):
+    return pl.pallas_call(
+        partial(exchange_kernel, members),
+        out_shape=jax.ShapeDtypeStruct(outgoing.shape, outgoing.dtype),
+        in_specs=[pl.BlockSpec(memory_space=pltpu.VMEM)],
+        out_specs=pl.BlockSpec(memory_space=pltpu.VMEM),
+        scratch_shapes=[
+            pltpu.SemaphoreType.DMA((members,)),
+            pltpu.SemaphoreType.DMA((members,)),
+            pltpu.SemaphoreType.DMA(()),
+        ],
+        compiler_params=pltpu.CompilerParams(collective_id=1, has_side_effects=True),
+    )(outgoing)
 
 
 def expert_gather(flat, members):
@@ -289,7 +341,7 @@
         rows_dev, members, capacity
     )
     outgoing = jnp.einsum("rxc,rd->xcd", own_matrix, normed, preferred_element_type=jnp.bfloat16)
-    arrived = lax.all_to_all(outgoing, "expert", split_axis=0, concat_axis=0, tiled=True)
+    arrived = expert_exchange(outgoing, members)
     shared_ready = (
         weights["shared_gate"],
         weights["shared_up"],

time: 327 us -> 329 us (level)
  Pallas kernels: 61.4 us -> 101 us
  blocking collectives: 97.2 us -> 59.7 us
    pallas_call x0 -> x1, Pallas kernels: none -> 39.8 us  [expert_exchange(): pl.pallas_call(partial(exchange_kernel, members), out_shape=jax.ShapeDtyp...]
    all_to_all x1 -> x0, blocking collectives: 39.6 us -> none  [shards(): lax.all_to_all(outgoing, 'expert', split_axis=0, concat_axis=0, tiled=True)]
where the time goes in v11:
time: 329 us; the launch traced here: 328 us
  Pallas kernels  101 us (31%)
  blocking collectives  59.7 us (18%)
  local copies, waits for them, and re-layouts  53.5 us (16%)
  waiting for transfers between devices  37.8 us (11%)
  starting transfers between devices  34.5 us (10%)
  matrix products  18.5 us (6%)
  between operations  16.3 us (5%)
  other arithmetic  6.65 us (2%)
    pallas_call x1, Pallas kernels, expert_gather(): pl.pallas_call(partial(gather_kernel, nx, nz), out_shape=jax.ShapeDtypeSt...  61.4 us
    pallas_call x1, Pallas kernels, expert_exchange(): pl.pallas_call(partial(exchange_kernel, members), out_shape=jax.ShapeDtyp...  39.8 us
    unnamed x1, blocking collectives  21.8 us
    all_gather x1, waiting for transfers between devices, shards(): routed_piece = lax.all_gather(expert_act, 'dp', axis=1, tiled=True)  21.2 us
    all_gather x1, waiting for transfers between devices, shards(): lax.all_gather(arrived.reshape(members, 1, capacity, D), 'dp', axis=1, ti...  16.5 us
    all_to_all x1, starting transfers between devices, shards(): lax.all_to_all(expert_out.reshape(members, groups * capacity, col_width),...  15.3 us
    all_gather x1, blocking collectives, shards(): group_both = lax.all_gather(own_both[None], 'dp', axis=0, tiled=True)  14.8 us
    all_gather x1, blocking collectives, shards(): shared_piece = lax.all_gather(shared_act, 'dp', axis=1, tiled=True)  13.5 us
  transfers between devices with their start and end apart: 7, of which 2 were waited for; matrix products, arithmetic and copies ran while one was open for 13% of the time, Pallas kernels for 19%

profile of v11, /device:TPU:1, one launch (start us, length us, event | category | flops | bytes accessed | tf_op | source)
XLA Modules:
  0.0 328.1 jit_solution(17503384029544906239)
XLA Ops:
  8.0 0.7 slice_convert_fusion.1
  8.7 1.7 fusion.92
  10.4 0.9 convert_convert_fusion
  11.3 1.6 fusion.93
  12.9 0.7 broadcast_maximum_fusion
  13.7 0.7 exponential_add_fusion
  14.3 1.1 fusion.3
  16.1 0.9 copy.78
  17.0 10.2 %all-to-all-start = ((bf16[17,16,512]{2,0,1:T(8,128)(2,1)}), bf16[17,16,512]{2,0,1:T(8,128)(2,1)S(1)}, u32[]{:S(2)}, u32[]{:S(2)}) async-start(bf16[17,16,512]{2,0,1:T(8,128)(2,1)} %copy.78), calls=%async_computation | async-start | bytes 786432 | tf_op jit(solution)/shard_map/all_to_all | solution.py:318
  29.6 61.4 %shard_map.203 = bf16[16,4,232,128]{3,2,1,0:T(8,128)(2,1)} custom-call(bf16[232,128]{1,0:T(8,128)(2,1)} %pad_bitcast_fusion.shard_ref), custom_call_target="tpu_custom_call" | custom-call | tf_op jit(solution)/shard_map/pallas_call | solution.py:189
  91.0 2.3 copy.75
  93.9 1.8 copy-done.1
  96.4 0.7 sub.97
  97.1 0.8 reshape.476
  98.0 1.7 copy.81
  99.7 1.5 reshape.477
  101.1 0.7 multiply_add_fusion
  102.9 21.8 %fusion = bf16[24,2048]{1,0:T(8,128)(2,1)S(1)} fusion(bf16[136,2048]{1,0:T(8,128)(2,1)S(1)} %fusion.1), kind=kCustom, calls=%all-reduce-scatter | all-reduce-scatter fusion | flops 393217 | bytes 657408
  124.7 1.3 collective-permute-start.1
  126.0 3.5 %collective-permute-start = (bf16[24,2048]{1,0:T(8,128)(2,1)S(1)}, bf16[24,2048]{1,0:T(8,128)(2,1)S(1)}, u32[]{:S(2)}, u32[]{:S(2)}) collective-permute-start(bf16[24,2048]{1,0:T(8,128)(2,1)S(1)} %fusion), channel_id=1, source_target_pairs={{0,64},{64,128},{128,192},{192,256},{256,320},{320,384},{384,448},... | collective-permute-start | bytes 294920
  129.5 4.1 %collective-permute-start.2 = (bf16[1,2048]{1,0:T(2,128)(2,1)S(1)}, bf16[1,2048]{1,0:T(2,128)(2,1)S(1)}, u32[]{:S(2)}, u32[]{:S(2)}) collective-permute-start(bf16[1,2048]{1,0:T(2,128)(2,1)S(1)} %slice.94), channel_id=1, source_target_pairs={{0,192},{64,256},{128,320},{192,384},{256,448},{1,193},{65,257},{1... | collective-permute-start | bytes 12296
  133.7 1.3 dynamic-slice.4
  137.0 1.3 copy.84.send_ref
  138.3 39.8 %shard_map.204 = bf16[64,2,2048]{2,1,0:T(2,128)(2,1)} custom-call(bf16[64,2,2048]{2,1,0:T(2,128)(2,1)} %copy.84.send_ref), custom_call_target="tpu_custom_call" | custom-call | tf_op jit(solution)/shard_map/pallas_call | solution.py:170
  178.1 2.0 copy.85
  180.5 14.8 %all-gather.2 = bf16[8,18,2048]{2,1,0:T(8,128)(2,1)S(1)} all-gather(bf16[1,18,2048]{2,1,0:T(8,128)(2,1)S(1)} %bitcast.158), channel_id=3, replica_groups=mesh['dp'=8,'expert'=64] {'dp'}, dimensions={0}, use_global_device_ids=true | all-gather | bytes 663552 | tf_op jit(solution)/shard_map/all_gather | solution.py:358
  195.2 16.5 %all-gather.9.cloned.1.call-done = bf16[64,16,2048]{2,0,1:T(8,128)(2,1)} async-done(((bf16[64,2,2048]{2,0,1:T(8,128)(2,1)}), bf16[64,16,2048]{2,0,1:T(8,128)(2,1)}) %all-gather.9.cloned.1.call-update) | async-done | bytes 4194320 | tf_op jit(solution)/shard_map/all_gather | solution.py:351
  211.8 4.5 %copy.86 = bf16[64,16,2048]{2,1,0:T(8,128)(2,1)S(1)} copy(bf16[64,16,2048]{2,0,1:T(8,128)(2,1)} %all-gather.9.cloned.1.call-done) | data formatting | bytes 8388608 | tf_op jit(solution)/shard_map/all_gather | solution.py:351
  216.3 1.6 fusion.27
  217.8 2.4 fusion.2
  220.4 2.5 fusion.91
  222.9 1.8 reshape_reshape.12
  224.7 3.0 reshape_reshape.11
  227.7 3.0 reshape_reshape.10
  230.9 2.0 select_reduce_fusion
  233.0 21.2 %all-gather.7.cloned.1.call-done = bf16[1024,1408]{0,1:T(8,128)(2,1)} async-done(((bf16[1024,176]{0,1:T(8,128)(2,1)}), bf16[1024,1408]{0,1:T(8,128)(2,1)}) %all-gather.7.cloned.1.call-update) | async-done | bytes 2883600 | tf_op jit(solution)/shard_map/all_gather | solution.py:376
  254.2 3.7 %convolution_convert_fusion = bf16[1024,256]{1,0:T(8,128)(2,1)} fusion(bf16[1024,1408]{0,1:T(8,128)(2,1)} %all-gather.7.cloned.1.call-done, bf16[1,1408,256]{2,1,0:T(8,128)(2,1)S(1)} %copy-done), kind=kOutput, calls=%fused_computation.5 | convolution fusion | flops 738459648 | bytes 4128768 | tf_op jit(solution)/shard_map/dot_general | solution.py:378
  257.9 15.3 %all-to-all-start.1 = ((bf16[64,16,256]{2,1,0:T(8,128)(2,1)}), bf16[64,16,256]{2,1,0:T(8,128)(2,1)S(1)}, u32[]{:S(2)}, u32[]{:S(2)}) async-start(bf16[64,16,256]{2,1,0:T(8,128)(2,1)} %bitcast.157), calls=%async_computation.1 | async-start | bytes 1048576 | tf_op jit(solution)/shard_map/all_to_all | solution.py:382
  274.3 1.3 reshape.481
  275.7 1.3 fusion.33
  276.9 10.7 %gather_fusion.1 = f32[816]{0:T(1024)S(1)} fusion(f32[136,64]{0,1:T(8,128)S(1)} %fusion.33, s32[816]{0:T(1024)S(1)} %reshape.500), kind=kCustom, calls=%fused_computation.1 | custom fusion | bytes 13056 | tf_op jit(solution)/shard_map/jit(take_along_axis)/gather | solution.py:396
  288.3 1.5 fusion.11
  289.9 13.5 %all-gather.3 = bf16[8,176,136]{1,2,0:T(8,128)(2,1)S(1)} all-gather(bf16[1,176,136]{1,2,0:T(8,128)(2,1)S(1)} %fusion.11), channel_id=1, replica_groups=mesh['dp'=8,'expert'=64] {'dp'}, dimensions={0}, use_global_device_ids=true | all-gather | bytes 430848 | tf_op jit(solution)/shard_map/all_gather | solution.py:377
  303.5 1.3 reshape.513
  304.8 3.4 %gather_fusion = bf16[816,256]{1,0:T(8,128)(2,1)S(1)} fusion(bf16[1024,256]{1,0:T(8,128)(2,1)S(1)} %bitcast.140, s32[1024]{0:T(1024)S(1)} %pad_clamp_fusion), kind=kCustom, calls=%fused_computation | custom fusion | bytes 838848 | tf_op jit(solution)/shard_map/jit(_take)/gather | solution.py:393
  308.9 1.3 fusion.10
  310.2 9.6 %all_to_all.32 = bf16[8,17,256]{2,1,0:T(8,128)(2,1)S(1)} all-to-all(bf16[8,17,256]{2,1,0:T(8,128)(2,1)S(1)} %convert_element_type.222), channel_id=1, replica_groups=mesh['dp'=8,'expert'=64] {'dp'}, dimensions={0} | all-to-all | bytes 139264 | tf_op jit(solution)/shard_map/all_to_all | solution.py:402
  320.6 0.6 slice.92
  (125 shorter events, 10.6 us)
Async XLA Ops:
  7.2 247.1 %copy-start = (bf16[1,1408,256]{2,1,0:T(8,128)(2,1)S(1)}, bf16[1,1408,256]{2,1,0:T(8,128)(2,1)}, u32[]{:S(2)}) copy-start(bf16[1,1408,256]{2,1,0:T(8,128)(2,1)} %param.36) | copy-start | bytes 2162692
  7.2 8.5 %copy-start.4 = (bf16[1,1024,576]{1,2,0:T(8,128)(2,1)S(1)}, bf16[1,1024,576]{1,2,0:T(8,128)(2,1)}, u32[]{:S(2)}) copy-start(bf16[1,1024,576]{1,2,0:T(8,128)(2,1)} %param.27) | copy-start | bytes 3538948
  7.2 8.4 %copy-start.13 = (f32[16]{0:T(128)S(1)}, f32[16]{0:T(128)}, u32[]{:S(2)}) copy-start(f32[16]{0:T(128)} %param.28) | copy-start | bytes 196
  7.2 20.0 %copy-start.6 = (bf16[32,176]{1,0:T(8,128)(2,1)S(1)}, bf16[32,176]{1,0:T(8,128)(2,1)}, u32[]{:S(2)}) copy-start(bf16[32,176]{1,0:T(8,128)(2,1)} %param.37) | copy-start | bytes 33796
  7.2 20.1 %copy-start.7 = (bf16[32,176]{1,0:T(8,128)(2,1)S(1)}, bf16[32,176]{1,0:T(8,128)(2,1)}, u32[]{:S(2)}) copy-start(bf16[32,176]{1,0:T(8,128)(2,1)} %param.38) | copy-start | bytes 33796
  7.2 20.2 %copy-start.10 = (bf16[22,256]{1,0:T(8,128)(2,1)S(1)}, bf16[22,256]{1,0:T(8,128)(2,1)}, u32[]{:S(2)}) copy-start(bf16[22,256]{1,0:T(8,128)(2,1)} %param.39) | copy-start | bytes 33796
  7.2 20.3 %copy-start.8 = (bf16[2,2,2048]{2,1,0:T(2,128)(2,1)S(1)}, bf16[2,2,2048]{2,1,0:T(2,128)(2,1)}, u32[]{:S(2)}) copy-start(bf16[2,2,2048]{2,1,0:T(2,128)(2,1)} %param.30) | copy-start | bytes 49156
  7.2 20.3 %copy-start.15 = (bf16[2,8,128]{2,1,0:T(8,128)(2,1)S(1)}, bf16[2,8,128]{2,1,0:T(8,128)(2,1)}, u32[]{:S(2)}) copy-start(bf16[2,8,128]{2,1,0:T(8,128)(2,1)} %param.29) | copy-start | bytes 12292
  7.3 20.3 %copy-start.12 = (bf16[2048,1]{0,1:T(2,128)(2,1)S(1)}, bf16[2048,1]{0,1:T(2,128)(2,1)}, u32[]{:S(2)}) copy-start(bf16[2048,1]{0,1:T(2,128)(2,1)} %param.32) | copy-start | bytes 12292
  17.0 85.1 %all-to-all-start = ((bf16[17,16,512]{2,0,1:T(8,128)(2,1)}), bf16[17,16,512]{2,0,1:T(8,128)(2,1)S(1)}, u32[]{:S(2)}, u32[]{:S(2)}) async-start(bf16[17,16,512]{2,0,1:T(8,128)(2,1)} %copy.78), calls=%async_computation | async-start | bytes 786432 | tf_op jit(solution)/shard_map/all_to_all | solution.py:318
  27.2 184.5 %all-gather.9.cloned.1.call-start = ((), (), s32[]{:S(2)}) async-start(), calls=%async_computation.4 | async-start | bytes 4718592 | tf_op jit(solution)/shard_map/all_gather | solution.py:351
  93.4 2.4 copy-start.9
  93.9 1.8 copy-start.1
  97.9 38.3 %copy-start.5 = (bf16[16,2048]{1,0:T(8,128)(2,1)S(1)}, bf16[16,2048]{1,0:T(8,128)(2,1)}, u32[]{:S(2)}) copy-start(bf16[16,2048]{1,0:T(8,128)(2,1)} %param.22) | copy-start | bytes 196612
  99.7 34.0 %copy-start.14 = (bf16[2048]{0:T(1024)(128)(2,1)S(1)}, bf16[2048]{0:T(1024)(128)(2,1)}, u32[]{:S(2)}) copy-start(bf16[2048]{0:T(1024)(128)(2,1)} %param.31) | copy-start | bytes 12292
  99.7 36.6 %copy-start.11 = (bf16[1,2048]{1,0:T(2,128)(2,1)S(1)}, bf16[1,2048]{1,0:T(2,128)(2,1)}, u32[]{:S(2)}) copy-start(bf16[1,2048]{1,0:T(2,128)(2,1)} %param.25) | copy-start | bytes 12292
  124.7 10.9 %collective-permute-start.1 = (bf16[24,2048]{1,0:T(8,128)(2,1)S(1)}, bf16[24,2048]{1,0:T(8,128)(2,1)S(1)}, u32[]{:S(2)}, u32[]{:S(2)}) collective-permute-start(bf16[24,2048]{1,0:T(8,128)(2,1)S(1)} %fusion), channel_id=1, source_target_pairs={{0,128},{64,192},{128,256},{192,320},{256,384},{320,448},{1,129},{... | collective-permute-start | bytes 294920
  126.0 9.6 %collective-permute-start = (bf16[24,2048]{1,0:T(8,128)(2,1)S(1)}, bf16[24,2048]{1,0:T(8,128)(2,1)S(1)}, u32[]{:S(2)}, u32[]{:S(2)}) collective-permute-start(bf16[24,2048]{1,0:T(8,128)(2,1)S(1)} %fusion), channel_id=1, source_target_pairs={{0,64},{64,128},{128,192},{192,256},{256,320},{320,384},{384,448},... | collective-permute-start | bytes 294920
  129.5 6.1 %collective-permute-start.2 = (bf16[1,2048]{1,0:T(2,128)(2,1)S(1)}, bf16[1,2048]{1,0:T(2,128)(2,1)S(1)}, u32[]{:S(2)}, u32[]{:S(2)}) collective-permute-start(bf16[1,2048]{1,0:T(2,128)(2,1)S(1)} %slice.94), channel_id=1, source_target_pairs={{0,192},{64,256},{128,320},{192,384},{256,448},{1,193},{65,257},{1... | collective-permute-start | bytes 12296
  180.2 74.1 %all-gather.7.cloned.1.call-start = ((), (), s32[]{:S(2)}) async-start(), calls=%async_computation.3 | async-start | bytes 3244032 | tf_op jit(solution)/shard_map/all_gather | solution.py:376
  195.2 78.3 %copy-start.2 = (bf16[8,18,2048]{2,1,0:T(8,128)(2,1)}, bf16[8,18,2048]{2,1,0:T(8,128)(2,1)S(1)}, u32[]{:S(2)}) copy-start(bf16[8,18,2048]{2,1,0:T(8,128)(2,1)S(1)} %all-gather.2) | copy-start | bytes 1769476
  195.2 21.0 %copy-start.16 = (bf16[1,2048,176]{1,2,0:T(8,128)(2,1)S(1)}, bf16[1,2048,176]{1,2,0:T(8,128)(2,1)}, u32[]{:S(2)}) copy-start(bf16[1,2048,176]{1,2,0:T(8,128)(2,1)} %param.34) | copy-start | bytes 2162692
  216.2 1.6 copy-start.17
  257.9 46.9 %all-to-all-start.1 = ((bf16[64,16,256]{2,1,0:T(8,128)(2,1)}), bf16[64,16,256]{2,1,0:T(8,128)(2,1)S(1)}, u32[]{:S(2)}, u32[]{:S(2)}) async-start(bf16[64,16,256]{2,1,0:T(8,128)(2,1)} %bitcast.157), calls=%async_computation.1 | async-start | bytes 1048576 | tf_op jit(solution)/shard_map/all_to_all | solution.py:382
  303.5 5.4 %copy-start.3 = (bf16[1408,256]{1,0:T(8,128)(2,1)S(1)}, bf16[1408,256]{1,0:T(8,128)(2,1)}, u32[]{:S(2)}) copy-start(bf16[1408,256]{1,0:T(8,128)(2,1)} %reshape_reshape.12) | copy-start | bytes 2162692
Sparse Core Ops, SparseCore 0:
  180.3 31.4 all-gather.8
  220.3 33.8 all-gather.6

commit v12 on v10

--- a/solution.py
+++ b/solution.py
@@ -315,14 +315,16 @@
     up_proj = jnp.dot(expert_rows, up_weight[0], preferred_element_type=jnp.float32)
     expert_act = (jax.nn.silu(gate_proj) * up_proj).astype(jnp.bfloat16)
     shared_gate_full, shared_up_full, shared_down_full, router_full = shared_ready
+    shared_tokens, expert_act = lax.optimization_barrier((group_tokens, expert_act))
     shared_act = (
-        jax.nn.silu(jnp.dot(group_tokens, shared_gate_full, preferred_element_type=jnp.float32))
-        * jnp.dot(group_tokens, shared_up_full, preferred_element_type=jnp.float32)
+        jax.nn.silu(jnp.dot(shared_tokens, shared_gate_full, preferred_element_type=jnp.float32))
+        * jnp.dot(shared_tokens, shared_up_full, preferred_element_type=jnp.float32)
     ).astype(jnp.bfloat16)
     down_local = down_weight[0]
     col_width = down_local.shape[1]
     routed_piece = lax.all_gather(expert_act, "dp", axis=1, tiled=True)
     shared_piece = lax.all_gather(shared_act, "dp", axis=1, tiled=True)
+    routed_piece, shared_piece = lax.optimization_barrier((routed_piece, shared_piece))
     routed_cols = jnp.dot(routed_piece, down_local, preferred_element_type=jnp.float32)
     shared_cols = jnp.dot(shared_piece, shared_down_full, preferred_element_type=jnp.float32)
     expert_out = routed_cols.astype(jnp.bfloat16)

time: 327 us -> 332 us (1.015)
  local copies, waits for them, and re-layouts: 51.7 us -> 55.7 us
    all_gather x1, waiting for transfers between devices: 21.8 us -> 4.53 us  [shards(): routed_piece = lax.all_gather(expert_act, 'dp', axis=1, tiled=True)]
    all_to_all x1, waiting for transfers between devices: 0.01 us -> 14.3 us  [shards(): lax.all_to_all(expert_out.reshape(members, groups * capacity, col_width),...]
    unnamed x52 -> x54, local copies, waits for them, and re-layouts: 6.87 us -> 8.07 us
  transfers between devices with their start and end apart: 7 -> 7, of which waited for: 2 -> 3; matrix products, arithmetic and copies ran while one was open for 13% -> 14% of each run, Pallas kernels for 19% -> 19%
where the time goes in v12:
time: 332 us; the launch traced here: 330 us
  blocking collectives  99.1 us (30%)
  Pallas kernels  61.4 us (18%)
  local copies, waits for them, and re-layouts  55.7 us (17%)
  waiting for transfers between devices  37 us (11%)
  starting transfers between devices  34.5 us (10%)
  matrix products  19.8 us (6%)
  between operations  16.3 us (5%)
  other arithmetic  6.65 us (2%)
    pallas_call x1, Pallas kernels, expert_gather(): pl.pallas_call(partial(gather_kernel, nx, nz), out_shape=jax.ShapeDtypeSt...  61.4 us
    all_to_all x1, blocking collectives, shards(): lax.all_to_all(outgoing, 'expert', split_axis=0, concat_axis=0, tiled=True)  39.6 us
    unnamed x1, blocking collectives  21.8 us
    all_gather x1, waiting for transfers between devices, shards(): lax.all_gather(arrived.reshape(members, 1, capacity, D), 'dp', axis=1, ti...  18.1 us
    all_to_all x1, starting transfers between devices, shards(): lax.all_to_all(expert_out.reshape(members, groups * capacity, col_width),...  15.3 us
    all_to_all x1, waiting for transfers between devices, shards(): lax.all_to_all(expert_out.reshape(members, groups * capacity, col_width),...  14.3 us
    all_gather x1, blocking collectives, shards(): shared_piece = lax.all_gather(shared_act, 'dp', axis=1, tiled=True)  14.2 us
    all_gather x1, blocking collectives, shards(): group_both = lax.all_gather(own_both[None], 'dp', axis=0, tiled=True)  12.6 us
  transfers between devices with their start and end apart: 7, of which 3 were waited for; matrix products, arithmetic and copies ran while one was open for 14% of the time, Pallas kernels for 19%

profile of v12, /device:TPU:1, one launch (start us, length us, event | category | flops | bytes accessed | tf_op | source)
XLA Modules:
  0.0 330.4 jit_solution(13485974137109475011)
XLA Ops:
  8.0 0.7 slice_convert_fusion.1
  8.7 1.7 fusion.92
  10.4 0.9 convert_convert_fusion
  11.3 1.6 fusion.93
  12.9 0.7 broadcast_maximum_fusion
  13.7 0.7 exponential_add_fusion
  14.3 1.1 fusion.3
  16.1 0.9 copy.78
  17.0 10.2 %all-to-all-start = ((bf16[17,16,512]{2,0,1:T(8,128)(2,1)}), bf16[17,16,512]{2,0,1:T(8,128)(2,1)S(1)}, u32[]{:S(2)}, u32[]{:S(2)}) async-start(bf16[17,16,512]{2,0,1:T(8,128)(2,1)} %copy.78), calls=%async_computation | async-start | bytes 786432 | tf_op jit(solution)/shard_map/all_to_all | solution.py:266
  29.0 0.6 pad_bitcast_fusion.shard_ref
  29.6 61.4 %shard_map.203 = bf16[16,4,232,128]{3,2,1,0:T(8,128)(2,1)} custom-call(bf16[232,128]{1,0:T(8,128)(2,1)} %pad_bitcast_fusion.shard_ref), custom_call_target="tpu_custom_call" | custom-call | tf_op jit(solution)/shard_map/pallas_call | solution.py:137
  91.0 2.3 copy.75
  93.9 1.8 copy-done.1
  96.5 0.7 sub.97
  97.2 0.8 reshape.476
  98.0 1.7 copy.81
  99.7 1.5 reshape.477
  101.2 0.7 multiply_add_fusion
  102.9 21.8 %fusion = bf16[24,2048]{1,0:T(8,128)(2,1)S(1)} fusion(bf16[136,2048]{1,0:T(8,128)(2,1)S(1)} %fusion.1), kind=kCustom, calls=%all-reduce-scatter | all-reduce-scatter fusion | flops 393217 | bytes 657408
  124.8 1.3 collective-permute-start.1
  126.1 3.5 %collective-permute-start = (bf16[24,2048]{1,0:T(8,128)(2,1)S(1)}, bf16[24,2048]{1,0:T(8,128)(2,1)S(1)}, u32[]{:S(2)}, u32[]{:S(2)}) collective-permute-start(bf16[24,2048]{1,0:T(8,128)(2,1)S(1)} %fusion), channel_id=1, source_target_pairs={{0,64},{64,128},{128,192},{192,256},{256,320},{320,384},{384,448},... | collective-permute-start | bytes 294920
  129.6 4.1 %collective-permute-start.2 = (bf16[1,2048]{1,0:T(2,128)(2,1)S(1)}, bf16[1,2048]{1,0:T(2,128)(2,1)S(1)}, u32[]{:S(2)}, u32[]{:S(2)}) collective-permute-start(bf16[1,2048]{1,0:T(2,128)(2,1)S(1)} %slice.94), channel_id=1, source_target_pairs={{0,192},{64,256},{128,320},{192,384},{256,448},{1,193},{65,257},{1... | collective-permute-start | bytes 12296
  133.7 1.3 dynamic-slice.4
  137.6 39.6 %all_to_all.37 = bf16[64,2,2048]{2,1,0:T(2,128)(2,1)S(1)} all-to-all(bf16[64,2,2048]{2,1,0:T(2,128)(2,1)S(1)} %copy.84), channel_id=1, replica_groups=mesh['dp'=8,'expert'=64] {'expert'}, dimensions={0} | all-to-all | bytes 1048576 | tf_op jit(solution)/shard_map/all_to_all | solution.py:292
  177.2 1.0 copy.85
  178.5 12.6 %all-gather.2 = bf16[8,18,2048]{2,1,0:T(8,128)(2,1)S(1)} all-gather(bf16[1,18,2048]{2,1,0:T(8,128)(2,1)S(1)} %bitcast.159), channel_id=3, replica_groups=mesh['dp'=8,'expert'=64] {'dp'}, dimensions={0}, use_global_device_ids=true | all-gather | bytes 663552 | tf_op jit(solution)/shard_map/all_gather | solution.py:306
  191.1 18.1 %all-gather.9.cloned.1.call-done = bf16[64,16,2048]{2,0,1:T(8,128)(2,1)} async-done(((bf16[64,2,2048]{2,0,1:T(8,128)(2,1)}), bf16[64,16,2048]{2,0,1:T(8,128)(2,1)}) %all-gather.9.cloned.1.call-update) | async-done | bytes 4194320 | tf_op jit(solution)/shard_map/all_gather | solution.py:299
  209.2 6.5 %copy.86 = bf16[64,16,2048]{2,1,0:T(8,128)(2,1)} copy(bf16[64,16,2048]{2,0,1:T(8,128)(2,1)} %all-gather.9.cloned.1.call-done) | data formatting | bytes 8388608 | tf_op jit(solution)/shard_map/all_gather | solution.py:299
  215.9 3.9 %fusion.27 = f32[1024,176]{0,1:T(8,128)S(1)} fusion(bf16[1024,2048]{1,0:T(8,128)(2,1)} %bitcast.148, bf16[1,2048,176]{1,2,0:T(8,128)(2,1)S(1)} %copy-done.17), kind=kOutput, calls=%fused_computation.36 | convolution fusion | flops 738197504 | bytes 5636096 | tf_op jit(solution)/shard_map/dot_general | solution.py:314
  219.8 2.3 fusion.2
  222.3 2.8 fusion.91
  225.2 2.7 reshape_reshape.12
  227.8 3.0 reshape_reshape.11
  230.8 3.0 reshape_reshape.10
  234.2 1.5 fusion.11
  235.7 14.2 %all-gather.3 = bf16[8,176,136]{1,2,0:T(8,128)(2,1)S(1)} all-gather(bf16[1,176,136]{1,2,0:T(8,128)(2,1)S(1)} %fusion.11), channel_id=1, replica_groups=mesh['dp'=8,'expert'=64] {'dp'}, dimensions={0}, use_global_device_ids=true | all-gather | bytes 430848 | tf_op jit(solution)/shard_map/all_gather | solution.py:326
  250.0 0.9 copy.88
  250.9 2.4 reshape.513
  253.3 4.5 %all-gather.7.cloned.1.call-done = bf16[1024,1408]{0,1:T(8,128)(2,1)} async-done(((bf16[1024,176]{0,1:T(8,128)(2,1)}), bf16[1024,1408]{0,1:T(8,128)(2,1)}) %all-gather.7.cloned.1.call-update) | async-done | bytes 2883600 | tf_op jit(solution)/shard_map/all_gather | solution.py:325
  257.8 3.7 %convolution_convert_fusion = bf16[1024,256]{1,0:T(8,128)(2,1)} fusion(bf16[1024,1408]{0,1:T(8,128)(2,1)} %all-gather.7.cloned.1.call-done, bf16[1,1408,256]{2,1,0:T(8,128)(2,1)S(1)} %copy-done), kind=kOutput, calls=%fused_computation.5 | convolution fusion | flops 738459648 | bytes 4128768 | tf_op jit(solution)/shard_map/dot_general | solution.py:328
  261.5 15.3 %all-to-all-start.2 = ((bf16[64,16,256]{2,1,0:T(8,128)(2,1)}), bf16[64,16,256]{2,1,0:T(8,128)(2,1)S(1)}, u32[]{:S(2)}, u32[]{:S(2)}) async-start(bf16[64,16,256]{2,1,0:T(8,128)(2,1)} %bitcast.34), calls=%async_computation.2 | async-start | bytes 1048576 | tf_op jit(solution)/shard_map/all_to_all | solution.py:332
  277.0 2.0 select_reduce_fusion
  280.1 1.3 fusion.33
  281.4 10.7 %gather_fusion.1 = f32[816]{0:T(1024)S(1)} fusion(f32[136,64]{0,1:T(8,128)S(1)} %fusion.33, s32[816]{0:T(1024)S(1)} %reshape.500), kind=kCustom, calls=%fused_computation.1 | custom fusion | bytes 13056 | tf_op jit(solution)/shard_map/jit(take_along_axis)/gather | solution.py:346
  292.5 14.3 %all-to-all-done.2 = bf16[64,16,256]{2,1,0:T(8,128)(2,1)S(1)} async-done(((bf16[64,16,256]{2,1,0:T(8,128)(2,1)}), bf16[64,16,256]{2,1,0:T(8,128)(2,1)S(1)}, u32[]{:S(2)}, u32[]{:S(2)}) %all-to-all-start.2) | async-done | bytes 524320 | tf_op jit(solution)/shard_map/all_to_all | solution.py:332
  306.8 3.4 %gather_fusion = bf16[816,256]{1,0:T(8,128)(2,1)S(1)} fusion(bf16[1024,256]{1,0:T(8,128)(2,1)S(1)} %bitcast.141, s32[1024]{0:T(1024)S(1)} %pad_clamp_fusion), kind=kCustom, calls=%fused_computation | custom fusion | bytes 838848 | tf_op jit(solution)/shard_map/jit(_take)/gather | solution.py:343
  311.3 10.8 %all_to_all.38 = bf16[8,17,256]{2,1,0:T(8,128)(2,1)S(1)} all-to-all(bf16[8,17,256]{2,1,0:T(8,128)(2,1)S(1)} %convert_element_type.222), channel_id=1, replica_groups=mesh['dp'=8,'expert'=64] {'dp'}, dimensions={0} | all-to-all | bytes 139264 | tf_op jit(solution)/shard_map/all_to_all | solution.py:352
  322.9 0.6 slice.92
  (127 shorter events, 10.9 us)
Async XLA Ops:
  7.2 250.7 %copy-start = (bf16[1,1408,256]{2,1,0:T(8,128)(2,1)S(1)}, bf16[1,1408,256]{2,1,0:T(8,128)(2,1)}, u32[]{:S(2)}) copy-start(bf16[1,1408,256]{2,1,0:T(8,128)(2,1)} %param.36) | copy-start | bytes 2162692
  7.2 8.5 %copy-start.5 = (bf16[1,1024,576]{1,2,0:T(8,128)(2,1)S(1)}, bf16[1,1024,576]{1,2,0:T(8,128)(2,1)}, u32[]{:S(2)}) copy-start(bf16[1,1024,576]{1,2,0:T(8,128)(2,1)} %param.27) | copy-start | bytes 3538948
  7.2 8.4 %copy-start.14 = (f32[16]{0:T(128)S(1)}, f32[16]{0:T(128)}, u32[]{:S(2)}) copy-start(f32[16]{0:T(128)} %param.28) | copy-start | bytes 196
  7.2 20.0 %copy-start.7 = (bf16[32,176]{1,0:T(8,128)(2,1)S(1)}, bf16[32,176]{1,0:T(8,128)(2,1)}, u32[]{:S(2)}) copy-start(bf16[32,176]{1,0:T(8,128)(2,1)} %param.37) | copy-start | bytes 33796
  7.2 20.1 %copy-start.8 = (bf16[32,176]{1,0:T(8,128)(2,1)S(1)}, bf16[32,176]{1,0:T(8,128)(2,1)}, u32[]{:S(2)}) copy-start(bf16[32,176]{1,0:T(8,128)(2,1)} %param.38) | copy-start | bytes 33796
  7.2 20.2 %copy-start.11 = (bf16[22,256]{1,0:T(8,128)(2,1)S(1)}, bf16[22,256]{1,0:T(8,128)(2,1)}, u32[]{:S(2)}) copy-start(bf16[22,256]{1,0:T(8,128)(2,1)} %param.39) | copy-start | bytes 33796
  7.2 20.3 %copy-start.9 = (bf16[2,2,2048]{2,1,0:T(2,128)(2,1)S(1)}, bf16[2,2,2048]{2,1,0:T(2,128)(2,1)}, u32[]{:S(2)}) copy-start(bf16[2,2,2048]{2,1,0:T(2,128)(2,1)} %param.30) | copy-start | bytes 49156
  7.2 20.3 %copy-start.16 = (bf16[2,8,128]{2,1,0:T(8,128)(2,1)S(1)}, bf16[2,8,128]{2,1,0:T(8,128)(2,1)}, u32[]{:S(2)}) copy-start(bf16[2,8,128]{2,1,0:T(8,128)(2,1)} %param.29) | copy-start | bytes 12292
  7.3 20.3 %copy-start.13 = (bf16[2048,1]{0,1:T(2,128)(2,1)S(1)}, bf16[2048,1]{0,1:T(2,128)(2,1)}, u32[]{:S(2)}) copy-start(bf16[2048,1]{0,1:T(2,128)(2,1)} %param.32) | copy-start | bytes 12292
  17.0 85.2 %all-to-all-start = ((bf16[17,16,512]{2,0,1:T(8,128)(2,1)}), bf16[17,16,512]{2,0,1:T(8,128)(2,1)S(1)}, u32[]{:S(2)}, u32[]{:S(2)}) async-start(bf16[17,16,512]{2,0,1:T(8,128)(2,1)} %copy.78), calls=%async_computation | async-start | bytes 786432 | tf_op jit(solution)/shard_map/all_to_all | solution.py:266
  27.2 182.0 %all-gather.9.cloned.1.call-start = ((), (), s32[]{:S(2)}) async-start(), calls=%async_computation.5 | async-start | bytes 4718592 | tf_op jit(solution)/shard_map/all_gather | solution.py:299
  93.4 2.5 copy-start.10
  93.9 1.9 copy-start.1
  98.0 38.3 %copy-start.6 = (bf16[16,2048]{1,0:T(8,128)(2,1)S(1)}, bf16[16,2048]{1,0:T(8,128)(2,1)}, u32[]{:S(2)}) copy-start(bf16[16,2048]{1,0:T(8,128)(2,1)} %param.22) | copy-start | bytes 196612
  99.7 34.0 %copy-start.15 = (bf16[2048]{0:T(1024)(128)(2,1)S(1)}, bf16[2048]{0:T(1024)(128)(2,1)}, u32[]{:S(2)}) copy-start(bf16[2048]{0:T(1024)(128)(2,1)} %param.31) | copy-start | bytes 12292
  99.7 36.6 %copy-start.12 = (bf16[1,2048]{1,0:T(2,128)(2,1)S(1)}, bf16[1,2048]{1,0:T(2,128)(2,1)}, u32[]{:S(2)}) copy-start(bf16[1,2048]{1,0:T(2,128)(2,1)} %param.25) | copy-start | bytes 12292
  124.8 10.9 %collective-permute-start.1 = (bf16[24,2048]{1,0:T(8,128)(2,1)S(1)}, bf16[24,2048]{1,0:T(8,128)(2,1)S(1)}, u32[]{:S(2)}, u32[]{:S(2)}) collective-permute-start(bf16[24,2048]{1,0:T(8,128)(2,1)S(1)} %fusion), channel_id=1, source_target_pairs={{0,128},{64,192},{128,256},{192,320},{256,384},{320,448},{1,129},{... | collective-permute-start | bytes 294920
  126.1 9.6 %collective-permute-start = (bf16[24,2048]{1,0:T(8,128)(2,1)S(1)}, bf16[24,2048]{1,0:T(8,128)(2,1)S(1)}, u32[]{:S(2)}, u32[]{:S(2)}) collective-permute-start(bf16[24,2048]{1,0:T(8,128)(2,1)S(1)} %fusion), channel_id=1, source_target_pairs={{0,64},{64,128},{128,192},{192,256},{256,320},{320,384},{384,448},... | collective-permute-start | bytes 294920
  129.6 6.1 %collective-permute-start.2 = (bf16[1,2048]{1,0:T(2,128)(2,1)S(1)}, bf16[1,2048]{1,0:T(2,128)(2,1)S(1)}, u32[]{:S(2)}, u32[]{:S(2)}) collective-permute-start(bf16[1,2048]{1,0:T(2,128)(2,1)S(1)} %slice.94), channel_id=1, source_target_pairs={{0,192},{64,256},{128,320},{192,384},{256,448},{1,193},{65,257},{1... | collective-permute-start | bytes 12296
  178.2 79.6 %all-gather.7.cloned.1.call-start = ((), (), s32[]{:S(2)}) async-start(), calls=%async_computation.4 | async-start | bytes 3244032 | tf_op jit(solution)/shard_map/all_gather | solution.py:325
  191.1 24.8 %copy-start.17 = (bf16[1,2048,176]{1,2,0:T(8,128)(2,1)S(1)}, bf16[1,2048,176]{1,2,0:T(8,128)(2,1)}, u32[]{:S(2)}) copy-start(bf16[1,2048,176]{1,2,0:T(8,128)(2,1)} %param.34) | copy-start | bytes 2162692
  215.9 3.9 %copy-start.2 = (bf16[64,16,2048]{2,1,0:T(8,128)(2,1)S(1)}, bf16[64,16,2048]{2,1,0:T(8,128)(2,1)}, u32[]{:S(2)}) copy-start(bf16[64,16,2048]{2,1,0:T(8,128)(2,1)} %copy.86) | copy-start | bytes 12582916
  215.9 3.9 %copy-start.18 = (bf16[1,2048,176]{1,2,0:T(8,128)(2,1)S(1)}, bf16[1,2048,176]{1,2,0:T(8,128)(2,1)}, u32[]{:S(2)}) copy-start(bf16[1,2048,176]{1,2,0:T(8,128)(2,1)} %param.35) | copy-start | bytes 2162692
  261.5 45.3 %all-to-all-start.2 = ((bf16[64,16,256]{2,1,0:T(8,128)(2,1)}), bf16[64,16,256]{2,1,0:T(8,128)(2,1)S(1)}, u32[]{:S(2)}, u32[]{:S(2)}) async-start(bf16[64,16,256]{2,1,0:T(8,128)(2,1)} %bitcast.34), calls=%async_computation.2 | async-start | bytes 1048576 | tf_op jit(solution)/shard_map/all_to_all | solution.py:332
  292.1 18.8 %copy-start.3 = (bf16[1408,256]{1,0:T(8,128)(2,1)S(1)}, bf16[1408,256]{1,0:T(8,128)(2,1)}, u32[]{:S(2)}) copy-start(bf16[1408,256]{1,0:T(8,128)(2,1)} %reshape_reshape.12) | copy-start | bytes 2162692
  292.1 18.8 %copy-start.4 = (bf16[1408,136]{0,1:T(8,128)(2,1)S(1)}, bf16[1408,136]{0,1:T(8,128)(2,1)}, u32[]{:S(2)}) copy-start(bf16[1408,136]{0,1:T(8,128)(2,1)} %reshape.513) | copy-start | bytes 1148932
Sparse Core Ops, SparseCore 0:
  178.3 30.8 all-gather.8
  222.3 35.4 all-gather.6

commit v13 on v10

--- a/solution.py
+++ b/solution.py
@@ -296,9 +296,7 @@
         weights["shared_down"],
         weights["router"],
     )
-    expert_rows = lax.all_gather(
-        arrived.reshape(members, 1, capacity, D), "dp", axis=1, tiled=True
-    )
+    expert_rows = lax.all_gather(arrived[None], "dp", axis=0, tiled=True)
     expert_rows = expert_rows.reshape(-1, D)
     own_both, _ = lax.optimization_barrier(
         (jnp.concatenate([normed, route_row], axis=0), arrived)
@@ -327,6 +325,7 @@
     shared_cols = jnp.dot(shared_piece, shared_down_full, preferred_element_type=jnp.float32)
     expert_out = routed_cols.astype(jnp.bfloat16)
     shared_out = shared_cols.astype(jnp.bfloat16)
+    expert_out = jnp.swapaxes(expert_out.reshape(groups, members, capacity, col_width), 0, 1)
     returned = lax.all_to_all(
         expert_out.reshape(members, groups * capacity, col_width),
         "expert",

time: 327 us -> 334 us (1.021)
  local copies, waits for them, and re-layouts: 51.7 us -> 55.8 us
    reshape x0 -> x4, local copies, waits for them, and re-layouts: none -> 9.6 us  [the longest x1 7.2 us: shards(): expert_rows = expert_rows.reshape(-1, D)]
    all_gather x1 -> x0, local copies, waits for them, and re-layouts: 4.49 us -> none  [shards(): lax.all_gather(arrived.reshape(members, 1, capacity, D), 'dp', axis=1, ti...]
    unnamed x52 -> x54, local copies, waits for them, and re-layouts: 6.87 us -> 6.94 us
  transfers between devices with their start and end apart: 7 -> 7, of which waited for: 2 -> 2; matrix products, arithmetic and copies ran while one was open for 13% -> 13% of each run, Pallas kernels for 19% -> 18%
where the time goes in v13:
time: 334 us; the launch traced here: 333 us
  blocking collectives  97 us (29%)
  Pallas kernels  61.4 us (18%)
  local copies, waits for them, and re-layouts  55.8 us (17%)
  waiting for transfers between devices  40 us (12%)
  starting transfers between devices  34.7 us (10%)
  matrix products  20.8 us (6%)
  between operations  16.3 us (5%)
  other arithmetic  6.65 us (2%)
    pallas_call x1, Pallas kernels, expert_gather(): pl.pallas_call(partial(gather_kernel, nx, nz), out_shape=jax.ShapeDtypeSt...  61.4 us
    all_to_all x1, blocking collectives, shards(): lax.all_to_all(outgoing, 'expert', split_axis=0, concat_axis=0, tiled=True)  39.7 us
    unnamed x1, blocking collectives  21.8 us
    all_gather x1, waiting for transfers between devices, shards(): routed_piece = lax.all_gather(expert_act, 'dp', axis=1, tiled=True)  21.8 us
    all_gather x1, waiting for transfers between devices, shards(): expert_rows = lax.all_gather(arrived[None], 'dp', axis=0, tiled=True)  18.1 us
    all_to_all x1, starting transfers between devices, shards(): lax.all_to_all(expert_out.reshape(members, groups * capacity, col_width),...  15.5 us
    all_gather x1, blocking collectives, shards(): shared_piece = lax.all_gather(shared_act, 'dp', axis=1, tiled=True)  13.5 us
    all_gather x1, blocking collectives, shards(): group_both = lax.all_gather(own_both[None], 'dp', axis=0, tiled=True)  12.6 us
  transfers between devices with their start and end apart: 7, of which 2 were waited for; matrix products, arithmetic and copies ran while one was open for 13% of the time, Pallas kernels for 18%

profile of v13, /device:TPU:1, one launch (start us, length us, event | category | flops | bytes accessed | tf_op | source)
XLA Modules:
  0.0 332.7 jit_solution(1016783768882409869)
XLA Ops:
  8.0 0.7 slice_convert_fusion.1
  8.7 1.7 fusion.92
  10.4 0.9 convert_convert_fusion
  11.3 1.6 fusion.93
  12.9 0.7 broadcast_maximum_fusion
  13.7 0.7 exponential_add_fusion
  14.3 1.1 fusion.3
  16.1 0.9 copy.98
  17.0 10.2 %all-to-all-start = ((bf16[17,16,512]{2,0,1:T(8,128)(2,1)}), bf16[17,16,512]{2,0,1:T(8,128)(2,1)S(1)}, u32[]{:S(2)}, u32[]{:S(2)}) async-start(bf16[17,16,512]{2,0,1:T(8,128)(2,1)} %copy.98), calls=%async_computation | async-start | bytes 786432 | tf_op jit(solution)/shard_map/all_to_all | solution.py:266
  29.6 61.4 %shard_map.203 = bf16[16,4,232,128]{3,2,1,0:T(8,128)(2,1)} custom-call(bf16[232,128]{1,0:T(8,128)(2,1)} %pad_bitcast_fusion.shard_ref), custom_call_target="tpu_custom_call" | custom-call | tf_op jit(solution)/shard_map/pallas_call | solution.py:137
  91.0 2.3 copy.95
  93.9 1.8 copy-done.1
  96.5 0.7 sub.97
  97.2 0.8 reshape.476
  98.0 1.7 copy.101
  99.7 1.5 reshape.477
  101.2 0.7 multiply_add_fusion
  102.9 21.8 %fusion = bf16[24,2048]{1,0:T(8,128)(2,1)S(1)} fusion(bf16[136,2048]{1,0:T(8,128)(2,1)S(1)} %fusion.1), kind=kCustom, calls=%all-reduce-scatter | all-reduce-scatter fusion | flops 393217 | bytes 657408
  124.8 1.3 collective-permute-start.1
  126.1 3.5 %collective-permute-start = (bf16[24,2048]{1,0:T(8,128)(2,1)S(1)}, bf16[24,2048]{1,0:T(8,128)(2,1)S(1)}, u32[]{:S(2)}, u32[]{:S(2)}) collective-permute-start(bf16[24,2048]{1,0:T(8,128)(2,1)S(1)} %fusion), channel_id=1, source_target_pairs={{0,64},{64,128},{128,192},{192,256},{256,320},{320,384},{384,448},... | collective-permute-start | bytes 294920
  129.6 4.1 %collective-permute-start.2 = (bf16[1,2048]{1,0:T(2,128)(2,1)S(1)}, bf16[1,2048]{1,0:T(2,128)(2,1)S(1)}, u32[]{:S(2)}, u32[]{:S(2)}) collective-permute-start(bf16[1,2048]{1,0:T(2,128)(2,1)S(1)} %slice.94), channel_id=1, source_target_pairs={{0,192},{64,256},{128,320},{192,384},{256,448},{1,193},{65,257},{1... | collective-permute-start | bytes 12296
  133.7 1.3 dynamic-slice.4
  137.6 39.7 %all_to_all.37 = bf16[64,2,2048]{2,1,0:T(2,128)(2,1)} all-to-all(bf16[64,2,2048]{2,1,0:T(2,128)(2,1)S(1)} %copy.104), channel_id=1, replica_groups=mesh['dp'=8,'expert'=64] {'expert'}, dimensions={0} | all-to-all | bytes 1048576 | tf_op jit(solution)/shard_map/all_to_all | solution.py:292
  177.6 12.6 %all-gather.2 = bf16[8,18,2048]{2,1,0:T(8,128)(2,1)S(1)} all-gather(bf16[1,18,2048]{2,1,0:T(8,128)(2,1)S(1)} %bitcast.157), channel_id=3, replica_groups=mesh['dp'=8,'expert'=64] {'dp'}, dimensions={0}, use_global_device_ids=true | all-gather | bytes 663552 | tf_op jit(solution)/shard_map/all_gather | solution.py:304
  190.3 18.1 %all-gather.9.cloned.1.call-done = bf16[512,2,2048]{2,1,0:T(2,128)(2,1)} async-done(((bf16[64,2,2048]{2,1,0:T(2,128)(2,1)}), bf16[512,2,2048]{2,1,0:T(2,128)(2,1)}) %all-gather.9.cloned.1.call-update) | async-done | bytes 4194320 | tf_op jit(solution)/shard_map/all_gather | solution.py:299
  208.4 7.2 %reshape.478 = bf16[1024,2048]{1,0:T(8,128)(2,1)} reshape(bf16[512,2,2048]{2,1,0:T(2,128)(2,1)} %all-gather.9.cloned.1.call-done) | data formatting | bytes 8388608 | tf_op jit(solution)/shard_map/reshape | solution.py:300
  215.6 3.9 %fusion.27 = f32[1024,176]{0,1:T(8,128)S(1)} fusion(bf16[1024,2048]{1,0:T(8,128)(2,1)} %reshape.478, bf16[1,2048,176]{1,2,0:T(8,128)(2,1)S(1)} %copy-done.17), kind=kOutput, calls=%fused_computation.36 | convolution fusion | flops 738197504 | bytes 5636096 | tf_op jit(solution)/shard_map/dot_general | solution.py:312
  219.5 2.4 fusion.2
  222.0 2.5 fusion.91
  224.6 1.7 reshape_reshape.12
  226.3 3.0 reshape_reshape.11
  229.3 3.0 reshape_reshape.10
  232.5 2.0 select_reduce_fusion
  234.6 21.8 %all-gather.7.cloned.1.call-done = bf16[1024,1408]{0,1:T(8,128)(2,1)} async-done(((bf16[1024,176]{0,1:T(8,128)(2,1)}), bf16[1024,1408]{0,1:T(8,128)(2,1)}) %all-gather.7.cloned.1.call-update) | async-done | bytes 2883600 | tf_op jit(solution)/shard_map/all_gather | solution.py:322
  256.4 3.6 %convolution_convert_fusion = bf16[1024,256]{1,0:T(8,128)(2,1)} fusion(bf16[1024,1408]{0,1:T(8,128)(2,1)} %all-gather.7.cloned.1.call-done, bf16[1,1408,256]{2,1,0:T(8,128)(2,1)S(1)} %copy-done), kind=kOutput, calls=%fused_computation.5 | convolution fusion | flops 738459648 | bytes 4128768 | tf_op jit(solution)/shard_map/dot_general | solution.py:324
  260.1 1.2 reshape.483
  261.4 1.1 copy.118
  262.5 15.5 %all-to-all-start.2 = ((bf16[64,16,256]{2,1,0:T(8,128)(2,1)}), bf16[64,16,256]{2,1,0:T(8,128)(2,1)S(1)}, u32[]{:S(2)}, u32[]{:S(2)}) async-start(bf16[64,16,256]{2,1,0:T(8,128)(2,1)} %copy.118), calls=%async_computation.2 | async-start | bytes 1048576 | tf_op jit(solution)/shard_map/all_to_all | solution.py:329
  279.1 1.3 reshape.480
  280.5 1.3 fusion.33
  281.7 10.7 %gather_fusion.1 = f32[816]{0:T(1024)S(1)} fusion(f32[136,64]{0,1:T(8,128)S(1)} %fusion.33, s32[816]{0:T(1024)S(1)} %reshape.500), kind=kCustom, calls=%fused_computation.1 | custom fusion | bytes 13056 | tf_op jit(solution)/shard_map/jit(take_along_axis)/gather | solution.py:343
  293.1 1.5 fusion.11
  294.7 13.5 %all-gather.3 = bf16[8,176,136]{1,2,0:T(8,128)(2,1)S(1)} all-gather(bf16[1,176,136]{1,2,0:T(8,128)(2,1)S(1)} %fusion.11), channel_id=1, replica_groups=mesh['dp'=8,'expert'=64] {'dp'}, dimensions={0}, use_global_device_ids=true | all-gather | bytes 430848 | tf_op jit(solution)/shard_map/all_gather | solution.py:323
  308.3 1.3 reshape.513
  309.6 3.4 %gather_fusion = bf16[816,256]{1,0:T(8,128)(2,1)S(1)} fusion(bf16[1024,256]{1,0:T(8,128)(2,1)S(1)} %bitcast.141, s32[1024]{0:T(1024)S(1)} %pad_clamp_fusion), kind=kCustom, calls=%fused_computation | custom fusion | bytes 838848 | tf_op jit(solution)/shard_map/jit(_take)/gather | solution.py:340
  313.7 1.3 fusion.10
  315.0 9.3 %all_to_all.38 = bf16[8,17,256]{2,1,0:T(8,128)(2,1)S(1)} all-to-all(bf16[8,17,256]{2,1,0:T(8,128)(2,1)S(1)} %convert_element_type.222), channel_id=1, replica_groups=mesh['dp'=8,'expert'=64] {'dp'}, dimensions={0} | all-to-all | bytes 139264 | tf_op jit(solution)/shard_map/all_to_all | solution.py:349
  325.2 0.6 slice.92
  (129 shorter events, 11.2 us)
Async XLA Ops:
  7.2 249.2 %copy-start = (bf16[1,1408,256]{2,1,0:T(8,128)(2,1)S(1)}, bf16[1,1408,256]{2,1,0:T(8,128)(2,1)}, u32[]{:S(2)}) copy-start(bf16[1,1408,256]{2,1,0:T(8,128)(2,1)} %param.36) | copy-start | bytes 2162692
  7.2 8.5 %copy-start.5 = (bf16[1,1024,576]{1,2,0:T(8,128)(2,1)S(1)}, bf16[1,1024,576]{1,2,0:T(8,128)(2,1)}, u32[]{:S(2)}) copy-start(bf16[1,1024,576]{1,2,0:T(8,128)(2,1)} %param.27) | copy-start | bytes 3538948
  7.2 8.4 %copy-start.14 = (f32[16]{0:T(128)S(1)}, f32[16]{0:T(128)}, u32[]{:S(2)}) copy-start(f32[16]{0:T(128)} %param.28) | copy-start | bytes 196
  7.2 20.0 %copy-start.7 = (bf16[32,176]{1,0:T(8,128)(2,1)S(1)}, bf16[32,176]{1,0:T(8,128)(2,1)}, u32[]{:S(2)}) copy-start(bf16[32,176]{1,0:T(8,128)(2,1)} %param.37) | copy-start | bytes 33796
  7.2 20.1 %copy-start.8 = (bf16[32,176]{1,0:T(8,128)(2,1)S(1)}, bf16[32,176]{1,0:T(8,128)(2,1)}, u32[]{:S(2)}) copy-start(bf16[32,176]{1,0:T(8,128)(2,1)} %param.38) | copy-start | bytes 33796
  7.2 20.2 %copy-start.11 = (bf16[22,256]{1,0:T(8,128)(2,1)S(1)}, bf16[22,256]{1,0:T(8,128)(2,1)}, u32[]{:S(2)}) copy-start(bf16[22,256]{1,0:T(8,128)(2,1)} %param.39) | copy-start | bytes 33796
  7.2 20.3 %copy-start.9 = (bf16[2,2,2048]{2,1,0:T(2,128)(2,1)S(1)}, bf16[2,2,2048]{2,1,0:T(2,128)(2,1)}, u32[]{:S(2)}) copy-start(bf16[2,2,2048]{2,1,0:T(2,128)(2,1)} %param.30) | copy-start | bytes 49156
  7.2 20.3 %copy-start.16 = (bf16[2,8,128]{2,1,0:T(8,128)(2,1)S(1)}, bf16[2,8,128]{2,1,0:T(8,128)(2,1)}, u32[]{:S(2)}) copy-start(bf16[2,8,128]{2,1,0:T(8,128)(2,1)} %param.29) | copy-start | bytes 12292
  7.3 20.3 %copy-start.13 = (bf16[2048,1]{0,1:T(2,128)(2,1)S(1)}, bf16[2048,1]{0,1:T(2,128)(2,1)}, u32[]{:S(2)}) copy-start(bf16[2048,1]{0,1:T(2,128)(2,1)} %param.32) | copy-start | bytes 12292
  17.0 85.2 %all-to-all-start = ((bf16[17,16,512]{2,0,1:T(8,128)(2,1)}), bf16[17,16,512]{2,0,1:T(8,128)(2,1)S(1)}, u32[]{:S(2)}, u32[]{:S(2)}) async-start(bf16[17,16,512]{2,0,1:T(8,128)(2,1)} %copy.98), calls=%async_computation | async-start | bytes 786432 | tf_op jit(solution)/shard_map/all_to_all | solution.py:266
  27.2 181.1 %all-gather.9.cloned.1.call-start = ((), (), s32[]{:S(2)}) async-start(), calls=%async_computation.5 | async-start | bytes 4718592 | tf_op jit(solution)/shard_map/all_gather | solution.py:299
  93.4 2.5 copy-start.10
  93.9 1.9 copy-start.1
  98.0 38.3 %copy-start.6 = (bf16[16,2048]{1,0:T(8,128)(2,1)S(1)}, bf16[16,2048]{1,0:T(8,128)(2,1)}, u32[]{:S(2)}) copy-start(bf16[16,2048]{1,0:T(8,128)(2,1)} %param.22) | copy-start | bytes 196612
  99.7 34.0 %copy-start.15 = (bf16[2048]{0:T(1024)(128)(2,1)S(1)}, bf16[2048]{0:T(1024)(128)(2,1)}, u32[]{:S(2)}) copy-start(bf16[2048]{0:T(1024)(128)(2,1)} %param.31) | copy-start | bytes 12292
  99.7 36.6 %copy-start.12 = (bf16[1,2048]{1,0:T(2,128)(2,1)S(1)}, bf16[1,2048]{1,0:T(2,128)(2,1)}, u32[]{:S(2)}) copy-start(bf16[1,2048]{1,0:T(2,128)(2,1)} %param.25) | copy-start | bytes 12292
  124.8 10.9 %collective-permute-start.1 = (bf16[24,2048]{1,0:T(8,128)(2,1)S(1)}, bf16[24,2048]{1,0:T(8,128)(2,1)S(1)}, u32[]{:S(2)}, u32[]{:S(2)}) collective-permute-start(bf16[24,2048]{1,0:T(8,128)(2,1)S(1)} %fusion), channel_id=1, source_target_pairs={{0,128},{64,192},{128,256},{192,320},{256,384},{320,448},{1,129},{... | collective-permute-start | bytes 294920
  126.1 9.6 %collective-permute-start = (bf16[24,2048]{1,0:T(8,128)(2,1)S(1)}, bf16[24,2048]{1,0:T(8,128)(2,1)S(1)}, u32[]{:S(2)}, u32[]{:S(2)}) collective-permute-start(bf16[24,2048]{1,0:T(8,128)(2,1)S(1)} %fusion), channel_id=1, source_target_pairs={{0,64},{64,128},{128,192},{192,256},{256,320},{320,384},{384,448},... | collective-permute-start | bytes 294920
  129.6 6.1 %collective-permute-start.2 = (bf16[1,2048]{1,0:T(2,128)(2,1)S(1)}, bf16[1,2048]{1,0:T(2,128)(2,1)S(1)}, u32[]{:S(2)}, u32[]{:S(2)}) collective-permute-start(bf16[1,2048]{1,0:T(2,128)(2,1)S(1)} %slice.94), channel_id=1, source_target_pairs={{0,192},{64,256},{128,320},{192,384},{256,448},{1,193},{65,257},{1... | collective-permute-start | bytes 12296
  177.4 79.0 %all-gather.7.cloned.1.call-start = ((), (), s32[]{:S(2)}) async-start(), calls=%async_computation.4 | async-start | bytes 3244032 | tf_op jit(solution)/shard_map/all_gather | solution.py:322
  190.2 88.0 %copy-start.3 = (bf16[8,18,2048]{2,1,0:T(8,128)(2,1)}, bf16[8,18,2048]{2,1,0:T(8,128)(2,1)S(1)}, u32[]{:S(2)}) copy-start(bf16[8,18,2048]{2,1,0:T(8,128)(2,1)S(1)} %all-gather.2) | copy-start | bytes 1769476
  190.3 25.3 %copy-start.17 = (bf16[1,2048,176]{1,2,0:T(8,128)(2,1)S(1)}, bf16[1,2048,176]{1,2,0:T(8,128)(2,1)}, u32[]{:S(2)}) copy-start(bf16[1,2048,176]{1,2,0:T(8,128)(2,1)} %param.34) | copy-start | bytes 2162692
  215.6 3.9 %copy-start.2 = (bf16[1024,2048]{1,0:T(8,128)(2,1)S(1)}, bf16[1024,2048]{1,0:T(8,128)(2,1)}, u32[]{:S(2)}) copy-start(bf16[1024,2048]{1,0:T(8,128)(2,1)} %reshape.478) | copy-start | bytes 12582916
  215.6 3.9 %copy-start.18 = (bf16[1,2048,176]{1,2,0:T(8,128)(2,1)S(1)}, bf16[1,2048,176]{1,2,0:T(8,128)(2,1)}, u32[]{:S(2)}) copy-start(bf16[1,2048,176]{1,2,0:T(8,128)(2,1)} %param.35) | copy-start | bytes 2162692
  262.5 47.1 %all-to-all-start.2 = ((bf16[64,16,256]{2,1,0:T(8,128)(2,1)}), bf16[64,16,256]{2,1,0:T(8,128)(2,1)S(1)}, u32[]{:S(2)}, u32[]{:S(2)}) async-start(bf16[64,16,256]{2,1,0:T(8,128)(2,1)} %copy.118), calls=%async_computation.2 | async-start | bytes 1048576 | tf_op jit(solution)/shard_map/all_to_all | solution.py:329
  308.3 5.4 %copy-start.4 = (bf16[1408,256]{1,0:T(8,128)(2,1)S(1)}, bf16[1408,256]{1,0:T(8,128)(2,1)}, u32[]{:S(2)}) copy-start(bf16[1408,256]{1,0:T(8,128)(2,1)} %reshape_reshape.12) | copy-start | bytes 2162692
Sparse Core Ops, SparseCore 0:
  177.5 30.8 all-gather.8
  222.0 34.3 all-gather.6

commit v14 on v10

--- a/solution.py
+++ b/solution.py
@@ -65,14 +65,14 @@
     if greeted:
         pl.semaphore_wait(barrier, greeted)
 
-    own = pltpu.make_async_copy(shard_ref, out_ref.at[z, x], own_sem)
+    own = pltpu.make_async_copy(shard_ref, out_ref.at[x, z], own_sem)
     own.start()
     x_copies = []
     for k in range(1, nx):
         px = (x + k) % nx
         send = pltpu.make_async_remote_copy(
             src_ref=shard_ref,
-            dst_ref=out_ref.at[z, x],
+            dst_ref=out_ref.at[x, z],
             send_sem=xs_sem.at[k],
             recv_sem=xr_sem.at[x],
             device_id=(d, px * nz + z),
@@ -85,7 +85,7 @@
         px = (x + k) % nx
         incoming = pltpu.make_async_remote_copy(
             src_ref=shard_ref,
-            dst_ref=out_ref.at[z, px],
+            dst_ref=out_ref.at[px, z],
             send_sem=xs_sem.at[k],
             recv_sem=xr_sem.at[px],
             device_id=(d, px * nz + z),
@@ -95,8 +95,8 @@
 
     def ring_copy(group, sems, step, target):
         return pltpu.make_async_remote_copy(
-            src_ref=out_ref.at[group],
-            dst_ref=out_ref.at[group],
+            src_ref=out_ref.at[:, group],
+            dst_ref=out_ref.at[:, group],
             send_sem=sems.at[step],
             recv_sem=rr_sem.at[group],
             device_id=(d, target),
@@ -136,7 +136,7 @@
     steps = max(nz // 2, 1)
     out = pl.pallas_call(
         partial(gather_kernel, nx, nz),
-        out_shape=jax.ShapeDtypeStruct((nz, nx, rows, lanes), flat.dtype),
+        out_shape=jax.ShapeDtypeStruct((nx, nz, rows, lanes), flat.dtype),
         in_specs=[pl.BlockSpec(memory_space=pltpu.VMEM)],
         out_specs=pl.BlockSpec(memory_space=pltpu.VMEM),
         scratch_shapes=[
@@ -149,7 +149,7 @@
         ],
         compiler_params=pltpu.CompilerParams(collective_id=0, has_side_effects=True),
     )(flat)
-    return jnp.swapaxes(out, 0, 1).reshape(members, rows * lanes)
+    return out.reshape(members, rows * lanes)
 
 
 def gather_weights(members, by_kernel, **parts):

time: 327 us -> 327 us (level)
    transpose x2 -> x0, local copies, waits for them, and re-layouts: 4.04 us -> none  [the longest x1 2.34 us: expert_gather(): return jnp.swapaxes(out, 0, 1).reshape(members, rows * lanes)]
where the time goes in v14:
time: 327 us; the launch traced here: 326 us
  blocking collectives  97.1 us (30%)
  Pallas kernels  61.4 us (19%)
  local copies, waits for them, and re-layouts  51.6 us (16%)
  waiting for transfers between devices  40 us (12%)
  starting transfers between devices  34.5 us (11%)
  matrix products  18.5 us (6%)
  between operations  16.3 us (5%)
  other arithmetic  6.65 us (2%)
    pallas_call x1, Pallas kernels, expert_gather(): pl.pallas_call(partial(gather_kernel, nx, nz), out_shape=jax.ShapeDtypeSt...  61.4 us
    all_to_all x1, blocking collectives, shards(): lax.all_to_all(outgoing, 'expert', split_axis=0, concat_axis=0, tiled=True)  39.6 us
    unnamed x1, blocking collectives  21.8 us
    all_gather x1, waiting for transfers between devices, shards(): routed_piece = lax.all_gather(expert_act, 'dp', axis=1, tiled=True)  21.8 us
    all_gather x1, waiting for transfers between devices, shards(): lax.all_gather(arrived.reshape(members, 1, capacity, D), 'dp', axis=1, ti...  18.1 us
    all_to_all x1, starting transfers between devices, shards(): lax.all_to_all(expert_out.reshape(members, groups * capacity, col_width),...  15.3 us
    all_gather x1, blocking collectives, shards(): shared_piece = lax.all_gather(shared_act, 'dp', axis=1, tiled=True)  13.5 us
    all_gather x1, blocking collectives, shards(): group_both = lax.all_gather(own_both[None], 'dp', axis=0, tiled=True)  12.6 us
  transfers between devices with their start and end apart: 7, of which 2 were waited for; matrix products, arithmetic and copies ran while one was open for 13% of the time, Pallas kernels for 19%

profile of v14, /device:TPU:1, one launch (start us, length us, event | category | flops | bytes accessed | tf_op | source)
XLA Modules:
  0.0 325.9 jit_solution(13217523383292141012)
XLA Ops:
  8.0 0.7 slice_convert_fusion.1
  8.7 1.7 fusion.92
  10.4 0.9 convert_convert_fusion
  11.3 1.6 fusion.93
  12.9 0.7 broadcast_maximum_fusion
  13.7 0.7 exponential_add_fusion
  14.3 1.1 fusion.3
  16.1 0.9 copy.86
  17.0 10.2 %all-to-all-start = ((bf16[17,16,512]{2,0,1:T(8,128)(2,1)}), bf16[17,16,512]{2,0,1:T(8,128)(2,1)S(1)}, u32[]{:S(2)}, u32[]{:S(2)}) async-start(bf16[17,16,512]{2,0,1:T(8,128)(2,1)} %copy.86), calls=%async_computation | async-start | bytes 786432 | tf_op jit(solution)/shard_map/all_to_all | solution.py:266
  29.0 0.6 pad_bitcast_fusion.shard_ref
  29.6 61.4 %shard_map.203 = bf16[4,16,232,128]{3,2,1,0:T(8,128)(2,1)} custom-call(bf16[232,128]{1,0:T(8,128)(2,1)} %pad_bitcast_fusion.shard_ref), custom_call_target="tpu_custom_call" | custom-call | tf_op jit(solution)/shard_map/pallas_call | solution.py:137
  91.0 2.7 copy.124
  93.8 1.8 copy-done.1
  96.3 0.7 sub.97
  97.0 0.8 reshape.476
  97.8 1.7 copy.125
  99.5 1.5 reshape.477
  101.0 0.7 multiply_add_fusion
  102.7 21.8 %fusion = bf16[24,2048]{1,0:T(8,128)(2,1)S(1)} fusion(bf16[136,2048]{1,0:T(8,128)(2,1)S(1)} %fusion.1), kind=kCustom, calls=%all-reduce-scatter | all-reduce-scatter fusion | flops 393217 | bytes 657408
  124.6 1.3 collective-permute-start.1
  125.9 3.5 %collective-permute-start = (bf16[24,2048]{1,0:T(8,128)(2,1)S(1)}, bf16[24,2048]{1,0:T(8,128)(2,1)S(1)}, u32[]{:S(2)}, u32[]{:S(2)}) collective-permute-start(bf16[24,2048]{1,0:T(8,128)(2,1)S(1)} %fusion), channel_id=1, source_target_pairs={{0,64},{64,128},{128,192},{192,256},{256,320},{320,384},{384,448},... | collective-permute-start | bytes 294920
  129.3 4.1 %collective-permute-start.2 = (bf16[1,2048]{1,0:T(2,128)(2,1)S(1)}, bf16[1,2048]{1,0:T(2,128)(2,1)S(1)}, u32[]{:S(2)}, u32[]{:S(2)}) collective-permute-start(bf16[1,2048]{1,0:T(2,128)(2,1)S(1)} %slice.94), channel_id=1, source_target_pairs={{0,192},{64,256},{128,320},{192,384},{256,448},{1,193},{65,257},{1... | collective-permute-start | bytes 12296
  133.5 1.3 dynamic-slice.4
  137.4 39.6 %all_to_all.37 = bf16[64,2,2048]{2,1,0:T(2,128)(2,1)S(1)} all-to-all(bf16[64,2,2048]{2,1,0:T(2,128)(2,1)S(1)} %copy.92), channel_id=1, replica_groups=mesh['dp'=8,'expert'=64] {'expert'}, dimensions={0} | all-to-all | bytes 1048576 | tf_op jit(solution)/shard_map/all_to_all | solution.py:292
  177.0 1.0 copy.93
  178.3 12.6 %all-gather.2 = bf16[8,18,2048]{2,1,0:T(8,128)(2,1)S(1)} all-gather(bf16[1,18,2048]{2,1,0:T(8,128)(2,1)S(1)} %bitcast.158), channel_id=3, replica_groups=mesh['dp'=8,'expert'=64] {'dp'}, dimensions={0}, use_global_device_ids=true | all-gather | bytes 663552 | tf_op jit(solution)/shard_map/all_gather | solution.py:306
  190.9 18.1 %all-gather.9.cloned.1.call-done = bf16[64,16,2048]{2,0,1:T(8,128)(2,1)} async-done(((bf16[64,2,2048]{2,0,1:T(8,128)(2,1)}), bf16[64,16,2048]{2,0,1:T(8,128)(2,1)}) %all-gather.9.cloned.1.call-update) | async-done | bytes 4194320 | tf_op jit(solution)/shard_map/all_gather | solution.py:299
  209.1 4.5 %copy.94 = bf16[64,16,2048]{2,1,0:T(8,128)(2,1)S(1)} copy(bf16[64,16,2048]{2,0,1:T(8,128)(2,1)} %all-gather.9.cloned.1.call-done) | data formatting | bytes 8388608 | tf_op jit(solution)/shard_map/all_gather | solution.py:299
  213.6 1.5 fusion.27
  215.1 2.4 fusion.2
  217.7 2.5 fusion.91
  220.2 1.8 reshape_reshape.12
  222.0 3.0 reshape_reshape.11
  225.0 3.0 reshape_reshape.10
  228.2 2.0 select_reduce_fusion
  230.3 21.8 %all-gather.7.cloned.1.call-done = bf16[1024,1408]{0,1:T(8,128)(2,1)} async-done(((bf16[1024,176]{0,1:T(8,128)(2,1)}), bf16[1024,1408]{0,1:T(8,128)(2,1)}) %all-gather.7.cloned.1.call-update) | async-done | bytes 2883600 | tf_op jit(solution)/shard_map/all_gather | solution.py:324
  252.1 3.7 %convolution_convert_fusion = bf16[1024,256]{1,0:T(8,128)(2,1)} fusion(bf16[1024,1408]{0,1:T(8,128)(2,1)} %all-gather.7.cloned.1.call-done, bf16[1,1408,256]{2,1,0:T(8,128)(2,1)S(1)} %copy-done), kind=kOutput, calls=%fused_computation.5 | convolution fusion | flops 738459648 | bytes 4128768 | tf_op jit(solution)/shard_map/dot_general | solution.py:326
  255.7 15.3 %all-to-all-start.2 = ((bf16[64,16,256]{2,1,0:T(8,128)(2,1)}), bf16[64,16,256]{2,1,0:T(8,128)(2,1)S(1)}, u32[]{:S(2)}, u32[]{:S(2)}) async-start(bf16[64,16,256]{2,1,0:T(8,128)(2,1)} %bitcast.157), calls=%async_computation.2 | async-start | bytes 1048576 | tf_op jit(solution)/shard_map/all_to_all | solution.py:330
  272.2 1.3 reshape.481
  273.5 1.3 fusion.33
  274.8 10.7 %gather_fusion.1 = f32[816]{0:T(1024)S(1)} fusion(f32[136,64]{0,1:T(8,128)S(1)} %fusion.33, s32[816]{0:T(1024)S(1)} %reshape.500), kind=kCustom, calls=%fused_computation.1 | custom fusion | bytes 13056 | tf_op jit(solution)/shard_map/jit(take_along_axis)/gather | solution.py:344
  286.2 1.5 fusion.11
  287.7 13.5 %all-gather.3 = bf16[8,176,136]{1,2,0:T(8,128)(2,1)S(1)} all-gather(bf16[1,176,136]{1,2,0:T(8,128)(2,1)S(1)} %fusion.11), channel_id=1, replica_groups=mesh['dp'=8,'expert'=64] {'dp'}, dimensions={0}, use_global_device_ids=true | all-gather | bytes 430848 | tf_op jit(solution)/shard_map/all_gather | solution.py:325
  301.4 1.3 reshape.513
  302.6 3.4 %gather_fusion = bf16[816,256]{1,0:T(8,128)(2,1)S(1)} fusion(bf16[1024,256]{1,0:T(8,128)(2,1)S(1)} %bitcast.141, s32[1024]{0:T(1024)S(1)} %pad_clamp_fusion), kind=kCustom, calls=%fused_computation | custom fusion | bytes 838848 | tf_op jit(solution)/shard_map/jit(_take)/gather | solution.py:341
  306.8 1.3 fusion.10
  308.1 9.6 %all_to_all.38 = bf16[8,17,256]{2,1,0:T(8,128)(2,1)S(1)} all-to-all(bf16[8,17,256]{2,1,0:T(8,128)(2,1)S(1)} %convert_element_type.222), channel_id=1, replica_groups=mesh['dp'=8,'expert'=64] {'dp'}, dimensions={0} | all-to-all | bytes 139264 | tf_op jit(solution)/shard_map/all_to_all | solution.py:350
  318.5 0.6 slice.92
  (124 shorter events, 10.0 us)
Async XLA Ops:
  7.2 244.9 %copy-start = (bf16[1,1408,256]{2,1,0:T(8,128)(2,1)S(1)}, bf16[1,1408,256]{2,1,0:T(8,128)(2,1)}, u32[]{:S(2)}) copy-start(bf16[1,1408,256]{2,1,0:T(8,128)(2,1)} %param.36) | copy-start | bytes 2162692
  7.2 8.5 %copy-start.4 = (bf16[1,1024,576]{1,2,0:T(8,128)(2,1)S(1)}, bf16[1,1024,576]{1,2,0:T(8,128)(2,1)}, u32[]{:S(2)}) copy-start(bf16[1,1024,576]{1,2,0:T(8,128)(2,1)} %param.27) | copy-start | bytes 3538948
  7.2 8.4 %copy-start.13 = (f32[16]{0:T(128)S(1)}, f32[16]{0:T(128)}, u32[]{:S(2)}) copy-start(f32[16]{0:T(128)} %param.28) | copy-start | bytes 196
  7.2 20.0 %copy-start.6 = (bf16[32,176]{1,0:T(8,128)(2,1)S(1)}, bf16[32,176]{1,0:T(8,128)(2,1)}, u32[]{:S(2)}) copy-start(bf16[32,176]{1,0:T(8,128)(2,1)} %param.37) | copy-start | bytes 33796
  7.2 20.1 %copy-start.7 = (bf16[32,176]{1,0:T(8,128)(2,1)S(1)}, bf16[32,176]{1,0:T(8,128)(2,1)}, u32[]{:S(2)}) copy-start(bf16[32,176]{1,0:T(8,128)(2,1)} %param.38) | copy-start | bytes 33796
  7.2 20.2 %copy-start.10 = (bf16[22,256]{1,0:T(8,128)(2,1)S(1)}, bf16[22,256]{1,0:T(8,128)(2,1)}, u32[]{:S(2)}) copy-start(bf16[22,256]{1,0:T(8,128)(2,1)} %param.39) | copy-start | bytes 33796
  7.2 20.3 %copy-start.8 = (bf16[2,2,2048]{2,1,0:T(2,128)(2,1)S(1)}, bf16[2,2,2048]{2,1,0:T(2,128)(2,1)}, u32[]{:S(2)}) copy-start(bf16[2,2,2048]{2,1,0:T(2,128)(2,1)} %param.30) | copy-start | bytes 49156
  7.2 20.3 %copy-start.15 = (bf16[2,8,128]{2,1,0:T(8,128)(2,1)S(1)}, bf16[2,8,128]{2,1,0:T(8,128)(2,1)}, u32[]{:S(2)}) copy-start(bf16[2,8,128]{2,1,0:T(8,128)(2,1)} %param.29) | copy-start | bytes 12292
  7.3 20.3 %copy-start.12 = (bf16[2048,1]{0,1:T(2,128)(2,1)S(1)}, bf16[2048,1]{0,1:T(2,128)(2,1)}, u32[]{:S(2)}) copy-start(bf16[2048,1]{0,1:T(2,128)(2,1)} %param.32) | copy-start | bytes 12292
  17.0 85.0 %all-to-all-start = ((bf16[17,16,512]{2,0,1:T(8,128)(2,1)}), bf16[17,16,512]{2,0,1:T(8,128)(2,1)S(1)}, u32[]{:S(2)}, u32[]{:S(2)}) async-start(bf16[17,16,512]{2,0,1:T(8,128)(2,1)} %copy.86), calls=%async_computation | async-start | bytes 786432 | tf_op jit(solution)/shard_map/all_to_all | solution.py:266
  27.2 181.8 %all-gather.9.cloned.1.call-start = ((), (), s32[]{:S(2)}) async-start(), calls=%async_computation.5 | async-start | bytes 4718592 | tf_op jit(solution)/shard_map/all_gather | solution.py:299
  91.0 4.6 %copy-start.9 = (s32[17,6]{0,1:T(8,128)S(1)}, s32[17,6]{0,1:T(8,128)}, u32[]{:S(2)}) copy-start(s32[17,6]{0,1:T(8,128)} %param.33) | copy-start | bytes 1228
  93.7 1.8 copy-start.1
  97.8 38.3 %copy-start.5 = (bf16[16,2048]{1,0:T(8,128)(2,1)S(1)}, bf16[16,2048]{1,0:T(8,128)(2,1)}, u32[]{:S(2)}) copy-start(bf16[16,2048]{1,0:T(8,128)(2,1)} %param.22) | copy-start | bytes 196612
  99.5 34.0 %copy-start.14 = (bf16[2048]{0:T(1024)(128)(2,1)S(1)}, bf16[2048]{0:T(1024)(128)(2,1)}, u32[]{:S(2)}) copy-start(bf16[2048]{0:T(1024)(128)(2,1)} %param.31) | copy-start | bytes 12292
  99.5 36.6 %copy-start.11 = (bf16[1,2048]{1,0:T(2,128)(2,1)S(1)}, bf16[1,2048]{1,0:T(2,128)(2,1)}, u32[]{:S(2)}) copy-start(bf16[1,2048]{1,0:T(2,128)(2,1)} %param.25) | copy-start | bytes 12292
  124.6 10.9 %collective-permute-start.1 = (bf16[24,2048]{1,0:T(8,128)(2,1)S(1)}, bf16[24,2048]{1,0:T(8,128)(2,1)S(1)}, u32[]{:S(2)}, u32[]{:S(2)}) collective-permute-start(bf16[24,2048]{1,0:T(8,128)(2,1)S(1)} %fusion), channel_id=1, source_target_pairs={{0,128},{64,192},{128,256},{192,320},{256,384},{320,448},{1,129},{... | collective-permute-start | bytes 294920
  125.9 9.6 %collective-permute-start = (bf16[24,2048]{1,0:T(8,128)(2,1)S(1)}, bf16[24,2048]{1,0:T(8,128)(2,1)S(1)}, u32[]{:S(2)}, u32[]{:S(2)}) collective-permute-start(bf16[24,2048]{1,0:T(8,128)(2,1)S(1)} %fusion), channel_id=1, source_target_pairs={{0,64},{64,128},{128,192},{192,256},{256,320},{320,384},{384,448},... | collective-permute-start | bytes 294920
  129.3 6.1 %collective-permute-start.2 = (bf16[1,2048]{1,0:T(2,128)(2,1)S(1)}, bf16[1,2048]{1,0:T(2,128)(2,1)S(1)}, u32[]{:S(2)}, u32[]{:S(2)}) collective-permute-start(bf16[1,2048]{1,0:T(2,128)(2,1)S(1)} %slice.94), channel_id=1, source_target_pairs={{0,192},{64,256},{128,320},{192,384},{256,448},{1,193},{65,257},{1... | collective-permute-start | bytes 12296
  178.0 74.0 %all-gather.7.cloned.1.call-start = ((), (), s32[]{:S(2)}) async-start(), calls=%async_computation.4 | async-start | bytes 3244032 | tf_op jit(solution)/shard_map/all_gather | solution.py:324
  190.9 80.4 %copy-start.2 = (bf16[8,18,2048]{2,1,0:T(8,128)(2,1)}, bf16[8,18,2048]{2,1,0:T(8,128)(2,1)S(1)}, u32[]{:S(2)}) copy-start(bf16[8,18,2048]{2,1,0:T(8,128)(2,1)S(1)} %all-gather.2) | copy-start | bytes 1769476
  190.9 22.6 %copy-start.16 = (bf16[1,2048,176]{1,2,0:T(8,128)(2,1)S(1)}, bf16[1,2048,176]{1,2,0:T(8,128)(2,1)}, u32[]{:S(2)}) copy-start(bf16[1,2048,176]{1,2,0:T(8,128)(2,1)} %param.34) | copy-start | bytes 2162692
  213.6 1.6 copy-start.17
  255.7 46.9 %all-to-all-start.2 = ((bf16[64,16,256]{2,1,0:T(8,128)(2,1)}), bf16[64,16,256]{2,1,0:T(8,128)(2,1)S(1)}, u32[]{:S(2)}, u32[]{:S(2)}) async-start(bf16[64,16,256]{2,1,0:T(8,128)(2,1)} %bitcast.157), calls=%async_computation.2 | async-start | bytes 1048576 | tf_op jit(solution)/shard_map/all_to_all | solution.py:330
  301.4 5.4 %copy-start.3 = (bf16[1408,256]{1,0:T(8,128)(2,1)S(1)}, bf16[1408,256]{1,0:T(8,128)(2,1)}, u32[]{:S(2)}) copy-start(bf16[1408,256]{1,0:T(8,128)(2,1)} %reshape_reshape.12) | copy-start | bytes 2162692
Sparse Core Ops, SparseCore 0:
  178.2 30.8 all-gather.8
  217.7 34.3 all-gather.6
